TPU v7x, 32 devices: a whole 2x2x4 slice. The times are simulated.
32 devices in a mesh: seq: 4 (over x, core), fsdp: 8 (over z, y).
Axes of the slice: x: 2, y: 2, z: 4, core: 2. Of those that a mesh axis runs over, the one named last changes fastest.
Arguments:
- tokens: bfloat16 [8, 1536, 1024], P('fsdp', 'seq'), may hold values from -6 to 6
- first_values: bfloat16 [8, 1536, 1024], P('fsdp', 'seq'), may hold values from -6 to 6
- cotangent: bfloat16 [8, 1536, 1024], P('fsdp', 'seq'), may hold values from -6 to 6
- first_gain: bfloat16 [1024], P('fsdp'), may hold values from 0.099609375 to 1.8984375
- query_weight: bfloat16 [1024, 1024], P('fsdp'), may hold values from -0.25 to 0.25
- key_weight: bfloat16 [1024, 1024], P('fsdp'), may hold values from -0.25 to 0.25
- value_weight: bfloat16 [1024, 1024], P('fsdp'), may hold values from -0.1875 to 0.1875
- out_weight: bfloat16 [1024, 1024], P('fsdp'), may hold values from -2 to 2
- second_gain: bfloat16 [1024], P('fsdp'), may hold values from 0.099609375 to 1.8984375
- gate_weight: bfloat16 [1024, 2816], P('fsdp'), may hold values from -0.1875 to 0.1875
- up_weight: bfloat16 [1024, 2816], P('fsdp'), may hold values from -0.1875 to 0.1875
- down_weight: bfloat16 [1024, 2816], P('fsdp'), may hold values from -0.109375 to 0.109375
Outputs:
- output: bfloat16 [8, 1536, 1024], P('fsdp', 'seq')
- tokens_grad: float32 [8, 1536, 1024], P('fsdp', 'seq')
- values_grad: float32 [8, 1536, 1024], P('fsdp', 'seq')
- first_gain_grad: float32 [1024], P('fsdp')
- query_grad: float32 [1024, 1024], P('fsdp')
- key_grad: float32 [1024, 1024], P('fsdp')
- value_grad: float32 [1024, 1024], P('fsdp')
- out_grad: float32 [1024, 1024], P('fsdp')
- second_gain_grad: float32 [1024], P('fsdp')
- gate_grad: float32 [1024, 2816], P('fsdp')
- up_grad: float32 [1024, 2816], P('fsdp')
- down_grad: float32 [1024, 2816], P('fsdp')
All inputs are finite; a program needn't handle non-finite values.
Results may differ from a plain program's by a relative error of at most 0.018.
The roundings to bfloat16 on the way count: a program that leaves them out, or rounds other values in their place, can miss the bound.
Values may be sent and summed in bfloat16 or wider, within the bound.
No kernel may reach another device: no remote copies, remote signals or barrier semaphores. Data moves between devices by JAX's collectives and lax.ppermute only.
A program may use at most 192 MiB of HBM per device.

v0:
```python
import functools
import math

import jax
import jax.numpy as jnp
from jax import lax
from jax.experimental import pallas as pl
from jax.experimental.pallas import tpu as pltpu
from jax.sharding import PartitionSpec as P

HEADS = 16
HEAD_DIM = 64
GROUPS = 4
EPSILON = 1e-06
NEGATIVE = -1e30
F32 = jnp.float32
BF16 = jnp.bfloat16
PARAMS = pltpu.CompilerParams(vmem_limit_bytes=56 * 2**20)


def nn(a, b):
    return lax.dot_general(a, b, (((1,), (0,)), ((), ())), preferred_element_type=F32)


def nt(a, b):
    return lax.dot_general(a, b, (((1,), (1,)), ((), ())), preferred_element_type=F32)


def tn(a, b):
    return lax.dot_general(a, b, (((0,), (0,)), ((), ())), preferred_element_type=F32)


def cost(flops, nbytes, trans=0):
    flops, nbytes, trans = 1, 1, 0
    return pl.CostEstimate(flops=int(flops), bytes_accessed=int(nbytes), transcendentals=int(trans))


def turn(u, cosine, sine):
    lane = lax.broadcasted_iota(jnp.int32, (u.shape[0], 128), 1)
    first = lane % HEAD_DIM < HEAD_DIM // 2
    parts = []
    for j in range(u.shape[1] // 128):
        part = u[:, 128 * j : 128 * (j + 1)]
        other = jnp.where(first, pltpu.roll(part, 96, 1), pltpu.roll(part, 32, 1))
        parts.append(part * cosine + other * sine)
    return jnp.concatenate(parts, axis=1)


def inverse_rms(v):
    return lax.rsqrt(jnp.mean(v * v, axis=-1, keepdims=True) + EPSILON)


ANY = pl.BlockSpec(memory_space=pl.ANY)


def qkv_kernel(count, me, t0, f0, p1, p2, p3, *refs):
    pieces, rest = refs[:count], refs[count:]
    cosine, sine, q, k, v, n, w, tv, fv, sems = rest
    width = q.shape[-1]
    d = tv.shape[-1]
    share = d // count
    first = []
    for i, piece in enumerate(pieces):
        at = pl.ds(pl.multiple_of((me[0] ^ i) * share, share), share)
        first.append(pltpu.make_async_copy(piece, w.at[:, at], sems.at[8 + i]))
    loads = [(t0, f0)] + [(p.at[:, :d], p.at[:, d : d + width]) for p in (p1, p2, p3)]
    copies = []
    for i, (t, f) in enumerate(loads):
        copies.append(pltpu.make_async_copy(t, tv.at[i], sems.at[2 * i]))
        copies.append(pltpu.make_async_copy(f, fv.at[i], sems.at[2 * i + 1]))
    for copy in copies[:2] + first + copies[2:]:
        copy.start()
    for i in range(4):
        copies[2 * i].wait()
        if i == 0:
            for copy in first:
                copy.wait()
        gain = w[3 * width : 3 * width + 1].astype(F32)
        x = tv[i].astype(F32)
        normed = (x * inverse_rms(x) * gain).astype(BF16)
        n[i] = normed
        u = nt(normed, w[: 3 * width])
        c, s = cosine[i], sine[i]
        q[i] = (turn(u[:, :width], c, s).astype(BF16).astype(F32) * 0.125).astype(BF16)
        k[i] = turn(u[:, width : 2 * width], c, s).astype(BF16)
        copies[2 * i + 1].wait()
        v[i] = (0.5 * u[:, 2 * width :] + 0.5 * fv[i].astype(F32)).astype(BF16)


def qkv(where, t, f, packed, pieces, cosine, sine):
    rows, d = t.shape
    width = f.shape[1]
    full = lambda *shape: pl.BlockSpec(shape, lambda i, me: (0,) * len(shape))
    shapes = [(4, rows, width)] * 3 + [(4, rows, d), (pieces[0].shape[0], d)]
    return pl.pallas_call(
        functools.partial(qkv_kernel, len(pieces)),
        grid_spec=pltpu.PrefetchScalarGridSpec(
            num_scalar_prefetch=1,
            grid=(1,),
            in_specs=[ANY] * (5 + len(pieces)) + [full(4, rows, 128)] * 2,
            out_specs=[full(*s) for s in shapes],
            scratch_shapes=[
                pltpu.VMEM((4, rows, d), BF16),
                pltpu.VMEM((4, rows, width), BF16),
                pltpu.SemaphoreType.DMA((8 + len(pieces),)),
            ],
        ),
        out_shape=[jax.ShapeDtypeStruct(s, BF16) for s in shapes],
        compiler_params=PARAMS,
        cost_estimate=cost(2 * 4 * rows * d * 3 * width, 12e6),
        name="qkv",
    )(where.reshape(1), t, f, *packed, *pieces, cosine, sine)


def attn_kernel(me, q, k, v, *refs):
    before, (o0, o1, o2, o3, lse, o) = refs[:-6], refs[-6:]
    h = pl.program_id(0)
    rows, width = q.shape[1:]
    mine = lax.broadcasted_iota(jnp.int32, (1, width), 1) // HEAD_DIM == h
    row = lax.broadcasted_iota(jnp.int32, (rows, rows), 0)
    col = lax.broadcasted_iota(jnp.int32, (rows, rows), 1)
    s = me[0]
    for i in range(GROUPS):
        ri = i ^ s
        qi = jnp.where(mine, q[ri], jnp.zeros((), BF16))
        tiles = []
        for j in range(i + 1):
            tile = nt(qi, k[j ^ s])
            if j == i:
                tile = jnp.where(col <= row, tile, NEGATIVE)
            tiles.append(tile)
        largest = tiles[0].max(axis=1, keepdims=True)
        for tile in tiles[1:]:
            largest = jnp.maximum(largest, tile.max(axis=1, keepdims=True))
        tiles = [jnp.exp(tile - largest) for tile in tiles]
        total = tiles[0].sum(axis=1, keepdims=True)
        for tile in tiles[1:]:
            total = total + tile.sum(axis=1, keepdims=True)
        inverse = 1.0 / total
        acc = jnp.zeros((rows, width), F32)
        for j in range(i + 1):
            acc = acc + nn((tiles[j] * inverse).astype(BF16), v[j ^ s])
        o[ri] = jnp.where(mine, acc.astype(BF16), o[ri])
        stat = jnp.broadcast_to(largest + jnp.log(total), (rows, 128))
        lse[0, i] = jnp.transpose(stat)[:8]

    @pl.when(h == pl.num_programs(0) - 1)
    def _():
        for r, out in enumerate((o0, o1, o2, o3)):
            if before:
                out[:, :width] = before[r][...]
                out[:, width:] = o[r]
            else:
                out[...] = o[r]


def attention(part, me, q, k, v, *before):
    rows = q.shape[1]
    width = 2 * HEAD_DIM
    full = lambda *shape: pl.BlockSpec(shape, lambda h, me: (0,) * len(shape))
    pair = pl.BlockSpec((4, rows, width), lambda h, me: (0, 0, part))
    both = (rows, 2 * width if before else width)
    return pl.pallas_call(
        attn_kernel,
        grid_spec=pltpu.PrefetchScalarGridSpec(
            num_scalar_prefetch=1,
            grid=(2,),
            in_specs=[pair] * 3 + [full(*one.shape) for one in before],
            out_specs=[full(*both)] * 4
            + [pl.BlockSpec((1, 4, 8, rows), lambda h, me: (h, 0, 0, 0))],
            scratch_shapes=[pltpu.VMEM((4, rows, width), BF16)],
        ),
        out_shape=[jax.ShapeDtypeStruct(both, BF16)] * 4
        + [jax.ShapeDtypeStruct((2, 4, 8, rows), F32)],
        compiler_params=PARAMS,
        cost_estimate=cost(2 * 2 * 10 * rows * rows * width * 4, 4e6, 20 * rows * rows),
        name="attention",
    )(me, q, k, v, *before)


def attn_back_kernel(me, q, k, v, b0, b1, b2, b3, lse, cosine, sine, *rest):
    before, (out, vout, do, dq, dk, dv) = rest[:-6], rest[-6:]
    h = pl.program_id(0)
    rows, width = q.shape[1:]
    mine = lax.broadcasted_iota(jnp.int32, (1, width), 1) // HEAD_DIM == h
    key = lax.broadcasted_iota(jnp.int32, (rows, rows), 0)
    query = lax.broadcasted_iota(jnp.int32, (rows, rows), 1)
    s = me[0]
    zero = jnp.zeros((), BF16)

    @pl.when(h == 0)
    def _():
        for r, b in enumerate((b0, b1, b2, b3)):
            do[r] = b[...]
        dq[...] = jnp.zeros_like(dq)
        dk[...] = jnp.zeros_like(dk)
        dv[...] = jnp.zeros_like(dv)

    for i in range(GROUPS):
        qi = jnp.where(mine, q[i ^ s], zero)
        doi = jnp.where(mine, do[i ^ s], zero)
        stat = lse[0, i][:1]
        soft, back = [], []
        dot = jnp.zeros((1, rows), F32)
        for j in range(i + 1):
            tile = nt(k[j ^ s], qi)
            if j == i:
                tile = jnp.where(key <= query, tile, NEGATIVE)
            p = jnp.exp(tile - stat)
            dp = nt(v[j ^ s], doi)
            dot = dot + jnp.sum(p * dp, axis=0, keepdims=True)
            soft.append(p)
            back.append(dp)
        acc = jnp.zeros((rows, width), F32)
        for j in range(i + 1):
            ds = (soft[j] * (back[j] - dot)).astype(BF16)
            dk[j] += nn(ds, qi)
            dv[j] += nn(soft[j].astype(BF16), doi)
            acc = acc + tn(ds, jnp.where(mine, k[j ^ s], zero))
        dq[i] += acc

    @pl.when(h == pl.num_programs(0) - 1)
    def _():
        for i in range(GROUPS):
            ri = i ^ s
            c, n = cosine[ri], -sine[ri]
            out[ri, :, :width] = turn(dq[i] * 0.125, c, n).astype(BF16)
            out[ri, :, width : 2 * width] = turn(dk[i], c, n).astype(BF16)
            half = (0.5 * dv[i]).astype(BF16)
            out[ri, :, 2 * width :] = half
            vout[i, :, len(before) * width :] = half
            if before:
                vout[i, :, :width] = before[0][i]


def attention_back(part, me, q, k, v, b, lse, cosine, sine, *before):
    rows = q.shape[1]
    width = 2 * HEAD_DIM
    full = lambda *shape: pl.BlockSpec(shape, lambda h, me: (0,) * len(shape))
    pair = pl.BlockSpec((4, rows, width), lambda h, me: (0, 0, part))
    return pl.pallas_call(
        attn_back_kernel,
        grid_spec=pltpu.PrefetchScalarGridSpec(
            num_scalar_prefetch=1,
            grid=(2,),
            in_specs=[pair] * 3
            + [pl.BlockSpec((rows, width), lambda h, me: (0, part))] * 4
            + [pl.BlockSpec((1, 4, 8, rows), lambda h, me: (h, 0, 0, 0))]
            + [full(4, rows, 128)] * 2
            + [full(*one.shape) for one in before],
            out_specs=[full(4, rows, 3 * width), full(4, rows, (1 + len(before)) * width)],
            scratch_shapes=[pltpu.VMEM((4, rows, width), BF16)]
            + [pltpu.VMEM((4, rows, width), F32)] * 3,
        ),
        out_shape=[
            jax.ShapeDtypeStruct((4, rows, 3 * width), BF16),
            jax.ShapeDtypeStruct((4, rows, (1 + len(before)) * width), BF16),
        ],
        compiler_params=PARAMS,
        cost_estimate=cost(5 * 2 * 10 * rows * rows * width * 4, 4e6, 20 * rows * rows),
        name="attention_back",
    )(me, q, k, v, *b, lse, cosine, sine, *before)


def out_kernel(me, m0, m1, m2, m3, w0, x0, x1, x2, x3, t, gains, middle, second):
    s = me[0]
    width = m0.shape[1]
    quarter = x0.shape[0]
    first = w0.shape[0] - 4 * quarter
    ws = [[w0.at[first + i * quarter : first + (i + 1) * quarter] for i in range(4)], [x0, x1, x2, x3]]
    for j in range(2):
        for i, w in enumerate(ws[j]):
            start = ((s % 2) ^ j) * 4 * quarter + i * quarter
            cols = pl.ds(pl.multiple_of(start, quarter), quarter)
            part = None
            for r, m in enumerate((m0, m1, m2, m3)):
                one = nt(m[...], w[:, pl.ds(pl.multiple_of((s ^ r) * width, width), width)])
                part = one if part is None else part + one
            middle[:, cols] = t[:, cols].astype(F32) + part
    acc = middle[...]
    second[...] = (acc * inverse_rms(acc) * gains[1:2].astype(F32)).astype(BF16)


def vmem_call(kernel, name, shapes, me, args, estimate, scratch=()):
    full = lambda shape: pl.BlockSpec(shape, lambda i, me: (0,) * len(shape))
    outs = [jax.ShapeDtypeStruct(s, t) for s, t in shapes]
    return pl.pallas_call(
        kernel,
        grid_spec=pltpu.PrefetchScalarGridSpec(
            num_scalar_prefetch=1,
            grid=(1,),
            in_specs=[full(a.shape) for a in args],
            out_specs=[full(s) for s, _ in shapes],
            scratch_shapes=scratch,
        ),
        out_shape=outs,
        compiler_params=PARAMS,
        cost_estimate=estimate,
        name=name,
    )(me, *args)


def mlp_kernel(count, me, sa, sb, ga, gb, down, *refs):
    pieces, outs = refs[:count], refs[count : count + 5]
    sv, gv, wv, dv, hid, gback, uback, sback, sems = refs[count + 5 :]
    units, d = dv.shape
    share = d // count
    rows = sa.shape[0]
    copies = [pltpu.make_async_copy(sa, sv.at[0], sems.at[0])]
    parts = [[], []]
    for h in range(2):
        for i, piece in enumerate(pieces):
            at = pl.ds(pl.multiple_of((me[0] ^ i) * share, share), share)
            part = piece.at[h * units : (h + 1) * units]
            sem = sems.at[15 + h * count + i]
            parts[h].append(pltpu.make_async_copy(part, wv.at[h, :, at], sem))
    copies.append(pltpu.make_async_copy(ga, gv.at[0], sems.at[4]))
    copies.append(pltpu.make_async_copy(down.at[down.shape[0] - units :], dv, sems.at[1]))
    copies.append(pltpu.make_async_copy(sb, sv.at[1], sems.at[5]))
    copies.append(pltpu.make_async_copy(gb, gv.at[1], sems.at[6]))
    for copy in copies[:1] + parts[0] + parts[1] + copies[1:]:
        copy.start()
    writes = []

    def write(buf, out):
        copy = pltpu.make_async_copy(buf, out, sems.at[7 + len(writes)])
        copy.start()
        writes.append(copy)

    for i in range(2):
        copies[3 if i else 0].wait()
        if i == 0:
            for copy in parts[0]:
                copy.wait()
        gate = nt(sv[i], wv[0])
        if i == 0:
            for copy in parts[1]:
                copy.wait()
        up = nt(sv[i], wv[1])
        sg = jax.nn.sigmoid(gate)
        act = gate * sg
        hid[i] = (act * up).astype(BF16)
        at = slice(i * rows, (i + 1) * rows)
        write(hid.at[i], outs[0].at[at])
        copies[4 if i else 1].wait()
        if i == 0:
            copies[2].wait()
        hb = nt(gv[i], dv[...])
        gate_back = (hb * up * sg * (1.0 + gate * (1.0 - sg))).astype(BF16)
        up_back = (hb * act).astype(BF16)
        gback[i] = gate_back
        write(gback.at[i], outs[1].at[at])
        uback[i] = up_back
        write(uback.at[i], outs[2].at[at])
        sback[i] = (nn(gate_back, wv[0]) + nn(up_back, wv[1])).astype(BF16)
        write(sback.at[i], outs[3 + i])
    for copy in writes:
        copy.wait()


def any_call(kernel, name, shapes, me, args, estimate, scratch):
    return pl.pallas_call(
        kernel,
        grid_spec=pltpu.PrefetchScalarGridSpec(
            num_scalar_prefetch=1,
            grid=(1,),
            in_specs=[ANY] * len(args),
            out_specs=[ANY] * len(shapes),
            scratch_shapes=scratch,
        ),
        out_shape=[jax.ShapeDtypeStruct(s, t) for s, t in shapes],
        compiler_params=PARAMS,
        cost_estimate=estimate,
        name=name,
    )(me, *args)


def mlp(where, sa, sb, ga, gb, pieces, down):
    rows, d = sa.shape
    units = pieces[0].shape[0] // 2
    part = ((2 * rows, units), BF16)
    return any_call(
        functools.partial(mlp_kernel, len(pieces)),
        "mlp",
        [part] * 3 + [((rows, d), BF16)] * 2,
        where.reshape(1),
        [sa, sb, ga, gb, down, *pieces],
        cost(2 * 5 * 2 * rows * d * units, 12e6, 2 * rows * units),
        [pltpu.VMEM((2, rows, d), BF16)] * 2
        + [pltpu.VMEM((2, units, d), BF16), pltpu.VMEM((units, d), BF16)]
        + [pltpu.VMEM((2, rows, units), BF16)] * 3
        + [pltpu.VMEM((2, rows, d), BF16), pltpu.SemaphoreType.DMA((15 + 2 * len(pieces),))],
    )


def mlp_out_kernel(me, hn, hf, rest, o0, o1, o2, o3):
    rows = o0.shape[0]
    w = rest.at[rest.shape[0] - hn.shape[1] :]
    for h, outs in ((hn, (o0, o1)), (hf, (o2, o3))):
        for i, out in enumerate(outs):
            out[...] = nn(h[i * rows : (i + 1) * rows], w[...]).astype(BF16)


def unit_grad_kernel(count, me, *refs):
    ins, outs, acc = refs[: 2 * count + 4], refs[2 * count + 4 : -1], refs[-1]
    blocks = ins[2 * count :]
    y = me[0] % 2
    near = jnp.concatenate([blocks[0][...], blocks[1][...]], axis=0)
    far = jnp.concatenate([blocks[2][...], blocks[3][...]], axis=0)
    share = outs[0].shape[2]
    for i in range(count):
        acc[...] = tn(ins[2 * i][...], near) + tn(ins[2 * i + 1][...], far)
        for z in range(outs[0].shape[0]):
            for j in range(2):
                at = pl.multiple_of((2 * z + (y ^ j)) * share, share)
                outs[2 * i + j][z] = acc[:, pl.ds(at, share)].astype(BF16)


def unit_grads(pairs, blocks):
    n = lax.axis_size("fsdp")
    units, d = pairs[0][0].shape[1], blocks[0].shape[1]
    if n != 8:
        near, far = jnp.concatenate(blocks[:2]), jnp.concatenate(blocks[2:])
        outs = [(tn(a, near) + tn(b, far)).astype(BF16) for a, b in pairs]
        return [(jnp.transpose(o.reshape(units, n, d // n), (1, 0, 2)),) for o in outs]
    me = lax.axis_index("fsdp").astype(jnp.int32).reshape(1)
    outs = vmem_call(
        functools.partial(unit_grad_kernel, len(pairs)),
        "unit_grads",
        [((n // 2, units, d // n), BF16)] * (2 * len(pairs)),
        me,
        [a for pair in pairs for a in pair] + list(blocks),
        cost(2 * 4 * blocks[0].shape[0] * units * d * len(pairs), 6e6),
        [pltpu.VMEM((units, d), F32)],
    )
    return [outs[2 * i : 2 * i + 2] for i in range(len(pairs))]


def out_grad_kernel(me, m0, m1, m2, m3, beside, low, low_beside, gain, mine, other, acc):
    s, y = me[0], me[1] % 2
    width = m0.shape[1]
    half = acc.shape[0]
    low_here = low[:, pl.ds(pl.multiple_of((s % 2) * half, half), half)]
    for r, m in enumerate((m0, m1, m2, m3)):
        cols = pl.ds(pl.multiple_of((s ^ r) * width, width), width)
        theirs = beside[:, (r ^ 1) * width : ((r ^ 1) + 1) * width]
        acc[:, cols] = tn(low_here, m[...]) + tn(low_beside[...], theirs)
    share = mine.shape[2]
    for j, out in enumerate((mine, other)):
        for z in range(out.shape[0]):
            cols = pl.ds(pl.multiple_of((2 * z + (y ^ j)) * share, share), share)
            out[z, :half] = acc[:, cols].astype(BF16)
            out[z, half:] = gain[:, cols].astype(BF16)


def qkv_grad_kernel(me, normed, da, db, w, mine, other, acc):
    y = me[1] % 2
    share = mine.shape[2]
    pair = da.shape[1] // 3
    total = jnp.zeros((1, acc.shape[1]), F32)
    for part, dd in enumerate((da, db)):
        acc[3 * part * pair : 3 * (part + 1) * pair] = tn(dd[...], normed[...])
        for i in range(3):
            one = acc[(3 * part + i) * pair : (3 * part + i + 1) * pair]
            rows = w[(2 * i + part) * pair : (2 * i + part + 1) * pair].astype(F32)
            total = total + jnp.sum(one * rows, axis=0, keepdims=True)
    total = total / w[6 * pair : 6 * pair + 1].astype(F32)
    for j, out in enumerate((mine, other)):
        for z in range(mine.shape[0]):
            cols = pl.ds(pl.multiple_of((2 * z + (y ^ j)) * share, share), share)
            out[z, : 6 * pair] = acc[:, cols].astype(BF16)
    for f in range(acc.shape[1] // share):
        row = jnp.broadcast_to(total[:, f * share : (f + 1) * share], (8, share)).astype(BF16)
        for j, out in enumerate((mine, other)):

            @pl.when((f % 2) == (y ^ j))
            def _():
                out[f // 2, 6 * pair :] = row


def joined(r, da, db):
    pair = da.shape[2] // 3
    parts = [d[r, :, j * pair : (j + 1) * pair] for j in range(3) for d in (da, db)]
    return jnp.concatenate(parts, axis=1)


def normed_back_kernel(me, da, db, w, n3, n2, n1):
    for r, out in ((3, n3), (2, n2), (1, n1)):
        out[...] = nn(joined(r, da, db), w[: 2 * da.shape[2]]).astype(BF16)


def place_values_kernel(me, v, out):
    width = v.shape[2]
    for j in range(GROUPS):
        out[:, j * width : (j + 1) * width] = v[j].astype(F32)


def place_qkv_kernel(me, p0, p1, p2, p3, oq, ok, ov, gain):
    s = me[0]
    size = (p0.shape[0] - 8) // 6
    share = p0.shape[1]
    total = jnp.zeros((8, share), F32)
    for r, piece in enumerate((p0, p1, p2, p3)):
        for p in range(2):
            start = p * 3 * size
            at = pl.multiple_of((s ^ r) * 2 * size + p * size, size)
            for i, out in enumerate((oq, ok, ov)):
                block = piece[start + i * size : start + (i + 1) * size]
                out[:, pl.ds(at, size)] = jnp.transpose(block.astype(F32))
        total = total + piece[6 * size :].astype(F32)
    gain[...] = total[:1]


def place_units_kernel(me, p0, p1, p2, p3, *refs):
    outs, buf = refs[:-1], refs[-1]
    s = me[0]
    units = p0.shape[0] // len(outs)
    for r, p in enumerate((p0, p1, p2, p3)):
        buf[s ^ r] = p[...].astype(F32)
    for i, out in enumerate(outs):
        for j in range(GROUPS):
            out[:, j * units : (j + 1) * units] = jnp.transpose(buf[j, i * units : (i + 1) * units])


def place_out_kernel(me, own, other, out, gain):
    core = me[0] % 2
    half = own.shape[0] - 8
    for j, piece in enumerate((own, other)):
        at = pl.multiple_of((core ^ j) * half, half)
        out[:, pl.ds(at, half)] = jnp.transpose(piece[:half].astype(F32))
    gain[...] = own[half : half + 1].astype(F32) + other[half : half + 1].astype(F32)


def middle_kernel(me, p0, p1, p2, middle, g, gains, w0, x0, x1, x2, x3, mback, mlow, mhalf, b0, b1, b2, b3, ggrad):
    s = me[0]
    width = b0.shape[1]
    dn = p0[...].astype(F32) + p1[...].astype(F32) + p2[...].astype(F32)
    v = middle[...]
    r = inverse_rms(v)
    x = v * r
    ggrad[...] = jnp.broadcast_to(jnp.sum(dn * x, axis=0, keepdims=True), ggrad.shape)
    dx = dn * gains[1:2].astype(F32)
    total = g[...].astype(F32) + r * (dx - x * jnp.mean(dx * x, axis=-1, keepdims=True))
    mback[...] = total
    mlow[...] = total.astype(BF16)
    half = 4 * x0.shape[0]
    lows = [mlow[:, pl.ds(pl.multiple_of(((s % 2) ^ j) * half, half), half)] for j in range(2)]
    mhalf[...] = lows[1]
    for i, b in enumerate((b0, b1, b2, b3)):
        cols = pl.ds(pl.multiple_of((s ^ i) * width, width), width)
        w1 = jnp.concatenate([x[:, cols] for x in (x0, x1, x2, x3)], axis=0)
        b[...] = (nn(lows[0], w0[w0.shape[0] - half :, cols]) + nn(lows[1], w1)).astype(BF16)


def final_kernel(me, p1, p2, da, db, w, t, gains, mback, out):
    dn = nn(joined(0, da, db), w[: 2 * da.shape[2]])
    dn = dn + p1[...].astype(F32) + p2[...].astype(F32)
    v = t[...].astype(F32)
    r = inverse_rms(v)
    x = v * r
    dx = dn * gains[:1].astype(F32)
    out[...] = mback[...] + r * (dx - x * jnp.mean(dx * x, axis=-1, keepdims=True))


def after(value, *others):
    return lax.optimization_barrier((value,) + others)[0]


def all_after(values, *others):
    return list(lax.optimization_barrier(tuple(values) + others)[: len(values)])


def add(*terms):
    return sum((term.astype(F32) for term in terms[1:]), terms[0].astype(F32)).astype(BF16)


def seq_permute(value, flip):
    return lax.ppermute(value, "seq", [(i, i ^ flip) for i in range(GROUPS)])


def gather_four(own):
    near = seq_permute(own, 1)
    far = seq_permute(own, 2)
    return own, near, far, seq_permute(far, 1)


def exchange_four(pieces):
    return [pieces[0]] + [seq_permute(pieces[r], r) for r in (1, 2, 3)]


def fsdp_permute(value, flip):
    n = lax.axis_size("fsdp")
    return lax.ppermute(value, "fsdp", [(i, i ^ flip) for i in range(n)])


def fsdp_send(both):
    z = lax.axis_index("fsdp") // 2
    parts = [lax.dynamic_index_in_dim(both, z ^ k, 0, keepdims=False) for k in range(both.shape[0])]
    return [parts[0]] + [fsdp_permute(parts[k], 2 * k) for k in range(1, len(parts))]


def scatter_whole(parts):
    return lax.psum_scatter(parts, "fsdp", scatter_dimension=0, tiled=False)


def per_device(
    tokens,
    first_values,
    cotangent,
    first_gain,
    query_weight,
    key_weight,
    value_weight,
    out_weight,
    second_gain,
    gate_weight,
    up_weight,
    down_weight,
):
    n = lax.axis_size("fsdp")
    s = lax.axis_index("seq").astype(jnp.int32)
    me = s.reshape(1)
    place3 = [jnp.stack([s, lax.axis_index("fsdp").astype(jnp.int32), jnp.int32(p)]) for p in (0, 1)]
    t0, g0, f0 = tokens[0], cotangent[0], first_values[0]
    rows, d = t0.shape
    width = d // GROUPS
    pair = width // 2
    units = gate_weight.shape[1] // GROUPS
    share = d // n
    core = s % 2
    ring = n == 8

    def columns(v, which, size):
        return lax.dynamic_slice_in_dim(v, which * size, size, 1)

    here = lax.axis_index("fsdp").astype(jnp.int32)
    gains = jnp.concatenate([first_gain[None], second_gain[None], jnp.zeros((6, share), BF16)])
    qkv_weights = (query_weight, key_weight, value_weight)
    own_qkv = [columns(w, s, width).T for w in qkv_weights]
    own_qkv += [gains, columns(out_weight, core, d // 2).T]
    own_qkv = jnp.concatenate(own_qkv, axis=0)
    own_units = [columns(w, s, units).T for w in (gate_weight, up_weight, down_weight)]
    own_units, own_down = jnp.concatenate(own_units[:2], axis=0), own_units[2]
    places = (jnp.arange(4, dtype=jnp.int32) ^ s)[:, None] * rows + jnp.arange(rows, dtype=jnp.int32)
    half_dim = HEAD_DIM // 2
    freqs = jnp.exp(jnp.arange(half_dim, dtype=F32) * (-2.0 * math.log(10000.0) / HEAD_DIM))
    angles = places.astype(F32)[:, :, None] * jnp.tile(freqs, 4)
    sign = jnp.tile(jnp.repeat(jnp.array([-1.0, 1.0], F32), half_dim), 2)
    cosine, sine = jnp.cos(angles), jnp.sin(angles) * sign
    f = [columns(f0, s ^ r, width) for r in range(4)]
    if ring:
        first = [fsdp_permute(own_qkv, flip) for flip in (6, 4, 2)][::-1]
        first_y = fsdp_permute(own_qkv, 1)
    packed2 = seq_permute(jnp.concatenate([t0, f[2], f[3]], axis=1), 2)
    if ring:
        pieces = [own_qkv, first_y]
        for i in range(3):
            one = after(first[i], cosine, sine) if i == 0 else first[i]
            pieces += [one, fsdp_permute(one, 1)]
    else:
        pieces = [lax.all_gather(own_qkv, "fsdp", axis=1, tiled=True)]
        unit_pieces = [lax.all_gather(own_units, "fsdp", axis=1, tiled=True)]
    w_down = lax.all_gather(own_down, "fsdp", axis=1, tiled=True)
    where = here if ring else jnp.int32(0)
    packed1 = seq_permute(jnp.concatenate([t0, f[1]], axis=1), 1)
    crossing = jnp.concatenate([packed2[:, :d], packed2[:, d + width :]], axis=1)
    if ring:
        crossing = after(crossing, *pieces[1::2])
    packed3 = seq_permute(crossing, 1)

    if ring:
        sent = after(own_units, pieces[3])
        second = [fsdp_permute(sent, flip) for flip in (2, 4, 6)]
        second_y = fsdp_permute(after(own_units, pieces[5]), 1)
    g2 = seq_permute(after(g0, packed2, *pieces[1::2]), 2)

    q, k, v, normed, w_qkv = qkv(where, t0, f[0], (packed1, packed2, packed3), pieces, cosine, sine)
    gains = w_qkv[3 * width : 3 * width + 8]
    w_out_sent = w_qkv[3 * width + 8 :]
    *m, lse_a = attention(0, me, q, k, v)
    *m, lse_b = attention(1, me, q, k, v, *m)
    g2 = after(g2, m[0])
    if ring:
        second_y, *second = all_after([second_y] + second, m[0])
        m = all_after(m, second_y, *second)
    m = all_after(m, g2)
    m = exchange_four(m)
    w_out_sent = after(w_out_sent, m[2], m[3])
    w_out_other = [
        seq_permute(lax.slice_in_dim(w_out_sent, i * (d // 8), (i + 1) * (d // 8)), 1) for i in range(4)
    ]
    if ring:
        unit_pieces = [own_units, second_y]
        for one in second:
            unit_pieces += [one, after(fsdp_permute(one, 1), m[1])]
        m = all_after(m, *unit_pieces[3::2])
    m = all_after(m, *w_out_other, w_down)
    middle, second = vmem_call(
        out_kernel,
        "out",
        [((rows, d), F32), ((rows, d), BF16)],
        me,
        [*m, w_qkv, *w_out_other, t0, gains],
        cost(2 * rows * d * d, 8e6),
    )
    s0, s1, s2 = second, seq_permute(second, 1), seq_permute(second, 2)
    g1 = seq_permute(after(g0, second), 1)
    g3 = seq_permute(g2, 1)
    hid_near, gate_near, up_near, sb0, sb1 = mlp(where, s0, s1, g0, g1, unit_pieces, w_down)
    s2 = after(s2, sb0)
    s3 = seq_permute(s2, 1)
    hid_far, gate_far, up_far, sb2, sb3 = mlp(where, s2, s3, g2, g3, unit_pieces, w_down)
    sb_both = add(sb2, seq_permute(sb3, 1))
    p = [sb0, seq_permute(after(sb1, sb_both), 1), seq_permute(sb_both, 2)]

    (down_part,) = unit_grads([(hid_near, after(hid_far, p[1]))], (g0, g1, g2, g3))
    if ring:
        down_crossed = fsdp_permute(down_part[1], 1)
    o = vmem_call(
        mlp_out_kernel,
        "mlp_out",
        [((rows, d), BF16)] * 4,
        me,
        [hid_near, after(hid_far, down_part[0]), w_down],
        cost(2 * 4 * rows * d * units, 8e6),
    )
    (gate_part,) = unit_grads([(gate_near, after(gate_far, o[0]))], (s0, s1, s2, s3))
    o1, o3 = all_after([seq_permute(o[1], 1), seq_permute(o[3], 1)], gate_part[0])
    p[2] = after(p[2], gate_part[0])
    p[0] = after(p[0], o3, o1)
    if ring:
        down_both = add(down_part[0], after(down_crossed, p[2]))
        p[2] = after(p[2], down_both)
        gate_crossed = fsdp_permute(after(gate_part[1], down_both), 1)
        mixed_beside = seq_permute(jnp.concatenate(m, axis=1), 1)
        p[0] = after(p[0], mixed_beside)
    mback, mlow, mhalf, b0, b1, b2, b3, ggrad_second = vmem_call(
        middle_kernel,
        "middle",
        [((rows, d), F32), ((rows, d), BF16), ((rows, d // 2), BF16)]
        + [((rows, width), BF16)] * 4
        + [((8, d), F32)],
        me,
        [*p, middle, g0, gains, w_qkv, *w_out_other],
        cost(2 * rows * d * d, 12e6),
    )
    b = exchange_four([b0, b1, b2, b3])
    o_both = add(o[2], after(o3, mlow))
    flat = lambda x: x.reshape(4 * rows, -1)
    qb = q
    if ring:
        low_beside = seq_permute(mhalf, 1)
        out_part = vmem_call(
            out_grad_kernel,
            "out_grad",
            [((n // 2, d // 2 + 8, share), BF16)] * 2,
            place3[0],
            [*m, mixed_beside, mlow, low_beside, ggrad_second],
            cost(2 * rows * d * d, 6e6),
            [pltpu.VMEM((d // 2, d), F32)],
        )
        (up_part,) = unit_grads([(up_near, after(up_far, out_part[0]))], (s0, s1, s2, s3))
        b[1:] = all_after(b[1:], up_part[0], o_both)
        down_sent = fsdp_send(after(down_both, b[2], b[3]))
    else:
        (up_part,) = unit_grads([(up_near, up_far)], (s0, s1, s2, s3))

    def qkv_grads(d_a, d_b):
        if ring:
            return vmem_call(
                qkv_grad_kernel,
                "qkv_grad",
                [((n // 2, 6 * pair + 8, share), BF16)] * 2,
                place3[0],
                [flat(normed), flat(d_a), flat(d_b), w_qkv],
                cost(2 * 4 * rows * d * 6 * pair, 6e6),
                [pltpu.VMEM((6 * pair, d), F32)],
            )
        whole = tn(jnp.concatenate([flat(d_a), flat(d_b)], axis=1), flat(normed))
        starts = [i * width + part * pair for part in range(2) for i in range(3)]
        w = jnp.concatenate([w_qkv[i : i + pair] for i in starts]).astype(F32)
        gain_part = jnp.sum(whole * w, axis=0, keepdims=True) / gains[:1].astype(F32)
        whole = jnp.concatenate([whole, gain_part, jnp.zeros((7, d), F32)]).astype(BF16)
        return (jnp.transpose(whole.reshape(6 * pair + 8, n, share), (1, 0, 2)),)

    d_a, v_a = attention_back(0, me, qb, k, v, b, lse_a, cosine, sine)
    o2 = seq_permute(after(o_both, d_a), 2)
    qb = after(qb, d_a)
    if ring:
        gate_both = add(gate_part[0], after(gate_crossed, d_a))
        down_share = add(*all_after(down_sent, d_a))
        gate_sent = fsdp_send(after(gate_both, down_share))
        up_crossed = fsdp_permute(after(up_part[1], gate_both), 1)
        qb = after(qb, gate_both, down_share)
    d_b, v_b = attention_back(1, me, qb, k, v, b, lse_b, cosine, sine, v_a)
    o2 = after(o2, d_b)
    d_b = after(d_b, o2)
    if ring:
        up_crossed, *gate_sent = all_after([up_crossed] + gate_sent, d_b)
        up_both = add(up_part[0], up_crossed)
        gate_share = add(*gate_sent)
        up_sent = fsdp_send(after(up_both, gate_share))
        out_crossed = fsdp_permute(after(out_part[1], up_both), 1)
        d_b = after(d_b, up_both, gate_share)

    nb3, nb2, nb1 = vmem_call(
        normed_back_kernel,
        "normed_back",
        [((rows, d), BF16)] * 3,
        me,
        [d_a, d_b, w_qkv],
        cost(2 * 3 * rows * d * 3 * width, 8e6),
    )
    nb_both = add(nb2, seq_permute(nb3, 1))
    beside = seq_permute(nb1, 1)
    crossed_far = seq_permute(nb_both, 2)
    qkv_sums = qkv_grads(d_a, after(d_b, nb_both, beside))
    crossed_far = after(crossed_far, qkv_sums[0])
    if ring:
        out_both = add(out_part[0], after(out_crossed, qkv_sums[0]))
        qkv_crossed = fsdp_permute(after(qkv_sums[1], out_both), 1)
        up_share = add(*all_after(up_sent, qkv_sums[0]))
        out_sent = fsdp_send(after(out_both, up_share))
        beside = after(beside, up_share)
    (tokens_grad,) = vmem_call(
        final_kernel,
        "final",
        [((rows, d), F32)],
        me,
        [beside, crossed_far, d_a, d_b, w_qkv, t0, gains, mback],
        cost(0, 6e6),
    )
    if ring:
        qkv_both = add(qkv_sums[0], after(qkv_crossed, tokens_grad))
        out_share = add(*all_after(out_sent, tokens_grad))
        qkv_sent = fsdp_send(after(qkv_both, out_share))
        units_sent = after(jnp.concatenate([gate_share, up_share, down_share], axis=0), tokens_grad)
    else:
        gate_share, up_share, down_share, qkv_share = (
            scatter_whole(v[0]) for v in (gate_part, up_part, down_part, qkv_sums)
        )
        mixed_rows = jnp.zeros((rows, d), BF16)
        for r in range(4):
            mixed_rows = lax.dynamic_update_slice(mixed_rows, m[r], (0, (s ^ r) * width))
        out_part = tn(mlow, mixed_rows)
        halves = [lax.dynamic_slice_in_dim(out_part, (core ^ j) * (d // 2), d // 2) for j in range(2)]
        keep = jnp.concatenate([halves[0], ggrad_second]).reshape(d // 2 + 8, n, share)
        send = jnp.pad(halves[1], ((0, 8), (0, 0))).astype(BF16).reshape(d // 2 + 8, n, share)
        whole = (keep + seq_permute(send, 1).astype(F32)).astype(BF16)
        out_share = scatter_whole(jnp.transpose(whole, (1, 0, 2)))
        units_sent = jnp.concatenate([gate_share, up_share, down_share], axis=0)
    out_share = add(out_share, seq_permute(out_share, 2))
    v_all = lax.all_to_all(after(v_b, tokens_grad), "seq", split_axis=0, concat_axis=0)
    output = add(middle, o[0], o1, o2)[None]
    out_grad, second_gain_grad = vmem_call(
        place_out_kernel,
        "place_out",
        [((share, d), F32), ((1, share), F32)],
        me,
        [out_share, seq_permute(out_share, 1)],
        cost(0, 1e6),
    )
    (values_grad,) = vmem_call(
        place_values_kernel, "place_values", [((rows, d), F32)], me, [v_all], cost(0, 3e6)
    )
    units_far = seq_permute(units_sent, 2)
    if ring:
        qkv_share = add(*all_after(qkv_sent, out_grad, values_grad, output))
        units_far = after(units_far, qkv_share)
    qkv_far = seq_permute(qkv_share, 2)
    gate_grad, up_grad, down_grad = vmem_call(
        place_units_kernel,
        "place_units",
        [((share, 4 * units), F32)] * 3,
        me,
        [units_sent, seq_permute(units_sent, 1), units_far, seq_permute(units_far, 1)],
        cost(0, 3e6),
        [pltpu.VMEM((4, 3 * units, share), F32)],
    )
    qkv_far = after(qkv_far, gate_grad)
    qkv_all = [qkv_share, seq_permute(qkv_share, 1), qkv_far, seq_permute(qkv_far, 1)]
    query_grad, key_grad, value_grad, gain_grad = vmem_call(
        place_qkv_kernel,
        "place_qkv",
        [((share, d), F32)] * 3 + [((1, share), F32)],
        me,
        qkv_all,
        cost(0, 3e6),
    )
    return (
        output,
        tokens_grad[None],
        values_grad[None],
        gain_grad.reshape(share),
        query_grad,
        key_grad,
        value_grad,
        out_grad,
        second_gain_grad.reshape(share),
        gate_grad,
        up_grad,
        down_grad,
    )


def solution(mesh):
    rows = P("fsdp", "seq", None)
    weight = P("fsdp", None)
    gain = P("fsdp")
    in_specs = (rows,) * 3 + (gain,) + (weight,) * 4 + (gain,) + (weight,) * 3
    out_specs = (rows,) * 3 + (gain,) + (weight,) * 4 + (gain,) + (weight,) * 3
    return jax.shard_map(
        per_device, mesh=mesh, in_specs=in_specs, out_specs=out_specs, check_vma=False
    )
```

profile of v0, /device:TPU:0, one launch (start us, length us, event | category | flops | bytes accessed | tf_op | source)
XLA Modules:
  0.0 370.0 jit_solution(8890042932757073494)
XLA Ops:
  10.5 2.9 collective-permute-start.1
  24.4 4.3 %fusion = (f32[4,384,128]{2,1,0:T(8,128)}, f32[4,384,128]{2,1,0:T(8,128)}) fusion(f32[128]{0:T(128)S(1)} %mul.78, f32[128]{0:T(128)S(1)} %mul.75, f32[4,384]{1,0:T(4,128)S(1)} %add_convert_fusion.15), kind=kLoop, calls=%fused_computation.14 | loop fusion | flops 393216 | bytes 1580032 | tf_op jit(solution)/shard_map/mul | solution.py:649
  28.6 2.8 collective-permute-done.3.refs_2_
  32.9 14.0 %collective-permute-done.5.refs_4_ = bf16[1288,128]{1,0:T(8,128)(2,1)} collective-permute-done((bf16[1288,128]{1,0:T(8,128)(2,1)S(1)}, bf16[1288,128]{1,0:T(8,128)(2,1)}, u32[]{:S(2)}, u32[]{:S(2)}) %collective-permute-start.5) | collective-permute-done | bytes 329760 | tf_op jit(solution)/shard_map/ppermute | solution.py:593
  51.4 2.9 collective-permute-done.6.refs_5_
  54.3 3.5 collective-permute-done.8.refs_7_
  59.1 9.9 %collective-permute-start.11 = (bf16[1408,128]{1,0:T(8,128)(2,1)S(1)}, bf16[1408,128]{1,0:T(8,128)(2,1)S(1)}, u32[]{:S(2)}, u32[]{:S(2)}) collective-permute-start(bf16[1408,128]{1,0:T(8,128)(2,1)S(1)} %pad_maximum_fusion.5.refs_0_), channel_id=1, source_target_pairs={{0,2},{1,3},{2,0},{3,1},{4,6},{5,7},{6,4},{7,5},{8,10},{9,11},{10,... | collective-permute-start | bytes 1081352 | tf_op jit(solution)/shard_map/ppermute | solution.py:593
  74.0 11.5 %qkv.1 = (bf16[4,384,256]{2,1,0:T(8,128)(2,1)}, bf16[4,384,256]{2,1,0:T(8,128)(2,1)}, bf16[4,384,256]{2,1,0:T(8,128)(2,1)}, bf16[4,384,1024]{2,1,0:T(8,128)(2,1)}, bf16[1288,1024]{1,0:T(8,128)(2,1)}) custom-call(s32[1]{0:T(128)} %bitcast.1.me, bf16[384,1024]{1,0:T(8,128)(2,1)} %bitcast.70, bf16[384,256]{1,0:T(8,128)(2,1)} %get-tuple-element.340.f0, ...), custom_call_target="tpu_custom_call" | custom-call | flops 1 | bytes 1 | tf_op jit(solution)/shard_map/qkv/pallas_call | solution.py:95
  85.6 8.4 %attention.2 = (bf16[384,128]{1,0:T(8,128)(2,1)}, bf16[384,128]{1,0:T(8,128)(2,1)}, bf16[384,128]{1,0:T(8,128)(2,1)}, bf16[384,128]{1,0:T(8,128)(2,1)}, f32[2,4,8,384]{3,2,1,0:T(8,128)}) custom-call(s32[1]{0:T(128)} %bitcast.me, bf16[4,384,256]{2,1,0:T(8,128)(2,1)} %get-tuple-element.271.q, bf16[4,384,256]{2,1,0:T(8,128)(2,1)} %get-tuple-element.174.k, ...), custom_call_target="tpu_custom_call" | custom-call | flops 1 | bytes 1 | tf_op jit(solution)/shard_map/attention/pallas_call | solution.py:163
  94.0 9.1 %attention.3 = (bf16[384,256]{1,0:T(8,128)(2,1)}, bf16[384,256]{1,0:T(8,128)(2,1)}, bf16[384,256]{1,0:T(8,128)(2,1)}, bf16[384,256]{1,0:T(8,128)(2,1)}, f32[2,4,8,384]{3,2,1,0:T(8,128)}) custom-call(s32[1]{0:T(128)} %bitcast.me, bf16[4,384,256]{2,1,0:T(8,128)(2,1)} %get-tuple-element.271.q, bf16[4,384,256]{2,1,0:T(8,128)(2,1)} %get-tuple-element.174.k, ...), custom_call_target="tpu_custom_call" | custom-call | flops 1 | bytes 1 | tf_op jit(solution)/shard_map/attention/pallas_call | solution.py:163
  116.0 7.7 %collective-permute-done.19.refs_5_ = bf16[1408,128]{1,0:T(8,128)(2,1)S(1)} collective-permute-done((bf16[1408,128]{1,0:T(8,128)(2,1)S(1)}, bf16[1408,128]{1,0:T(8,128)(2,1)S(1)}, u32[]{:S(2)}, u32[]{:S(2)}) %collective-permute-start.19) | collective-permute-done | bytes 360480 | tf_op jit(solution)/shard_map/ppermute | solution.py:593
  125.7 5.6 %collective-permute-done.18.refs_3_ = bf16[1408,128]{1,0:T(8,128)(2,1)} collective-permute-done((bf16[1408,128]{1,0:T(8,128)(2,1)S(1)}, bf16[1408,128]{1,0:T(8,128)(2,1)}, u32[]{:S(2)}, u32[]{:S(2)}) %collective-permute-start.18) | collective-permute-done | bytes 360480 | tf_op jit(solution)/shard_map/ppermute | solution.py:593
  132.7 5.8 %out.1 = (f32[384,1024]{1,0:T(8,128)}, bf16[384,1024]{1,0:T(8,128)(2,1)}) custom-call(s32[1]{0:T(128)} %bitcast.me, bf16[384,256]{1,0:T(8,128)(2,1)} %get-tuple-element.209.m0, bf16[384,256]{1,0:T(8,128)(2,1)} %copy-done.20, bf16[384,256]{1,0:T(8,128)(2,1)} %copy-done.16, bf16[384,256]{1,0:T(8,128)(2,1)} %copy-done.18, ...), custom_call_target="tpu_custom_call" | custom-call | flops 1 | bytes 1 | tf_op jit(solution)/shard_map/out/pallas_call | solution.py:287
  143.8 12.5 %mlp.2 = (bf16[768,704]{1,0:T(8,128)(2,1)}, bf16[768,704]{1,0:T(8,128)(2,1)}, bf16[768,704]{1,0:T(8,128)(2,1)}, bf16[384,1024]{1,0:T(8,128)(2,1)}, bf16[384,1024]{1,0:T(8,128)(2,1)}) custom-call(s32[1]{0:T(128)} %bitcast.1.me, bf16[384,1024]{1,0:T(8,128)(2,1)} %get-tuple-element.214.sa.refs_2_, bf16[384,1024]{1,0:T(8,128)(2,1)} %copy-done.4, ...), custom_call_target="tpu_custom_call" | custom-call | flops 1 | bytes 1 | tf_op jit(solution)/shard_map/mlp/pallas_call | solution.py:362
  161.9 21.3 %mlp.3 = (bf16[768,704]{1,0:T(8,128)(2,1)}, bf16[768,704]{1,0:T(8,128)(2,1)}, bf16[768,704]{1,0:T(8,128)(2,1)}, bf16[384,1024]{1,0:T(8,128)(2,1)}, bf16[384,1024]{1,0:T(8,128)(2,1)}) custom-call(s32[1]{0:T(128)} %bitcast.1.me, bf16[384,1024]{1,0:T(8,128)(2,1)} %copy-done.5, bf16[384,1024]{1,0:T(8,128)(2,1)} %copy-done.6, bf16[384,1024]{1,0:T(8,128)(2,1)} %copy-done.11, ...), custom_call_target="tpu_custom_call" | custom-call | flops 1 | bytes 1 | tf_op jit(solution)/shard_map/mlp/pallas_call | solution.py:362
  189.6 6.7 %unit_grads.3 = (bf16[4,704,128]{2,1,0:T(8,128)(2,1)}, bf16[4,704,128]{2,1,0:T(8,128)(2,1)}) custom-call(s32[1]{0:T(128)} %bitcast.1.me, bf16[768,704]{1,0:T(8,128)(2,1)} %get-tuple-element.216.refs_0_.hn, bf16[768,704]{1,0:T(8,128)(2,1)} %get-tuple-element.226.refs_1_.hf, bf16[384,1024]{1,0:T(8,128)(2,1)} %bitcast.78, bf16[384,1024]{1,0:T(8,128)(2,1)} %copy-done.12, ...), custom_call_target="tpu_custom_call" | custom-call | flops 1 | bytes 1 | tf_op jit(solution)/shard_map/unit_grads/pallas_call | solution.py:287
  196.5 5.6 %mlp_out.1 = (bf16[384,1024]{1,0:T(8,128)(2,1)}, bf16[384,1024]{1,0:T(8,128)(2,1)}, bf16[384,1024]{1,0:T(8,128)(2,1)}, bf16[384,1024]{1,0:T(8,128)(2,1)}) custom-call(s32[1]{0:T(128)} %bitcast.me, bf16[768,704]{1,0:T(8,128)(2,1)} %get-tuple-element.216.refs_0_.hn, bf16[768,704]{1,0:T(8,128)(2,1)} %get-tuple-element.226.refs_1_.hf, ...), custom_call_target="tpu_custom_call" | custom-call | flops 1 | bytes 1 | tf_op jit(solution)/shard_map/mlp_out/pallas_call | solution.py:287
  202.9 6.9 %unit_grads.4 = (bf16[4,704,128]{2,1,0:T(8,128)(2,1)}, bf16[4,704,128]{2,1,0:T(8,128)(2,1)}) custom-call(s32[1]{0:T(128)} %bitcast.1.me, bf16[768,704]{1,0:T(8,128)(2,1)} %get-tuple-element.230.refs_0_, bf16[768,704]{1,0:T(8,128)(2,1)} %get-tuple-element.232.refs_1_, bf16[384,1024]{1,0:T(8,128)(2,1)} %get-tuple-element.214.sa.refs_2_, ...), custom_call_target="tpu_custom_call" | custom-call | flops 1 | bytes 1 | tf_op jit(solution)/shard_map/unit_grads/pallas_call | solution.py:287
  209.7 5.0 %collective-permute-done.36 = bf16[4,704,128]{2,1,0:T(8,128)(2,1)S(1)} collective-permute-done((bf16[4,704,128]{2,1,0:T(8,128)(2,1)}, bf16[4,704,128]{2,1,0:T(8,128)(2,1)S(1)}, u32[]{:S(2)}, u32[]{:S(2)}) %collective-permute-start.36) | collective-permute-done | bytes 720928 | tf_op jit(solution)/shard_map/ppermute | solution.py:593
  215.3 6.5 %middle.1 = (f32[384,1024]{1,0:T(8,128)}, bf16[384,1024]{1,0:T(8,128)(2,1)}, bf16[384,512]{1,0:T(8,128)(2,1)}, bf16[384,256]{1,0:T(8,128)(2,1)}, bf16[384,256]{1...) custom-call(s32[1]{0:T(128)} %bitcast.me, ...), custom_call_target="tpu_custom_call" | custom-call | flops 1 | bytes 1 | tf_op jit(solution)/shard_map/middle/pallas_call | solution.py:287
  226.6 4.9 %out_grad.1 = (bf16[4,520,128]{2,1,0:T(8,128)(2,1)}, bf16[4,520,128]{2,1,0:T(8,128)(2,1)}) custom-call(s32[3]{0:T(128)} %pad_add_fusion.me, bf16[384,256]{1,0:T(8,128)(2,1)} %get-tuple-element.209.m0, bf16[384,256]{1,0:T(8,128)(2,1)} %copy-done.20, bf16[384,256]{1,0:T(8,128)(2,1)} %copy-done.16, bf16[384,256]{1,0:T(8,128)(2,1)} %copy-done.18, ...), custom_call_target="tpu_custom_call" | custom-call | flops 1 | bytes 1 | tf_op jit(solution)/shard_map/out_grad/pallas_call | solution.py:287
  231.5 6.3 %unit_grads.5 = (bf16[4,704,128]{2,1,0:T(8,128)(2,1)}, bf16[4,704,128]{2,1,0:T(8,128)(2,1)}) custom-call(s32[1]{0:T(128)} %bitcast.1.me, bf16[768,704]{1,0:T(8,128)(2,1)} %get-tuple-element.249.refs_0_, bf16[768,704]{1,0:T(8,128)(2,1)} %get-tuple-element.254.refs_1_, bf16[384,1024]{1,0:T(8,128)(2,1)} %get-tuple-element.214.sa.refs_2_, ...), custom_call_target="tpu_custom_call" | custom-call | flops 1 | bytes 1 | tf_op jit(solution)/shard_map/unit_grads/pallas_call | solution.py:287
  238.0 4.5 %collective-permute-start.43 = (bf16[704,128]{1,0:T(8,128)(2,1)S(1)}, bf16[704,128]{1,0:T(8,128)(2,1)S(1)}, u32[]{:S(2)}, u32[]{:S(2)}) collective-permute-start(bf16[704,128]{1,0:T(8,128)(2,1)S(1)} %get-tuple-element.352), channel_id=1, source_target_pairs={{0,2},{1,3},{2,0},{3,1},{4,6},{5,7},{6,4},{7,5},{8,10},{9,11},{10,... | collective-permute-start | bytes 540680 | tf_op jit(solution)/shard_map/ppermute | solution.py:593
  244.9 14.2 %attention_back.2 = (bf16[4,384,384]{2,1,0:T(8,128)(2,1)}, bf16[4,384,128]{2,1,0:T(8,128)(2,1)}) custom-call(s32[1]{0:T(128)} %bitcast.me, bf16[4,384,256]{2,1,0:T(8,128)(2,1)} %get-tuple-element.271.q, bf16[4,384,256]{2,1,0:T(8,128)(2,1)} %get-tuple-element.174.k, bf16[4,384,256]{2,1,0:T(8,128)(2,1)} %get-tuple-element.175.v, ...), custom_call_target="tpu_custom_call" | custom-call | flops 1 | bytes 1 | tf_op jit(solution)/shard_map/attention_back/pallas_call | solution.py:241
  268.0 14.6 %attention_back.3 = (bf16[4,384,384]{2,1,0:T(8,128)(2,1)}, bf16[4,384,256]{2,1,0:T(8,128)(2,1)}) custom-call(s32[1]{0:T(128)} %bitcast.me, bf16[4,384,256]{2,1,0:T(8,128)(2,1)} %get-tuple-element.271.q, bf16[4,384,256]{2,1,0:T(8,128)(2,1)} %get-tuple-element.174.k, bf16[4,384,256]{2,1,0:T(8,128)(2,1)} %get-tuple-element.175.v, ...), custom_call_target="tpu_custom_call" | custom-call | flops 1 | bytes 1 | tf_op jit(solution)/shard_map/attention_back/pallas_call | solution.py:241
  282.9 5.5 %normed_back.1 = (bf16[384,1024]{1,0:T(8,128)(2,1)}, bf16[384,1024]{1,0:T(8,128)(2,1)}, bf16[384,1024]{1,0:T(8,128)(2,1)}) custom-call(s32[1]{0:T(128)} %bitcast.me, bf16[4,384,384]{2,1,0:T(8,128)(2,1)} %get-tuple-element.260.da, bf16[4,384,384]{2,1,0:T(8,128)(2,1)} %get-tuple-element.291.db, bf16[1288,1024]{1,0:T(8,128)(2,1)} %get-tuple-element.207.w0.w), custom_call_target="tpu_custom_call" | custom-call | flops 1 | bytes 1 | tf_op jit(solution)/shard_map/normed_back/pallas_call | solution.py:287
  295.1 8.9 %qkv_grad.1 = (bf16[4,776,128]{2,1,0:T(8,128)(2,1)}, bf16[4,776,128]{2,1,0:T(8,128)(2,1)}) custom-call(s32[3]{0:T(128)} %pad_add_fusion.me, bf16[1536,1024]{1,0:T(8,128)(2,1)} %bitcast.82, bf16[1536,384]{1,0:T(8,128)(2,1)} %bitcast.75, bf16[1536,384]{1,0:T(8,128)(2,1)} %bitcast.76, bf16[1288,1024]{1,0:T(8,128)(2,1)} %get-tuple-element.207.w0.w), custom_call_target="tpu_custom_call" | custom-call | flops 1 | bytes 1 | tf_op jit(solution)/shard_map/qkv_grad/pallas_call | solution.py:287
  307.9 3.1 collective-permute-start.58
  314.5 6.0 %final.1 = f32[384,1024]{1,0:T(8,128)} custom-call(s32[1]{0:T(128)} %bitcast.me, bf16[384,1024]{1,0:T(8,128)(2,1)} %copy-done.45, bf16[384,1024]{1,0:T(8,128)(2,1)} %copy-done.46, bf16[4,384,384]{2,1,0:T(8,128)(2,1)} %get-tuple-element.260.da, bf16[4,384,384]{2,1,0:T(8,128)(2,1)} %get-tuple-element.291.db, bf16[1288,1024]{1,0:T(8,128)(2,1)} %get-tuple-element.207.w0.w, ...), custom_call_target="tpu_custom_call" | custom-call | flops 1 | bytes 1 | tf_op jit(solution)/shard_map/final/pallas_call | solution.py:287
  322.8 3.5 all-to-all-start
  333.0 5.6 %collective-permute-done.64 = bf16[520,128]{1,0:T(8,128)(2,1)S(1)} collective-permute-done((bf16[520,128]{1,0:T(8,128)(2,1)S(1)}, bf16[520,128]{1,0:T(8,128)(2,1)S(1)}, u32[]{:S(2)}, u32[]{:S(2)}) %collective-permute-start.64) | collective-permute-done | bytes 133152 | tf_op jit(solution)/shard_map/ppermute | solution.py:578
  352.8 5.4 %place_units.1 = (f32[128,2816]{1,0:T(8,128)}, f32[128,2816]{1,0:T(8,128)}, f32[128,2816]{1,0:T(8,128)}) custom-call(s32[1]{0:T(128)} %bitcast.me, bf16[2112,128]{1,0:T(8,128)(2,1)} %copy-done.14, bf16[2112,128]{1,0:T(8,128)(2,1)} %copy-done.50, bf16[2112,128]{1,0:T(8,128)(2,1)} %collective-permute-done.69.p2, bf16[2112,128]{1,0:T(8,128)(2,1)} %copy-done.51), custom_call_target="tpu_custom_call" | custom-call | flops 1 | bytes 1 | tf_op jit(solution)/shard_map/place_units/pallas_call | solution.py:287
  (335 shorter events, 119.1 us)
Async XLA Ops:
  7.2 124.1 %all-gather.2.cloned.1.call-start = ((), (), s32[]{:S(2)}) async-start(), calls=%async_computation.1 | async-start | bytes 1622016 | tf_op jit(solution)/shard_map/all_gather | solution.py:663
  10.5 39.5 %collective-permute-start.1 = (bf16[384,1536]{1,0:T(8,128)(2,1)}, bf16[384,1536]{1,0:T(8,128)(2,1)S(1)}, u32[]{:S(2)}, u32[]{:S(2)}) collective-permute-start(bf16[384,1536]{1,0:T(8,128)(2,1)} %pad_maximum_fusion), channel_id=1, source_target_pairs={{0,16},{8,24},{16,0},{24,8},{1,17},{9,25},{17,1},{25,9},{2,18},{10... | collective-permute-start | bytes 3538952 | tf_op jit(solution)/shard_map/ppermute | solution.py:578
  17.5 29.5 %collective-permute-start.5 = (bf16[1288,128]{1,0:T(8,128)(2,1)S(1)}, bf16[1288,128]{1,0:T(8,128)(2,1)}, u32[]{:S(2)}, u32[]{:S(2)}) collective-permute-start(bf16[1288,128]{1,0:T(8,128)(2,1)S(1)} %concatenate.24.refs_0_), channel_id=1, source_target_pairs={{0,4},{1,5},{2,6},{3,7},{4,0},{5,1},{6,2},{7,3},{8,12},{9,13},{10,... | collective-permute-start | bytes 989192 | tf_op jit(solution)/shard_map/ppermute | solution.py:593
  20.1 28.4 %collective-permute-start.7 = (bf16[1288,128]{1,0:T(8,128)(2,1)S(1)}, bf16[1288,128]{1,0:T(8,128)(2,1)}, u32[]{:S(2)}, u32[]{:S(2)}) collective-permute-start(bf16[1288,128]{1,0:T(8,128)(2,1)S(1)} %concatenate.24.refs_0_), channel_id=1, source_target_pairs={{0,6},{1,7},{2,4},{3,5},{4,2},{5,3},{6,0},{7,1},{8,14},{9,15},{10,... | collective-permute-start | bytes 989192 | tf_op jit(solution)/shard_map/ppermute | solution.py:593
  20.3 31.0 %collective-permute-start.2 = (bf16[1288,128]{1,0:T(8,128)(2,1)S(1)}, bf16[1288,128]{1,0:T(8,128)(2,1)}, u32[]{:S(2)}, u32[]{:S(2)}) collective-permute-start(bf16[1288,128]{1,0:T(8,128)(2,1)S(1)} %concatenate.24.refs_0_), channel_id=1, source_target_pairs={{0,1},{1,0},{2,3},{3,2},{4,5},{5,4},{6,7},{7,6},{8,9},{9,8},{10,11... | collective-permute-start | bytes 989192 | tf_op jit(solution)/shard_map/ppermute | solution.py:593
  31.4 20.0 %collective-permute-start.4 = (bf16[1288,128]{1,0:T(8,128)(2,1)}, bf16[1288,128]{1,0:T(8,128)(2,1)S(1)}, u32[]{:S(2)}, u32[]{:S(2)}) collective-permute-start(bf16[1288,128]{1,0:T(8,128)(2,1)} %collective-permute-done.3.refs_2_), channel_id=1, source_target_pairs={{0,1},{1,0},{2,3},{3,2},{4,5},{5,4},{6,7},{7,6},{8,9},{9,8},{10,11... | collective-permute-start | bytes 989192 | tf_op jit(solution)/shard_map/ppermute | solution.py:593
  50.0 20.2 %collective-permute-start = (bf16[384,1280]{1,0:T(8,128)(2,1)}, bf16[384,1280]{1,0:T(8,128)(2,1)}, u32[]{:S(2)}, u32[]{:S(2)}) collective-permute-start(bf16[384,1280]{1,0:T(8,128)(2,1)} %pad_maximum_fusion.1), channel_id=1, source_target_pairs={{0,8},{8,0},{16,24},{24,16},{1,9},{9,1},{17,25},{25,17},{2,10},{10... | collective-permute-start | bytes 2949128 | tf_op jit(solution)/shard_map/ppermute | solution.py:578
  57.8 45.3 %collective-permute-start.14 = (bf16[384,1024]{1,0:T(8,128)(2,1)S(1)}, bf16[384,1024]{1,0:T(8,128)(2,1)S(1)}, u32[]{:S(2)}, u32[]{:S(2)}) collective-permute-start(bf16[384,1024]{1,0:T(8,128)(2,1)S(1)} %bitcast.80), channel_id=1, source_target_pairs={{0,16},{8,24},{16,0},{24,8},{1,17},{9,25},{17,1},{25,9},{2,18},{10... | collective-permute-start | bytes 2359304 | tf_op jit(solution)/shard_map/ppermute | solution.py:578
  59.1 44.1 %collective-permute-start.11 = (bf16[1408,128]{1,0:T(8,128)(2,1)S(1)}, bf16[1408,128]{1,0:T(8,128)(2,1)S(1)}, u32[]{:S(2)}, u32[]{:S(2)}) collective-permute-start(bf16[1408,128]{1,0:T(8,128)(2,1)S(1)} %pad_maximum_fusion.5.refs_0_), channel_id=1, source_target_pairs={{0,2},{1,3},{2,0},{3,1},{4,6},{5,7},{6,4},{7,5},{8,10},{9,11},{10,... | collective-permute-start | bytes 1081352 | tf_op jit(solution)/shard_map/ppermute | solution.py:593
  69.0 34.1 %collective-permute-start.12 = (bf16[1408,128]{1,0:T(8,128)(2,1)S(1)}, bf16[1408,128]{1,0:T(8,128)(2,1)S(1)}, u32[]{:S(2)}, u32[]{:S(2)}) collective-permute-start(bf16[1408,128]{1,0:T(8,128)(2,1)S(1)} %pad_maximum_fusion.5.refs_0_), channel_id=1, source_target_pairs={{0,4},{1,5},{2,6},{3,7},{4,0},{5,1},{6,2},{7,3},{8,12},{9,13},{10,... | collective-permute-start | bytes 1081352 | tf_op jit(solution)/shard_map/ppermute | solution.py:593
  70.3 32.9 %collective-permute-start.13 = (bf16[1408,128]{1,0:T(8,128)(2,1)S(1)}, bf16[1408,128]{1,0:T(8,128)(2,1)S(1)}, u32[]{:S(2)}, u32[]{:S(2)}) collective-permute-start(bf16[1408,128]{1,0:T(8,128)(2,1)S(1)} %pad_maximum_fusion.5.refs_0_), channel_id=1, source_target_pairs={{0,6},{1,7},{2,4},{3,5},{4,2},{5,3},{6,0},{7,1},{8,14},{9,15},{10,... | collective-permute-start | bytes 1081352 | tf_op jit(solution)/shard_map/ppermute | solution.py:593
  71.7 31.5 %collective-permute-start.10 = (bf16[1408,128]{1,0:T(8,128)(2,1)S(1)}, bf16[1408,128]{1,0:T(8,128)(2,1)}, u32[]{:S(2)}, u32[]{:S(2)}) collective-permute-start(bf16[1408,128]{1,0:T(8,128)(2,1)S(1)} %pad_maximum_fusion.5.refs_0_), channel_id=1, source_target_pairs={{0,1},{1,0},{2,3},{3,2},{4,5},{5,4},{6,7},{7,6},{8,9},{9,8},{10,11... | collective-permute-start | bytes 1081352 | tf_op jit(solution)/shard_map/ppermute | solution.py:593
  104.7 19.0 %collective-permute-start.19 = (bf16[1408,128]{1,0:T(8,128)(2,1)S(1)}, bf16[1408,128]{1,0:T(8,128)(2,1)S(1)}, u32[]{:S(2)}, u32[]{:S(2)}) collective-permute-start(bf16[1408,128]{1,0:T(8,128)(2,1)S(1)} %collective-permute-done.12.refs_4_), channel_id=1, source_target_pairs={{0,1},{1,0},{2,3},{3,2},{4,5},{5,4},{6,7},{7,6},{8,9},{9,8},{10,11... | collective-permute-start | bytes 1081352 | tf_op jit(solution)/shard_map/ppermute | solution.py:593
  106.7 24.6 %collective-permute-start.18 = (bf16[1408,128]{1,0:T(8,128)(2,1)S(1)}, bf16[1408,128]{1,0:T(8,128)(2,1)}, u32[]{:S(2)}, u32[]{:S(2)}) collective-permute-start(bf16[1408,128]{1,0:T(8,128)(2,1)S(1)} %collective-permute-done.11.refs_2_), channel_id=1, source_target_pairs={{0,1},{1,0},{2,3},{3,2},{4,5},{5,4},{6,7},{7,6},{8,9},{9,8},{10,11... | collective-permute-start | bytes 1081352 | tf_op jit(solution)/shard_map/ppermute | solution.py:593
  113.9 17.4 %collective-permute-start.21 = (bf16[128,1024]{1,0:T(8,128)(2,1)}, bf16[128,1024]{1,0:T(8,128)(2,1)S(1)}, u32[]{:S(2)}, u32[]{:S(2)}) collective-permute-start(bf16[128,1024]{1,0:T(8,128)(2,1)} %get-tuple-element.333), channel_id=1, source_target_pairs={{0,8},{8,0},{16,24},{24,16},{1,9},{9,1},{17,25},{25,17},{2,10},{10... | collective-permute-start | bytes 786440 | tf_op jit(solution)/shard_map/ppermute | solution.py:578
  139.0 19.7 %collective-permute-start.27 = (bf16[384,1024]{1,0:T(8,128)(2,1)}, bf16[384,1024]{1,0:T(8,128)(2,1)S(1)}, u32[]{:S(2)}, u32[]{:S(2)}) collective-permute-start(bf16[384,1024]{1,0:T(8,128)(2,1)} %get-tuple-element.214.sa.refs_2_), channel_id=1, source_target_pairs={{0,16},{8,24},{16,0},{24,8},{1,17},{9,25},{17,1},{25,9},{2,18},{10... | collective-permute-start | bytes 2359304 | tf_op jit(solution)/shard_map/ppermute | solution.py:578
  139.5 19.2 %collective-permute-start.29 = (bf16[384,1024]{1,0:T(8,128)(2,1)S(1)}, bf16[384,1024]{1,0:T(8,128)(2,1)S(1)}, u32[]{:S(2)}, u32[]{:S(2)}) collective-permute-start(bf16[384,1024]{1,0:T(8,128)(2,1)S(1)} %collective-permute-done.14.ga.refs_4_), channel_id=1, source_target_pairs={{0,8},{8,0},{16,24},{24,16},{1,9},{9,1},{17,25},{25,17},{2,10},{10... | collective-permute-start | bytes 2359304 | tf_op jit(solution)/shard_map/ppermute | solution.py:578
  187.5 22.3 %collective-permute-start.35 = (bf16[384,1024]{1,0:T(8,128)(2,1)S(1)}, bf16[384,1024]{1,0:T(8,128)(2,1)S(1)}, u32[]{:S(2)}, u32[]{:S(2)}) collective-permute-start(bf16[384,1024]{1,0:T(8,128)(2,1)S(1)} %add_convert_fusion.4), channel_id=1, source_target_pairs={{0,16},{8,24},{16,0},{24,8},{1,17},{9,25},{17,1},{25,9},{2,18},{10... | collective-permute-start | bytes 2359304 | tf_op jit(solution)/shard_map/ppermute | solution.py:578
  196.3 18.4 %collective-permute-start.36 = (bf16[4,704,128]{2,1,0:T(8,128)(2,1)}, bf16[4,704,128]{2,1,0:T(8,128)(2,1)S(1)}, u32[]{:S(2)}, u32[]{:S(2)}) collective-permute-start(bf16[4,704,128]{2,1,0:T(8,128)(2,1)} %get-tuple-element.240), channel_id=1, source_target_pairs={{0,1},{1,0},{2,3},{3,2},{4,5},{5,4},{6,7},{7,6},{8,9},{9,8},{10,11... | collective-permute-start | bytes 2162696 | tf_op jit(solution)/shard_map/ppermute | solution.py:593
  214.9 45.3 %collective-permute-start.42 = (bf16[4,704,128]{2,1,0:T(8,128)(2,1)}, bf16[4,704,128]{2,1,0:T(8,128)(2,1)}, u32[]{:S(2)}, u32[]{:S(2)}) collective-permute-start(bf16[4,704,128]{2,1,0:T(8,128)(2,1)} %get-tuple-element.264), channel_id=1, source_target_pairs={{0,1},{1,0},{2,3},{3,2},{4,5},{5,4},{6,7},{7,6},{8,9},{9,8},{10,11... | collective-permute-start | bytes 2162696 | tf_op jit(solution)/shard_map/ppermute | solution.py:593
  238.0 25.3 %collective-permute-start.43 = (bf16[704,128]{1,0:T(8,128)(2,1)S(1)}, bf16[704,128]{1,0:T(8,128)(2,1)S(1)}, u32[]{:S(2)}, u32[]{:S(2)}) collective-permute-start(bf16[704,128]{1,0:T(8,128)(2,1)S(1)} %get-tuple-element.352), channel_id=1, source_target_pairs={{0,2},{1,3},{2,0},{3,1},{4,6},{5,7},{6,4},{7,5},{8,10},{9,11},{10,... | collective-permute-start | bytes 540680 | tf_op jit(solution)/shard_map/ppermute | solution.py:593
  242.4 20.9 %collective-permute-start.44 = (bf16[704,128]{1,0:T(8,128)(2,1)S(1)}, bf16[704,128]{1,0:T(8,128)(2,1)S(1)}, u32[]{:S(2)}, u32[]{:S(2)}) collective-permute-start(bf16[704,128]{1,0:T(8,128)(2,1)S(1)} %get-tuple-element.351), channel_id=1, source_target_pairs={{0,4},{1,5},{2,6},{3,7},{4,0},{5,1},{6,2},{7,3},{8,12},{9,13},{10,... | collective-permute-start | bytes 540680 | tf_op jit(solution)/shard_map/ppermute | solution.py:593
  242.4 20.9 %collective-permute-start.45 = (bf16[704,128]{1,0:T(8,128)(2,1)S(1)}, bf16[704,128]{1,0:T(8,128)(2,1)S(1)}, u32[]{:S(2)}, u32[]{:S(2)}) collective-permute-start(bf16[704,128]{1,0:T(8,128)(2,1)S(1)} %get-tuple-element.350), channel_id=1, source_target_pairs={{0,6},{1,7},{2,4},{3,5},{4,2},{5,3},{6,0},{7,1},{8,14},{9,15},{10,... | collective-permute-start | bytes 540680 | tf_op jit(solution)/shard_map/ppermute | solution.py:593
  259.1 23.4 %collective-permute-start.41 = (bf16[384,1024]{1,0:T(8,128)(2,1)S(1)}, bf16[384,1024]{1,0:T(8,128)(2,1)S(1)}, u32[]{:S(2)}, u32[]{:S(2)}) collective-permute-start(bf16[384,1024]{1,0:T(8,128)(2,1)S(1)} %add_convert_fusion.3), channel_id=1, source_target_pairs={{0,16},{8,24},{16,0},{24,8},{1,17},{9,25},{17,1},{25,9},{2,18},{10... | collective-permute-start | bytes 2359304 | tf_op jit(solution)/shard_map/ppermute | solution.py:578
  261.5 21.1 %collective-permute-start.46 = (bf16[4,704,128]{2,1,0:T(8,128)(2,1)S(1)}, bf16[4,704,128]{2,1,0:T(8,128)(2,1)S(1)}, u32[]{:S(2)}, u32[]{:S(2)}) collective-permute-start(bf16[4,704,128]{2,1,0:T(8,128)(2,1)S(1)} %copy-done.66), channel_id=1, source_target_pairs={{0,1},{1,0},{2,3},{3,2},{4,5},{5,4},{6,7},{7,6},{8,9},{9,8},{10,11... | collective-permute-start | bytes 2162696 | tf_op jit(solution)/shard_map/ppermute | solution.py:593
  263.5 19.1 %collective-permute-start.47 = (bf16[704,128]{1,0:T(8,128)(2,1)S(1)}, bf16[704,128]{1,0:T(8,128)(2,1)S(1)}, u32[]{:S(2)}, u32[]{:S(2)}) collective-permute-start(bf16[704,128]{1,0:T(8,128)(2,1)S(1)} %get-tuple-element.348), channel_id=1, source_target_pairs={{0,2},{1,3},{2,0},{3,1},{4,6},{5,7},{6,4},{7,5},{8,10},{9,11},{10,... | collective-permute-start | bytes 540680 | tf_op jit(solution)/shard_map/ppermute | solution.py:593
  264.6 18.0 %collective-permute-start.48 = (bf16[704,128]{1,0:T(8,128)(2,1)S(1)}, bf16[704,128]{1,0:T(8,128)(2,1)S(1)}, u32[]{:S(2)}, u32[]{:S(2)}) collective-permute-start(bf16[704,128]{1,0:T(8,128)(2,1)S(1)} %get-tuple-element.347), channel_id=1, source_target_pairs={{0,4},{1,5},{2,6},{3,7},{4,0},{5,1},{6,2},{7,3},{8,12},{9,13},{10,... | collective-permute-start | bytes 540680 | tf_op jit(solution)/shard_map/ppermute | solution.py:593
  294.1 19.4 %collective-permute-start.55 = (bf16[384,1024]{1,0:T(8,128)(2,1)S(1)}, bf16[384,1024]{1,0:T(8,128)(2,1)S(1)}, u32[]{:S(2)}, u32[]{:S(2)}) collective-permute-start(bf16[384,1024]{1,0:T(8,128)(2,1)S(1)} %add_convert_fusion.1), channel_id=1, source_target_pairs={{0,16},{8,24},{16,0},{24,8},{1,17},{9,25},{17,1},{25,9},{2,18},{10... | collective-permute-start | bytes 2359304 | tf_op jit(solution)/shard_map/ppermute | solution.py:578
  306.0 20.3 %collective-permute-start.57 = (bf16[4,776,128]{2,1,0:T(8,128)(2,1)}, bf16[4,776,128]{2,1,0:T(8,128)(2,1)}, u32[]{:S(2)}, u32[]{:S(2)}) collective-permute-start(bf16[4,776,128]{2,1,0:T(8,128)(2,1)} %get-tuple-element.306), channel_id=1, source_target_pairs={{0,1},{1,0},{2,3},{3,2},{4,5},{5,4},{6,7},{7,6},{8,9},{9,8},{10,11... | collective-permute-start | bytes 2383880 | tf_op jit(solution)/shard_map/ppermute | solution.py:593
  320.5 28.4 %collective-permute-start.69 = (bf16[2112,128]{1,0:T(8,128)(2,1)S(1)}, bf16[2112,128]{1,0:T(8,128)(2,1)}, u32[]{:S(2)}, u32[]{:S(2)}) collective-permute-start(bf16[2112,128]{1,0:T(8,128)(2,1)S(1)} %pad_maximum_fusion.4.p0), channel_id=1, source_target_pairs={{0,16},{8,24},{16,0},{24,8},{1,17},{9,25},{17,1},{25,9},{2,18},{10... | collective-permute-start | bytes 1622024 | tf_op jit(solution)/shard_map/ppermute | solution.py:578
  322.8 21.0 %all-to-all-start = ((bf16[4,384,256]{2,1,0:T(8,128)(2,1)}), bf16[4,384,256]{2,1,0:T(8,128)(2,1)S(1)}, u32[]{:S(2)}, u32[]{:S(2)}) async-start(bf16[4,384,256]{2,1,0:T(8,128)(2,1)} %get-tuple-element.301), calls=%async_computation | async-start | bytes 1572864 | tf_op jit(solution)/shard_map/all_to_all | solution.py:853
  328.0 19.2 %collective-permute-start.61 = (bf16[776,128]{1,0:T(8,128)(2,1)S(1)}, bf16[776,128]{1,0:T(8,128)(2,1)S(1)}, u32[]{:S(2)}, u32[]{:S(2)}) collective-permute-start(bf16[776,128]{1,0:T(8,128)(2,1)S(1)} %get-tuple-element.336), channel_id=1, source_target_pairs={{0,2},{1,3},{2,0},{3,1},{4,6},{5,7},{6,4},{7,5},{8,10},{9,11},{10,... | collective-permute-start | bytes 595976 | tf_op jit(solution)/shard_map/ppermute | solution.py:593
  (112 other events, 1059.0 us)
Sparse Core Ops, SparseCore 0:
  24.1 61.7 all-gather.1
where the time goes:
time: 376 us; the launch traced here: 370 us
  Pallas kernels  167 us (44%)
  starting transfers between devices  78.4 us (21%)
  waiting for transfers between devices  70.8 us (19%)
  local copies, waits for them, and re-layouts  20.6 us (5%)
  other arithmetic  17.7 us (5%)
  between operations  15.3 us (4%)
    pallas_call x14, Pallas kernels, vmem_call(): pl.pallas_call(kernel, grid_spec=pltpu.PrefetchScalarGridSpec(num_scalar_...  75.5 us
    ppermute x34, starting transfers between devices, fsdp_permute(): return lax.ppermute(value, 'fsdp', [(i, i ^ flip) for i in range(n)])  57.3 us
    ppermute x34, waiting for transfers between devices, fsdp_permute(): return lax.ppermute(value, 'fsdp', [(i, i ^ flip) for i in range(n)])  46.2 us
    pallas_call x2, Pallas kernels, any_call(): pl.pallas_call(kernel, grid_spec=pltpu.PrefetchScalarGridSpec(num_scalar_...  33.8 us
    pallas_call x2, Pallas kernels, attention_back(): pl.pallas_call(attn_back_kernel, grid_spec=pltpu.PrefetchScalarGridSpec(n...  28.8 us
    ppermute x38, waiting for transfers between devices, seq_permute(): return lax.ppermute(value, 'seq', [(i, i ^ flip) for i in range(GROUPS)])  23.4 us
    ppermute x38, starting transfers between devices, seq_permute(): return lax.ppermute(value, 'seq', [(i, i ^ flip) for i in range(GROUPS)])  17.6 us
    pallas_call x2, Pallas kernels, attention(): pl.pallas_call(attn_kernel, grid_spec=pltpu.PrefetchScalarGridSpec(num_sc...  17.5 us
  transfers between devices with their start and end apart: 74, of which 22 were waited for; matrix products, arithmetic and copies ran while one was open for 6% of the time, Pallas kernels for 36%

commit v1 on v0

--- a/solution.py
+++ b/solution.py
@@ -262,7 +262,7 @@
     )(me, q, k, v, *b, lse, cosine, sine, *before)
 
 
-def out_kernel(me, m0, m1, m2, m3, w0, x0, x1, x2, x3, t, gains, middle, second):
+def out_kernel(me, m0, m1, m2, m3, w0, x0, x1, x2, x3, t, gains, middle, lo, hi):
     s = me[0]
     width = m0.shape[1]
     quarter = x0.shape[0]
@@ -278,7 +278,9 @@
                 part = one if part is None else part + one
             middle[:, cols] = t[:, cols].astype(F32) + part
     acc = middle[...]
-    second[...] = (acc * inverse_rms(acc) * gains[1:2].astype(F32)).astype(BF16)
+    second = (acc * inverse_rms(acc) * gains[1:2].astype(F32)).astype(BF16)
+    lo[...] = second[: lo.shape[0]]
+    hi[...] = second[lo.shape[0] :]
 
 
 def vmem_call(kernel, name, shapes, me, args, estimate, scratch=()):
@@ -300,25 +302,32 @@
     )(me, *args)
 
 
-def mlp_kernel(count, me, sa, sb, ga, gb, down, *refs):
-    pieces, outs = refs[:count], refs[count : count + 5]
-    sv, gv, wv, dv, hid, gback, uback, sback, sems = refs[count + 5 :]
-    units, d = dv.shape
-    share = d // count
-    rows = sa.shape[0]
-    copies = [pltpu.make_async_copy(sa, sv.at[0], sems.at[0])]
-    parts = [[], []]
-    for h in range(2):
-        for i, piece in enumerate(pieces):
-            at = pl.ds(pl.multiple_of((me[0] ^ i) * share, share), share)
-            part = piece.at[h * units : (h + 1) * units]
-            sem = sems.at[15 + h * count + i]
-            parts[h].append(pltpu.make_async_copy(part, wv.at[h, :, at], sem))
+def mlp_kernel(count, me, sa0, sa1, sb0, sb1, ga, gb, *refs):
+    pieces, outs = refs[: 3 * count], refs[3 * count : 3 * count + 5]
+    sv, gv, wv, hid, gback, uback, sback, sems = refs[3 * count + 5 :]
+    _, units, d = wv.shape
+    rows = ga.shape[0]
+    copies = [pltpu.make_async_copy(sa0, sv.at[0, : rows // 2], sems.at[0])]
+    copies.append(pltpu.make_async_copy(sa1, sv.at[0, rows // 2 :], sems.at[1]))
+    parts = []
+    for h in range(3):
+        loads = []
+        if count == 1:
+            loads.append((pieces[h], wv.at[h]))
+        else:
+            share = d // 8
+            for k in range(4):
+                mine, other = pieces[h * count + k], pieces[h * count + 4].at[k * units : (k + 1) * units]
+                for piece, flip in ((mine, 2 * k), (other, 2 * k + 1)):
+                    at = pl.ds(pl.multiple_of((me[0] ^ flip) * share, share), share)
+                    loads.append((piece, wv.at[h, :, at]))
+        sem = lambda i, h=h: sems.at[15 + 8 * h + i]
+        parts.append([pltpu.make_async_copy(a, b, sem(i)) for i, (a, b) in enumerate(loads)])
     copies.append(pltpu.make_async_copy(ga, gv.at[0], sems.at[4]))
-    copies.append(pltpu.make_async_copy(down.at[down.shape[0] - units :], dv, sems.at[1]))
-    copies.append(pltpu.make_async_copy(sb, sv.at[1], sems.at[5]))
+    copies.append(pltpu.make_async_copy(sb0, sv.at[1, : rows // 2], sems.at[2]))
+    copies.append(pltpu.make_async_copy(sb1, sv.at[1, rows // 2 :], sems.at[5]))
     copies.append(pltpu.make_async_copy(gb, gv.at[1], sems.at[6]))
-    for copy in copies[:1] + parts[0] + parts[1] + copies[1:]:
+    for copy in copies[:2] + parts[0] + parts[1] + copies[2:3] + parts[2] + copies[3:]:
         copy.start()
     writes = []
 
@@ -329,6 +338,7 @@
 
     for i in range(2):
         copies[3 if i else 0].wait()
+        copies[4 if i else 1].wait()
         if i == 0:
             for copy in parts[0]:
                 copy.wait()
@@ -342,10 +352,11 @@
         hid[i] = (act * up).astype(BF16)
         at = slice(i * rows, (i + 1) * rows)
         write(hid.at[i], outs[0].at[at])
-        copies[4 if i else 1].wait()
+        copies[5 if i else 2].wait()
         if i == 0:
-            copies[2].wait()
-        hb = nt(gv[i], dv[...])
+            for copy in parts[2]:
+                copy.wait()
+        hb = nt(gv[i], wv[2])
         gate_back = (hb * up * sg * (1.0 + gate * (1.0 - sg))).astype(BF16)
         up_back = (hb * act).astype(BF16)
         gback[i] = gate_back
@@ -375,38 +386,46 @@
     )(me, *args)
 
 
-def mlp(where, sa, sb, ga, gb, pieces, down):
-    rows, d = sa.shape
-    units = pieces[0].shape[0] // 2
+def mlp(where, sa, sb, ga, gb, pieces):
+    rows, d = ga.shape
+    units = pieces[0][0].shape[0]
     part = ((2 * rows, units), BF16)
     return any_call(
-        functools.partial(mlp_kernel, len(pieces)),
+        functools.partial(mlp_kernel, len(pieces[0])),
         "mlp",
         [part] * 3 + [((rows, d), BF16)] * 2,
         where.reshape(1),
-        [sa, sb, ga, gb, down, *pieces],
+        [*sa, *sb, ga, gb] + [one for some in pieces for one in some],
         cost(2 * 5 * 2 * rows * d * units, 12e6, 2 * rows * units),
         [pltpu.VMEM((2, rows, d), BF16)] * 2
-        + [pltpu.VMEM((2, units, d), BF16), pltpu.VMEM((units, d), BF16)]
+        + [pltpu.VMEM((3, units, d), BF16)]
         + [pltpu.VMEM((2, rows, units), BF16)] * 3
-        + [pltpu.VMEM((2, rows, d), BF16), pltpu.SemaphoreType.DMA((15 + 2 * len(pieces),))],
-    )
-
-
-def mlp_out_kernel(me, hn, hf, rest, o0, o1, o2, o3):
-    rows = o0.shape[0]
-    w = rest.at[rest.shape[0] - hn.shape[1] :]
-    for h, outs in ((hn, (o0, o1)), (hf, (o2, o3))):
-        for i, out in enumerate(outs):
+        + [pltpu.VMEM((2, rows, d), BF16), pltpu.SemaphoreType.DMA((39,))],
+    )
+
+
+def mlp_out_kernel(count, me, hn, hf, *refs):
+    pieces, outs, w = refs[:count], refs[count : count + 4], refs[-1]
+    units, d = w.shape
+    rows = outs[0].shape[0]
+    if count == 1:
+        w[...] = pieces[0][...]
+    else:
+        share = d // 8
+        for k in range(4):
+            for piece, flip in ((pieces[k], 2 * k), (pieces[4].at[k * units : (k + 1) * units], 2 * k + 1)):
+                w[:, pl.ds(pl.multiple_of((me[0] ^ flip) * share, share), share)] = piece[...]
+    for h, pair in ((hn, outs[:2]), (hf, outs[2:])):
+        for i, out in enumerate(pair):
             out[...] = nn(h[i * rows : (i + 1) * rows], w[...]).astype(BF16)
 
 
 def unit_grad_kernel(count, me, *refs):
-    ins, outs, acc = refs[: 2 * count + 4], refs[2 * count + 4 : -1], refs[-1]
-    blocks = ins[2 * count :]
+    ins, outs, acc = refs[: -1 - 2 * count], refs[-1 - 2 * count : -1], refs[-1]
+    blocks = [block[...] for block in ins[2 * count :]]
     y = me[0] % 2
-    near = jnp.concatenate([blocks[0][...], blocks[1][...]], axis=0)
-    far = jnp.concatenate([blocks[2][...], blocks[3][...]], axis=0)
+    near = jnp.concatenate(blocks[: len(blocks) // 2], axis=0)
+    far = jnp.concatenate(blocks[len(blocks) // 2 :], axis=0)
     share = outs[0].shape[2]
     for i in range(count):
         acc[...] = tn(ins[2 * i][...], near) + tn(ins[2 * i + 1][...], far)
@@ -420,7 +439,8 @@
     n = lax.axis_size("fsdp")
     units, d = pairs[0][0].shape[1], blocks[0].shape[1]
     if n != 8:
-        near, far = jnp.concatenate(blocks[:2]), jnp.concatenate(blocks[2:])
+        half = len(blocks) // 2
+        near, far = jnp.concatenate(blocks[:half]), jnp.concatenate(blocks[half:])
         outs = [(tn(a, near) + tn(b, far)).astype(BF16) for a, b in pairs]
         return [(jnp.transpose(o.reshape(units, n, d // n), (1, 0, 2)),) for o in outs]
     me = lax.axis_index("fsdp").astype(jnp.int32).reshape(1)
@@ -430,7 +450,7 @@
         [((n // 2, units, d // n), BF16)] * (2 * len(pairs)),
         me,
         [a for pair in pairs for a in pair] + list(blocks),
-        cost(2 * 4 * blocks[0].shape[0] * units * d * len(pairs), 6e6),
+        cost(1, 1),
         [pltpu.VMEM((units, d), F32)],
     )
     return [outs[2 * i : 2 * i + 2] for i in range(len(pairs))]
@@ -640,7 +660,6 @@
     own_qkv += [gains, columns(out_weight, core, d // 2).T]
     own_qkv = jnp.concatenate(own_qkv, axis=0)
     own_units = [columns(w, s, units).T for w in (gate_weight, up_weight, down_weight)]
-    own_units, own_down = jnp.concatenate(own_units[:2], axis=0), own_units[2]
     places = (jnp.arange(4, dtype=jnp.int32) ^ s)[:, None] * rows + jnp.arange(rows, dtype=jnp.int32)
     half_dim = HEAD_DIM // 2
     freqs = jnp.exp(jnp.arange(half_dim, dtype=F32) * (-2.0 * math.log(10000.0) / HEAD_DIM))
@@ -659,57 +678,67 @@
             pieces += [one, fsdp_permute(one, 1)]
     else:
         pieces = [lax.all_gather(own_qkv, "fsdp", axis=1, tiled=True)]
-        unit_pieces = [lax.all_gather(own_units, "fsdp", axis=1, tiled=True)]
-    w_down = lax.all_gather(own_down, "fsdp", axis=1, tiled=True)
+        unit_pieces = [[lax.all_gather(w, "fsdp", axis=1, tiled=True)] for w in own_units]
     where = here if ring else jnp.int32(0)
     packed1 = seq_permute(jnp.concatenate([t0, f[1]], axis=1), 1)
     crossing = jnp.concatenate([packed2[:, :d], packed2[:, d + width :]], axis=1)
     if ring:
-        crossing = after(crossing, *pieces[1::2])
+        def pair_send(own, *waits):
+            own = after(own, *waits)
+            return [own] + [fsdp_permute(own, flip) for flip in (2, 4, 6)]
+
+        gate_w = pair_send(own_units[0], *first, pieces[1], pieces[3])
+        crossing = after(crossing, *pieces[1::2], *gate_w)
     packed3 = seq_permute(crossing, 1)
 
     if ring:
-        sent = after(own_units, pieces[3])
-        second = [fsdp_permute(sent, flip) for flip in (2, 4, 6)]
-        second_y = fsdp_permute(after(own_units, pieces[5]), 1)
+        gate_w.append(fsdp_permute(jnp.concatenate(gate_w, axis=0), 1))
+        up_w = pair_send(own_units[1], gate_w[1])
     g2 = seq_permute(after(g0, packed2, *pieces[1::2]), 2)
 
     q, k, v, normed, w_qkv = qkv(where, t0, f[0], (packed1, packed2, packed3), pieces, cosine, sine)
     gains = w_qkv[3 * width : 3 * width + 8]
     w_out_sent = w_qkv[3 * width + 8 :]
     *m, lse_a = attention(0, me, q, k, v)
+    g2 = after(g2, m[0])
+    q = after(q, g2)
+    g1, g3 = seq_permute(after(g0, g2), 1), seq_permute(g2, 1)
+    if ring:
+        up_w[1:] = all_after(up_w[1:], m[0])
+        gate_w[4] = after(gate_w[4], m[0])
+        up_w.append(fsdp_permute(jnp.concatenate(up_w, axis=0), 1))
+        down_w = pair_send(own_units[2], *up_w[:4])
+        q = after(q, gate_w[4])
     *m, lse_b = attention(1, me, q, k, v, *m)
-    g2 = after(g2, m[0])
-    if ring:
-        second_y, *second = all_after([second_y] + second, m[0])
-        m = all_after(m, second_y, *second)
-    m = all_after(m, g2)
+    if ring:
+        up_w[4] = after(up_w[4], m[0])
+        down_w[1:] = all_after(down_w[1:], m[0])
+        down_w.append(fsdp_permute(jnp.concatenate(down_w, axis=0), 1))
+        m = all_after(m, up_w[4])
     m = exchange_four(m)
+    if ring:
+        m = all_after(m, *down_w[:4])
     w_out_sent = after(w_out_sent, m[2], m[3])
     w_out_other = [
         seq_permute(lax.slice_in_dim(w_out_sent, i * (d // 8), (i + 1) * (d // 8)), 1) for i in range(4)
     ]
     if ring:
-        unit_pieces = [own_units, second_y]
-        for one in second:
-            unit_pieces += [one, after(fsdp_permute(one, 1), m[1])]
-        m = all_after(m, *unit_pieces[3::2])
-    m = all_after(m, *w_out_other, w_down)
-    middle, second = vmem_call(
+        unit_pieces = [gate_w, up_w, down_w]
+    m = all_after(m, *w_out_other)
+    middle, *s0 = vmem_call(
         out_kernel,
         "out",
-        [((rows, d), F32), ((rows, d), BF16)],
+        [((rows, d), F32)] + [((rows // 2, d), BF16)] * 2,
         me,
         [*m, w_qkv, *w_out_other, t0, gains],
         cost(2 * rows * d * d, 8e6),
     )
-    s0, s1, s2 = second, seq_permute(second, 1), seq_permute(second, 2)
-    g1 = seq_permute(after(g0, second), 1)
-    g3 = seq_permute(g2, 1)
-    hid_near, gate_near, up_near, sb0, sb1 = mlp(where, s0, s1, g0, g1, unit_pieces, w_down)
-    s2 = after(s2, sb0)
-    s3 = seq_permute(s2, 1)
-    hid_far, gate_far, up_far, sb2, sb3 = mlp(where, s2, s3, g2, g3, unit_pieces, w_down)
+    s1 = [seq_permute(one, 1) for one in s0]
+    s2 = [seq_permute(one, 2) for one in s0]
+    hid_near, gate_near, up_near, sb0, sb1 = mlp(where, s0, s1, g0, g1, unit_pieces)
+    s2 = all_after(s2, sb0)
+    s3 = [seq_permute(one, 1) for one in s2]
+    hid_far, gate_far, up_far, sb2, sb3 = mlp(where, s2, s3, g2, g3, unit_pieces)
     sb_both = add(sb2, seq_permute(sb3, 1))
     p = [sb0, seq_permute(after(sb1, sb_both), 1), seq_permute(sb_both, 2)]
 
@@ -717,14 +746,15 @@
     if ring:
         down_crossed = fsdp_permute(down_part[1], 1)
     o = vmem_call(
-        mlp_out_kernel,
+        functools.partial(mlp_out_kernel, len(unit_pieces[2])),
         "mlp_out",
         [((rows, d), BF16)] * 4,
-        me,
-        [hid_near, after(hid_far, down_part[0]), w_down],
+        where.reshape(1),
+        [hid_near, after(hid_far, down_part[0]), *unit_pieces[2]],
         cost(2 * 4 * rows * d * units, 8e6),
-    )
-    (gate_part,) = unit_grads([(gate_near, after(gate_far, o[0]))], (s0, s1, s2, s3))
+        [pltpu.VMEM((units, d), BF16)],
+    )
+    (gate_part,) = unit_grads([(gate_near, after(gate_far, o[0]))], (*s0, *s1, *s2, *s3))
     o1, o3 = all_after([seq_permute(o[1], 1), seq_permute(o[3], 1)], gate_part[0])
     p[2] = after(p[2], gate_part[0])
     p[0] = after(p[0], o3, o1)
@@ -759,11 +789,11 @@
             cost(2 * rows * d * d, 6e6),
             [pltpu.VMEM((d // 2, d), F32)],
         )
-        (up_part,) = unit_grads([(up_near, after(up_far, out_part[0]))], (s0, s1, s2, s3))
+        (up_part,) = unit_grads([(up_near, after(up_far, out_part[0]))], (*s0, *s1, *s2, *s3))
         b[1:] = all_after(b[1:], up_part[0], o_both)
         down_sent = fsdp_send(after(down_both, b[2], b[3]))
     else:
-        (up_part,) = unit_grads([(up_near, up_far)], (s0, s1, s2, s3))
+        (up_part,) = unit_grads([(up_near, up_far)], (*s0, *s1, *s2, *s3))
 
     def qkv_grads(d_a, d_b):
         if ring:
@@ -822,6 +852,8 @@
         up_share = add(*all_after(up_sent, qkv_sums[0]))
         out_sent = fsdp_send(after(out_both, up_share))
         beside = after(beside, up_share)
+        units_sent = jnp.concatenate([gate_share, up_share, down_share], axis=0)
+        units_far = seq_permute(units_sent, 2)
     (tokens_grad,) = vmem_call(
         final_kernel,
         "final",
@@ -831,10 +863,10 @@
         cost(0, 6e6),
     )
     if ring:
+        units_far = after(units_far, tokens_grad)
         qkv_both = add(qkv_sums[0], after(qkv_crossed, tokens_grad))
         out_share = add(*all_after(out_sent, tokens_grad))
         qkv_sent = fsdp_send(after(qkv_both, out_share))
-        units_sent = after(jnp.concatenate([gate_share, up_share, down_share], axis=0), tokens_grad)
     else:
         gate_share, up_share, down_share, qkv_share = (
             scatter_whole(v[0]) for v in (gate_part, up_part, down_part, qkv_sums)
@@ -849,25 +881,13 @@
         whole = (keep + seq_permute(send, 1).astype(F32)).astype(BF16)
         out_share = scatter_whole(jnp.transpose(whole, (1, 0, 2)))
         units_sent = jnp.concatenate([gate_share, up_share, down_share], axis=0)
-    out_share = add(out_share, seq_permute(out_share, 2))
     v_all = lax.all_to_all(after(v_b, tokens_grad), "seq", split_axis=0, concat_axis=0)
     output = add(middle, o[0], o1, o2)[None]
-    out_grad, second_gain_grad = vmem_call(
-        place_out_kernel,
-        "place_out",
-        [((share, d), F32), ((1, share), F32)],
-        me,
-        [out_share, seq_permute(out_share, 1)],
-        cost(0, 1e6),
-    )
     (values_grad,) = vmem_call(
         place_values_kernel, "place_values", [((rows, d), F32)], me, [v_all], cost(0, 3e6)
     )
-    units_far = seq_permute(units_sent, 2)
-    if ring:
-        qkv_share = add(*all_after(qkv_sent, out_grad, values_grad, output))
-        units_far = after(units_far, qkv_share)
-    qkv_far = seq_permute(qkv_share, 2)
+    if not ring:
+        units_far = seq_permute(units_sent, 2)
     gate_grad, up_grad, down_grad = vmem_call(
         place_units_kernel,
         "place_units",
@@ -877,7 +897,22 @@
         cost(0, 3e6),
         [pltpu.VMEM((4, 3 * units, share), F32)],
     )
-    qkv_far = after(qkv_far, gate_grad)
+    if ring:
+        out_far = after(seq_permute(after(out_share, qkv_both), 2), gate_grad)
+    else:
+        out_far = seq_permute(out_share, 2)
+    out_share = add(out_share, out_far)
+    out_grad, second_gain_grad = vmem_call(
+        place_out_kernel,
+        "place_out",
+        [((share, d), F32), ((1, share), F32)],
+        me,
+        [out_share, seq_permute(out_share, 1)],
+        cost(0, 1e6),
+    )
+    if ring:
+        qkv_share = add(*all_after(qkv_sent, out_grad, values_grad, output, gate_grad))
+    qkv_far = seq_permute(qkv_share, 2)
     qkv_all = [qkv_share, seq_permute(qkv_share, 1), qkv_far, seq_permute(qkv_far, 1)]
     query_grad, key_grad, value_grad, gain_grad = vmem_call(
         place_qkv_kernel,

time: 376 us -> 361 us (0.960)
  waiting for transfers between devices: 70.8 us -> 53.6 us
  between operations: 15.3 us -> 1.91 us
  local copies, waits for them, and re-layouts: 20.6 us -> 27.8 us
  starting transfers between devices: 78.4 us -> 83.3 us
    ppermute x34 -> x39, waiting for transfers between devices: 46.2 us -> 25.6 us  [fsdp_permute(): return lax.ppermute(value, 'fsdp', [(i, i ^ flip) for i in range(n)])]
    ppermute x38 -> x41, waiting for transfers between devices: 23.4 us -> 28 us  [seq_permute(): return lax.ppermute(value, 'seq', [(i, i ^ flip) for i in range(GROUPS)])]
    ppermute x38 -> x41, starting transfers between devices: 17.6 us -> 21.4 us  [seq_permute(): return lax.ppermute(value, 'seq', [(i, i ^ flip) for i in range(GROUPS)])]
    ppermute x34 -> x39, starting transfers between devices: 57.3 us -> 58.4 us  [fsdp_permute(): return lax.ppermute(value, 'fsdp', [(i, i ^ flip) for i in range(n)])]
    unnamed x147 -> x157, local copies, waits for them, and re-layouts: 10.9 us -> 10.8 us
  transfers between devices with their start and end apart: 74 -> 81, of which waited for: 22 -> 20; matrix products, arithmetic and copies ran while one was open for 6% -> 9% of each run, Pallas kernels for 36% -> 39%
where the time goes in v1:
time: 361 us; the launch traced here: 354 us
  Pallas kernels  168 us (47%)
  starting transfers between devices  83.3 us (23%)
  waiting for transfers between devices  53.6 us (15%)
  local copies, waits for them, and re-layouts  27.8 us (8%)
  other arithmetic  19 us (5%)
    pallas_call x14, Pallas kernels, vmem_call(): pl.pallas_call(kernel, grid_spec=pltpu.PrefetchScalarGridSpec(num_scalar_...  76 us
    ppermute x39, starting transfers between devices, fsdp_permute(): return lax.ppermute(value, 'fsdp', [(i, i ^ flip) for i in range(n)])  58.4 us
    pallas_call x2, Pallas kernels, any_call(): pl.pallas_call(kernel, grid_spec=pltpu.PrefetchScalarGridSpec(num_scalar_...  34 us
    pallas_call x2, Pallas kernels, attention_back(): pl.pallas_call(attn_back_kernel, grid_spec=pltpu.PrefetchScalarGridSpec(n...  28.9 us
    ppermute x41, waiting for transfers between devices, seq_permute(): return lax.ppermute(value, 'seq', [(i, i ^ flip) for i in range(GROUPS)])  28 us
    ppermute x39, waiting for transfers between devices, fsdp_permute(): return lax.ppermute(value, 'fsdp', [(i, i ^ flip) for i in range(n)])  25.6 us
    ppermute x41, starting transfers between devices, seq_permute(): return lax.ppermute(value, 'seq', [(i, i ^ flip) for i in range(GROUPS)])  21.4 us
    pallas_call x2, Pallas kernels, attention(): pl.pallas_call(attn_kernel, grid_spec=pltpu.PrefetchScalarGridSpec(num_sc...  17.5 us
  transfers between devices with their start and end apart: 81, of which 20 were waited for; matrix products, arithmetic and copies ran while one was open for 9% of the time, Pallas kernels for 39%

profile of v1, /device:TPU:0, one launch (start us, length us, event | category | flops | bytes accessed | tf_op | source)
XLA Modules:
  0.0 353.6 jit_solution(10851477511339033079)
XLA Ops:
  3.9 2.9 collective-permute-start.1
  22.2 5.0 %fusion = (f32[4,384,128]{2,1,0:T(8,128)}, f32[4,384,128]{2,1,0:T(8,128)}) fusion(f32[128]{0:T(128)} %mul.78, f32[128]{0:T(128)} %mul.75, f32[4,384]{1,0:T(4,128)S(1)} %add_convert_fusion.15), kind=kLoop, calls=%fused_computation.14 | loop fusion | flops 393216 | bytes 1580032 | tf_op jit(solution)/shard_map/mul | solution.py:668
  28.8 9.5 %collective-permute-done.5.refs_4_ = bf16[1288,128]{1,0:T(8,128)(2,1)} collective-permute-done((bf16[1288,128]{1,0:T(8,128)(2,1)S(1)}, bf16[1288,128]{1,0:T(8,128)(2,1)}, u32[]{:S(2)}, u32[]{:S(2)}) %collective-permute-start.5) | collective-permute-done | bytes 329760 | tf_op jit(solution)/shard_map/ppermute | solution.py:613
  40.6 5.2 %collective-permute-start.10 = (bf16[704,128]{1,0:T(8,128)(2,1)S(1)}, bf16[704,128]{1,0:T(8,128)(2,1)S(1)}, u32[]{:S(2)}, u32[]{:S(2)}) collective-permute-start(bf16[704,128]{1,0:T(8,128)(2,1)S(1)} %bitcast.90), channel_id=1, source_target_pairs={{0,4},{1,5},{2,6},{3,7},{4,0},{5,1},{6,2},{7,3},{8,12},{9,13},{10,... | collective-permute-start | bytes 540680 | tf_op jit(solution)/shard_map/ppermute | solution.py:613
  49.6 7.7 %collective-permute-done.10.refs_2_ = bf16[704,128]{1,0:T(8,128)(2,1)S(1)} collective-permute-done((bf16[704,128]{1,0:T(8,128)(2,1)S(1)}, bf16[704,128]{1,0:T(8,128)(2,1)S(1)}, u32[]{:S(2)}, u32[]{:S(2)}) %collective-permute-start.10) | collective-permute-done | bytes 180256 | tf_op jit(solution)/shard_map/ppermute | solution.py:613
  59.6 3.2 collective-permute-start.15
  68.2 11.5 %qkv.1 = (bf16[4,384,256]{2,1,0:T(8,128)(2,1)}, bf16[4,384,256]{2,1,0:T(8,128)(2,1)}, bf16[4,384,256]{2,1,0:T(8,128)(2,1)}, bf16[4,384,1024]{2,1,0:T(8,128)(2,1)}, bf16[1288,1024]{1,0:T(8,128)(2,1)}) custom-call(s32[1]{0:T(128)} %bitcast.1.me, bf16[384,1024]{1,0:T(8,128)(2,1)} %bitcast.70, bf16[384,256]{1,0:T(8,128)(2,1)} %get-tuple-element.344.f0, ...), custom_call_target="tpu_custom_call" | custom-call | flops 1 | bytes 1 | tf_op jit(solution)/shard_map/qkv/pallas_call | solution.py:95
  79.7 8.4 %attention.2 = (bf16[384,128]{1,0:T(8,128)(2,1)}, bf16[384,128]{1,0:T(8,128)(2,1)}, bf16[384,128]{1,0:T(8,128)(2,1)}, bf16[384,128]{1,0:T(8,128)(2,1)}, f32[2,4,8,384]{3,2,1,0:T(8,128)}) custom-call(s32[1]{0:T(128)} %bitcast.me, bf16[4,384,256]{2,1,0:T(8,128)(2,1)} %get-tuple-element.275.q, bf16[4,384,256]{2,1,0:T(8,128)(2,1)} %get-tuple-element.178.k, ...), custom_call_target="tpu_custom_call" | custom-call | flops 1 | bytes 1 | tf_op jit(solution)/shard_map/attention/pallas_call | solution.py:163
  97.4 9.1 %attention.3 = (bf16[384,256]{1,0:T(8,128)(2,1)}, bf16[384,256]{1,0:T(8,128)(2,1)}, bf16[384,256]{1,0:T(8,128)(2,1)}, bf16[384,256]{1,0:T(8,128)(2,1)}, f32[2,4,8,384]{3,2,1,0:T(8,128)}) custom-call(s32[1]{0:T(128)} %bitcast.me, bf16[4,384,256]{2,1,0:T(8,128)(2,1)} %get-tuple-element.275.q, bf16[4,384,256]{2,1,0:T(8,128)(2,1)} %get-tuple-element.178.k, ...), custom_call_target="tpu_custom_call" | custom-call | flops 1 | bytes 1 | tf_op jit(solution)/shard_map/attention/pallas_call | solution.py:163
  111.2 4.5 %collective-permute-done.20.m2 = bf16[384,256]{1,0:T(8,128)(2,1)S(1)} collective-permute-done((bf16[384,256]{1,0:T(8,128)(2,1)}, bf16[384,256]{1,0:T(8,128)(2,1)S(1)}, u32[]{:S(2)}, u32[]{:S(2)}) %collective-permute-start.20) | collective-permute-done | bytes 196640 | tf_op jit(solution)/shard_map/ppermute | solution.py:598
  115.7 3.3 collective-permute-done.21.m3
  124.2 5.9 %out.1 = (f32[384,1024]{1,0:T(8,128)}, bf16[192,1024]{1,0:T(8,128)(2,1)}, bf16[192,1024]{1,0:T(8,128)(2,1)}) custom-call(s32[1]{0:T(128)} %bitcast.me, bf16[384,256]{1,0:T(8,128)(2,1)} %get-tuple-element.211.m0, bf16[384,256]{1,0:T(8,128)(2,1)} %copy-done.27, bf16[384,256]{1,0:T(8,128)(2,1)} %copy-done.29, bf16[384,256]{1,0:T(8,128)(2,1)} %copy-done.31, ...), custom_call_target="tpu_custom_call" | custom-call | flops 1 | bytes 1 | tf_op jit(solution)/shard_map/out/pallas_call | solution.py:289
  134.4 12.6 %mlp.2 = (bf16[768,704]{1,0:T(8,128)(2,1)}, bf16[768,704]{1,0:T(8,128)(2,1)}, bf16[768,704]{1,0:T(8,128)(2,1)}, bf16[384,1024]{1,0:T(8,128)(2,1)}, bf16[384,1024]{1,0:T(8,128)(2,1)}) custom-call(s32[1]{0:T(128)} %bitcast.1.me, bf16[192,1024]{1,0:T(8,128)(2,1)} %get-tuple-element.216.sa0.refs_2_, bf16[192,1024]{1,0:T(8,128)(2,1)} %get-tuple-element.217.sa1.refs_3_, ...), custom_call_target="tpu_custom_call" | custom-call | flops 1 | bytes 1 | tf_op jit(solution)/shard_map/mlp/pallas_call | solution.py:373
  147.1 3.4 collective-permute-done.34.sa1.refs_7_
  153.6 21.4 %mlp.3 = (bf16[768,704]{1,0:T(8,128)(2,1)}, bf16[768,704]{1,0:T(8,128)(2,1)}, bf16[768,704]{1,0:T(8,128)(2,1)}, bf16[384,1024]{1,0:T(8,128)(2,1)}, bf16[384,1024]{1,0:T(8,128)(2,1)}) custom-call(s32[1]{0:T(128)} %bitcast.1.me, bf16[192,1024]{1,0:T(8,128)(2,1)} %copy-done.10, bf16[192,1024]{1,0:T(8,128)(2,1)} %copy-done.11, bf16[192,1024]{1,0:T(8,128)(2,1)} %copy-done.12, ...), custom_call_target="tpu_custom_call" | custom-call | flops 1 | bytes 1 | tf_op jit(solution)/shard_map/mlp/pallas_call | solution.py:373
  181.4 6.7 %unit_grads.3 = (bf16[4,704,128]{2,1,0:T(8,128)(2,1)}, bf16[4,704,128]{2,1,0:T(8,128)(2,1)}) custom-call(s32[1]{0:T(128)} %bitcast.1.me, bf16[768,704]{1,0:T(8,128)(2,1)} %get-tuple-element.219.refs_0_.hn, bf16[768,704]{1,0:T(8,128)(2,1)} %get-tuple-element.230.refs_1_.hf, bf16[384,1024]{1,0:T(8,128)(2,1)} %bitcast.78, bf16[384,1024]{1,0:T(8,128)(2,1)} %copy-done.16, ...), custom_call_target="tpu_custom_call" | custom-call | flops 1 | bytes 1 | tf_op jit(solution)/shard_map/unit_grads/pallas_call | solution.py:289
  189.6 6.1 %mlp_out.1 = (bf16[384,1024]{1,0:T(8,128)(2,1)}, bf16[384,1024]{1,0:T(8,128)(2,1)}, bf16[384,1024]{1,0:T(8,128)(2,1)}, bf16[384,1024]{1,0:T(8,128)(2,1)}) custom-call(s32[1]{0:T(128)} %bitcast.1.me, bf16[768,704]{1,0:T(8,128)(2,1)} %get-tuple-element.219.refs_0_.hn, bf16[768,704]{1,0:T(8,128)(2,1)} %get-tuple-element.230.refs_1_.hf, ...), custom_call_target="tpu_custom_call" | custom-call | flops 1 | bytes 1 | tf_op jit(solution)/shard_map/mlp_out/pallas_call | solution.py:289
  196.4 6.9 %unit_grads.4 = (bf16[4,704,128]{2,1,0:T(8,128)(2,1)}, bf16[4,704,128]{2,1,0:T(8,128)(2,1)}) custom-call(s32[1]{0:T(128)} %bitcast.1.me, bf16[768,704]{1,0:T(8,128)(2,1)} %get-tuple-element.234.refs_0_, bf16[768,704]{1,0:T(8,128)(2,1)} %get-tuple-element.236.refs_1_, bf16[192,1024]{1,0:T(8,128)(2,1)} %get-tuple-element.216.sa0.refs_2_, ...), custom_call_target="tpu_custom_call" | custom-call | flops 1 | bytes 1 | tf_op jit(solution)/shard_map/unit_grads/pallas_call | solution.py:289
  208.3 6.5 %middle.1 = (f32[384,1024]{1,0:T(8,128)}, bf16[384,1024]{1,0:T(8,128)(2,1)}, bf16[384,512]{1,0:T(8,128)(2,1)}, bf16[384,256]{1,0:T(8,128)(2,1)}, bf16[384,256]{1...) custom-call(s32[1]{0:T(128)} %bitcast.me, ...), custom_call_target="tpu_custom_call" | custom-call | flops 1 | bytes 1 | tf_op jit(solution)/shard_map/middle/pallas_call | solution.py:289
  219.7 5.0 %out_grad.1 = (bf16[4,520,128]{2,1,0:T(8,128)(2,1)}, bf16[4,520,128]{2,1,0:T(8,128)(2,1)}) custom-call(s32[3]{0:T(128)} %pad_add_fusion.me, bf16[384,256]{1,0:T(8,128)(2,1)} %get-tuple-element.211.m0, bf16[384,256]{1,0:T(8,128)(2,1)} %copy-done.27, bf16[384,256]{1,0:T(8,128)(2,1)} %copy-done.29, bf16[384,256]{1,0:T(8,128)(2,1)} %copy-done.31, ...), custom_call_target="tpu_custom_call" | custom-call | flops 1 | bytes 1 | tf_op jit(solution)/shard_map/out_grad/pallas_call | solution.py:289
  224.7 6.3 %unit_grads.5 = (bf16[4,704,128]{2,1,0:T(8,128)(2,1)}, bf16[4,704,128]{2,1,0:T(8,128)(2,1)}) custom-call(s32[1]{0:T(128)} %bitcast.1.me, bf16[768,704]{1,0:T(8,128)(2,1)} %get-tuple-element.253.refs_0_, bf16[768,704]{1,0:T(8,128)(2,1)} %get-tuple-element.258.refs_1_, bf16[192,1024]{1,0:T(8,128)(2,1)} %get-tuple-element.216.sa0.refs_2_, ...), custom_call_target="tpu_custom_call" | custom-call | flops 1 | bytes 1 | tf_op jit(solution)/shard_map/unit_grads/pallas_call | solution.py:289
  231.1 2.9 collective-permute-start.51
  236.5 14.2 %attention_back.2 = (bf16[4,384,384]{2,1,0:T(8,128)(2,1)}, bf16[4,384,128]{2,1,0:T(8,128)(2,1)}) custom-call(s32[1]{0:T(128)} %bitcast.me, bf16[4,384,256]{2,1,0:T(8,128)(2,1)} %get-tuple-element.275.q, bf16[4,384,256]{2,1,0:T(8,128)(2,1)} %get-tuple-element.178.k, bf16[4,384,256]{2,1,0:T(8,128)(2,1)} %get-tuple-element.179.v, ...), custom_call_target="tpu_custom_call" | custom-call | flops 1 | bytes 1 | tf_op jit(solution)/shard_map/attention_back/pallas_call | solution.py:241
  258.6 14.6 %attention_back.3 = (bf16[4,384,384]{2,1,0:T(8,128)(2,1)}, bf16[4,384,256]{2,1,0:T(8,128)(2,1)}) custom-call(s32[1]{0:T(128)} %bitcast.me, bf16[4,384,256]{2,1,0:T(8,128)(2,1)} %get-tuple-element.275.q, bf16[4,384,256]{2,1,0:T(8,128)(2,1)} %get-tuple-element.178.k, bf16[4,384,256]{2,1,0:T(8,128)(2,1)} %get-tuple-element.179.v, ...), custom_call_target="tpu_custom_call" | custom-call | flops 1 | bytes 1 | tf_op jit(solution)/shard_map/attention_back/pallas_call | solution.py:241
  274.4 5.4 %normed_back.1 = (bf16[384,1024]{1,0:T(8,128)(2,1)}, bf16[384,1024]{1,0:T(8,128)(2,1)}, bf16[384,1024]{1,0:T(8,128)(2,1)}) custom-call(s32[1]{0:T(128)} %bitcast.me, bf16[4,384,384]{2,1,0:T(8,128)(2,1)} %get-tuple-element.264.da, bf16[4,384,384]{2,1,0:T(8,128)(2,1)} %get-tuple-element.295.db, bf16[1288,1024]{1,0:T(8,128)(2,1)} %get-tuple-element.209.w0.w), custom_call_target="tpu_custom_call" | custom-call | flops 1 | bytes 1 | tf_op jit(solution)/shard_map/normed_back/pallas_call | solution.py:289
  287.4 8.9 %qkv_grad.1 = (bf16[4,776,128]{2,1,0:T(8,128)(2,1)}, bf16[4,776,128]{2,1,0:T(8,128)(2,1)}) custom-call(s32[3]{0:T(128)} %pad_add_fusion.me, bf16[1536,1024]{1,0:T(8,128)(2,1)} %bitcast.89, bf16[1536,384]{1,0:T(8,128)(2,1)} %bitcast.75, bf16[1536,384]{1,0:T(8,128)(2,1)} %bitcast.76, bf16[1288,1024]{1,0:T(8,128)(2,1)} %get-tuple-element.209.w0.w), custom_call_target="tpu_custom_call" | custom-call | flops 1 | bytes 1 | tf_op jit(solution)/shard_map/qkv_grad/pallas_call | solution.py:289
  299.9 3.2 collective-permute-start.66
  303.0 4.2 %collective-permute-done.63.p2 = bf16[384,1024]{1,0:T(8,128)(2,1)S(1)} collective-permute-done((bf16[384,1024]{1,0:T(8,128)(2,1)S(1)}, bf16[384,1024]{1,0:T(8,128)(2,1)S(1)}, u32[]{:S(2)}, u32[]{:S(2)}) %collective-permute-start.63) | collective-permute-done | bytes 786464 | tf_op jit(solution)/shard_map/ppermute | solution.py:598
  308.6 6.1 %final.1 = f32[384,1024]{1,0:T(8,128)} custom-call(s32[1]{0:T(128)} %bitcast.me, bf16[384,1024]{1,0:T(8,128)(2,1)} %copy-done.57, bf16[384,1024]{1,0:T(8,128)(2,1)} %copy-done.58, bf16[4,384,384]{2,1,0:T(8,128)(2,1)} %get-tuple-element.264.da, bf16[4,384,384]{2,1,0:T(8,128)(2,1)} %get-tuple-element.295.db, bf16[1288,1024]{1,0:T(8,128)(2,1)} %get-tuple-element.209.w0.w, ...), custom_call_target="tpu_custom_call" | custom-call | flops 1 | bytes 1 | tf_op jit(solution)/shard_map/final/pallas_call | solution.py:289
  318.3 3.5 all-to-all-start
  327.6 5.4 %place_units.1 = (f32[128,2816]{1,0:T(8,128)}, f32[128,2816]{1,0:T(8,128)}, f32[128,2816]{1,0:T(8,128)}) custom-call(s32[1]{0:T(128)} %bitcast.me, bf16[2112,128]{1,0:T(8,128)(2,1)} %copy-done.25, bf16[2112,128]{1,0:T(8,128)(2,1)} %collective-permute-done.73.p1, bf16[2112,128]{1,0:T(8,128)(2,1)} %collective-permute-done.74.p2, ...), custom_call_target="tpu_custom_call" | custom-call | flops 1 | bytes 1 | tf_op jit(solution)/shard_map/place_units/pallas_call | solution.py:289
  344.8 3.7 %collective-permute-done.78.p2 = bf16[776,128]{1,0:T(8,128)(2,1)S(1)} collective-permute-done((bf16[776,128]{1,0:T(8,128)(2,1)S(1)}, bf16[776,128]{1,0:T(8,128)(2,1)S(1)}, u32[]{:S(2)}, u32[]{:S(2)}) %collective-permute-start.78) | collective-permute-done | bytes 198688 | tf_op jit(solution)/shard_map/ppermute | solution.py:598
  (360 shorter events, 128.7 us)
Async XLA Ops:
  3.9 43.2 %collective-permute-start.1 = (bf16[384,1536]{1,0:T(8,128)(2,1)}, bf16[384,1536]{1,0:T(8,128)(2,1)S(1)}, u32[]{:S(2)}, u32[]{:S(2)}) collective-permute-start(bf16[384,1536]{1,0:T(8,128)(2,1)} %pad_maximum_fusion), channel_id=1, source_target_pairs={{0,16},{8,24},{16,0},{24,8},{1,17},{9,25},{17,1},{25,9},{2,18},{10... | collective-permute-start | bytes 3538952 | tf_op jit(solution)/shard_map/ppermute | solution.py:598
  9.2 17.9 %collective-permute-start.3 = (bf16[1288,128]{1,0:T(8,128)(2,1)S(1)}, bf16[1288,128]{1,0:T(8,128)(2,1)S(1)}, u32[]{:S(2)}, u32[]{:S(2)}) collective-permute-start(bf16[1288,128]{1,0:T(8,128)(2,1)S(1)} %concatenate.30.refs_0_), channel_id=1, source_target_pairs={{0,2},{1,3},{2,0},{3,1},{4,6},{5,7},{6,4},{7,5},{8,10},{9,11},{10,... | collective-permute-start | bytes 989192 | tf_op jit(solution)/shard_map/ppermute | solution.py:613
  10.9 29.7 %collective-permute-start.2 = (bf16[1288,128]{1,0:T(8,128)(2,1)S(1)}, bf16[1288,128]{1,0:T(8,128)(2,1)}, u32[]{:S(2)}, u32[]{:S(2)}) collective-permute-start(bf16[1288,128]{1,0:T(8,128)(2,1)S(1)} %concatenate.30.refs_0_), channel_id=1, source_target_pairs={{0,1},{1,0},{2,3},{3,2},{4,5},{5,4},{6,7},{7,6},{8,9},{9,8},{10,11... | collective-permute-start | bytes 989192 | tf_op jit(solution)/shard_map/ppermute | solution.py:613
  12.4 25.8 %collective-permute-start.5 = (bf16[1288,128]{1,0:T(8,128)(2,1)S(1)}, bf16[1288,128]{1,0:T(8,128)(2,1)}, u32[]{:S(2)}, u32[]{:S(2)}) collective-permute-start(bf16[1288,128]{1,0:T(8,128)(2,1)S(1)} %concatenate.30.refs_0_), channel_id=1, source_target_pairs={{0,4},{1,5},{2,6},{3,7},{4,0},{5,1},{6,2},{7,3},{8,12},{9,13},{10,... | collective-permute-start | bytes 989192 | tf_op jit(solution)/shard_map/ppermute | solution.py:613
  15.0 23.7 %collective-permute-start.7 = (bf16[1288,128]{1,0:T(8,128)(2,1)S(1)}, bf16[1288,128]{1,0:T(8,128)(2,1)}, u32[]{:S(2)}, u32[]{:S(2)}) collective-permute-start(bf16[1288,128]{1,0:T(8,128)(2,1)S(1)} %concatenate.30.refs_0_), channel_id=1, source_target_pairs={{0,6},{1,7},{2,4},{3,5},{4,2},{5,3},{6,0},{7,1},{8,14},{9,15},{10,... | collective-permute-start | bytes 989192 | tf_op jit(solution)/shard_map/ppermute | solution.py:613
  48.5 17.6 %collective-permute-start = (bf16[384,1280]{1,0:T(8,128)(2,1)}, bf16[384,1280]{1,0:T(8,128)(2,1)}, u32[]{:S(2)}, u32[]{:S(2)}) collective-permute-start(bf16[384,1280]{1,0:T(8,128)(2,1)} %pad_maximum_fusion.1), channel_id=1, source_target_pairs={{0,8},{8,0},{16,24},{24,16},{1,9},{9,1},{17,25},{25,17},{2,10},{10... | collective-permute-start | bytes 2949128 | tf_op jit(solution)/shard_map/ppermute | solution.py:598
  59.6 28.6 %collective-permute-start.15 = (bf16[704,128]{1,0:T(8,128)(2,1)S(1)}, bf16[704,128]{1,0:T(8,128)(2,1)S(1)}, u32[]{:S(2)}, u32[]{:S(2)}) collective-permute-start(bf16[704,128]{1,0:T(8,128)(2,1)S(1)} %bitcast.96), channel_id=1, source_target_pairs={{0,2},{1,3},{2,0},{3,1},{4,6},{5,7},{6,4},{7,5},{8,10},{9,11},{10,... | collective-permute-start | bytes 540680 | tf_op jit(solution)/shard_map/ppermute | solution.py:613
  62.8 25.4 %collective-permute-start.16 = (bf16[704,128]{1,0:T(8,128)(2,1)S(1)}, bf16[704,128]{1,0:T(8,128)(2,1)S(1)}, u32[]{:S(2)}, u32[]{:S(2)}) collective-permute-start(bf16[704,128]{1,0:T(8,128)(2,1)S(1)} %bitcast.97), channel_id=1, source_target_pairs={{0,4},{1,5},{2,6},{3,7},{4,0},{5,1},{6,2},{7,3},{8,12},{9,13},{10,... | collective-permute-start | bytes 540680 | tf_op jit(solution)/shard_map/ppermute | solution.py:613
  62.8 25.4 %collective-permute-start.17 = (bf16[704,128]{1,0:T(8,128)(2,1)S(1)}, bf16[704,128]{1,0:T(8,128)(2,1)S(1)}, u32[]{:S(2)}, u32[]{:S(2)}) collective-permute-start(bf16[704,128]{1,0:T(8,128)(2,1)S(1)} %bitcast.98), channel_id=1, source_target_pairs={{0,6},{1,7},{2,4},{3,5},{4,2},{5,3},{6,0},{7,1},{8,14},{9,15},{10,... | collective-permute-start | bytes 540680 | tf_op jit(solution)/shard_map/ppermute | solution.py:613
  66.1 29.7 %collective-permute-start.14 = (bf16[2816,128]{1,0:T(8,128)(2,1)}, bf16[2816,128]{1,0:T(8,128)(2,1)S(1)}, u32[]{:S(2)}, u32[]{:S(2)}) collective-permute-start(bf16[2816,128]{1,0:T(8,128)(2,1)} %pad_maximum_fusion.4), channel_id=1, source_target_pairs={{0,1},{1,0},{2,3},{3,2},{4,5},{5,4},{6,7},{7,6},{8,9},{9,8},{10,11... | collective-permute-start | bytes 2162696 | tf_op jit(solution)/shard_map/ppermute | solution.py:613
  67.7 25.7 %collective-permute-start.13 = (bf16[384,1024]{1,0:T(8,128)(2,1)S(1)}, bf16[384,1024]{1,0:T(8,128)(2,1)S(1)}, u32[]{:S(2)}, u32[]{:S(2)}) collective-permute-start(bf16[384,1024]{1,0:T(8,128)(2,1)S(1)} %bitcast.80), channel_id=1, source_target_pairs={{0,16},{8,24},{16,0},{24,8},{1,17},{9,25},{17,1},{25,9},{2,18},{10... | collective-permute-start | bytes 2359304 | tf_op jit(solution)/shard_map/ppermute | solution.py:598
  89.7 17.9 %collective-permute-start.18 = (bf16[2816,128]{1,0:T(8,128)(2,1)}, bf16[2816,128]{1,0:T(8,128)(2,1)S(1)}, u32[]{:S(2)}, u32[]{:S(2)}) collective-permute-start(bf16[2816,128]{1,0:T(8,128)(2,1)} %pad_maximum_fusion.5), channel_id=1, source_target_pairs={{0,1},{1,0},{2,3},{3,2},{4,5},{5,4},{6,7},{7,6},{8,9},{9,8},{10,11... | collective-permute-start | bytes 2162696 | tf_op jit(solution)/shard_map/ppermute | solution.py:613
  97.4 34.8 %collective-permute-start.31 = (bf16[384,1024]{1,0:T(8,128)(2,1)S(1)}, bf16[384,1024]{1,0:T(8,128)(2,1)S(1)}, u32[]{:S(2)}, u32[]{:S(2)}) collective-permute-start(bf16[384,1024]{1,0:T(8,128)(2,1)S(1)} %bitcast.81), channel_id=1, source_target_pairs={{0,8},{8,0},{16,24},{24,16},{1,9},{9,1},{17,25},{25,17},{2,10},{10... | collective-permute-start | bytes 2359304 | tf_op jit(solution)/shard_map/ppermute | solution.py:598
  109.6 23.1 %collective-permute-start.32 = (bf16[2816,128]{1,0:T(8,128)(2,1)S(1)}, bf16[2816,128]{1,0:T(8,128)(2,1)S(1)}, u32[]{:S(2)}, u32[]{:S(2)}) collective-permute-start(bf16[2816,128]{1,0:T(8,128)(2,1)S(1)} %pad_maximum_fusion.6), channel_id=1, source_target_pairs={{0,1},{1,0},{2,3},{3,2},{4,5},{5,4},{6,7},{7,6},{8,9},{9,8},{10,11... | collective-permute-start | bytes 2162696 | tf_op jit(solution)/shard_map/ppermute | solution.py:613
  132.2 18.3 %collective-permute-start.34 = (bf16[192,1024]{1,0:T(8,128)(2,1)}, bf16[192,1024]{1,0:T(8,128)(2,1)S(1)}, u32[]{:S(2)}, u32[]{:S(2)}) collective-permute-start(bf16[192,1024]{1,0:T(8,128)(2,1)} %get-tuple-element.217.sa1.refs_3_), channel_id=1, source_target_pairs={{0,16},{8,24},{16,0},{24,8},{1,17},{9,25},{17,1},{25,9},{2,18},{10... | collective-permute-start | bytes 1179656 | tf_op jit(solution)/shard_map/ppermute | solution.py:598
  132.7 18.3 %collective-permute-start.37 = (bf16[384,1024]{1,0:T(8,128)(2,1)S(1)}, bf16[384,1024]{1,0:T(8,128)(2,1)S(1)}, u32[]{:S(2)}, u32[]{:S(2)}) collective-permute-start(bf16[384,1024]{1,0:T(8,128)(2,1)S(1)} %collective-permute-done.13.ga.refs_4_), channel_id=1, source_target_pairs={{0,8},{8,0},{16,24},{24,16},{1,9},{9,1},{17,25},{25,17},{2,10},{10... | collective-permute-start | bytes 2359304 | tf_op jit(solution)/shard_map/ppermute | solution.py:598
  179.3 24.0 %collective-permute-start.43 = (bf16[384,1024]{1,0:T(8,128)(2,1)S(1)}, bf16[384,1024]{1,0:T(8,128)(2,1)S(1)}, u32[]{:S(2)}, u32[]{:S(2)}) collective-permute-start(bf16[384,1024]{1,0:T(8,128)(2,1)S(1)} %add_convert_fusion.4), channel_id=1, source_target_pairs={{0,16},{8,24},{16,0},{24,8},{1,17},{9,25},{17,1},{25,9},{2,18},{10... | collective-permute-start | bytes 2359304 | tf_op jit(solution)/shard_map/ppermute | solution.py:598
  188.1 18.4 %collective-permute-start.44 = (bf16[4,704,128]{2,1,0:T(8,128)(2,1)}, bf16[4,704,128]{2,1,0:T(8,128)(2,1)S(1)}, u32[]{:S(2)}, u32[]{:S(2)}) collective-permute-start(bf16[4,704,128]{2,1,0:T(8,128)(2,1)} %get-tuple-element.244), channel_id=1, source_target_pairs={{0,1},{1,0},{2,3},{3,2},{4,5},{5,4},{6,7},{7,6},{8,9},{9,8},{10,11... | collective-permute-start | bytes 2162696 | tf_op jit(solution)/shard_map/ppermute | solution.py:613
  206.7 45.4 %collective-permute-start.50 = (bf16[4,704,128]{2,1,0:T(8,128)(2,1)}, bf16[4,704,128]{2,1,0:T(8,128)(2,1)}, u32[]{:S(2)}, u32[]{:S(2)}) collective-permute-start(bf16[4,704,128]{2,1,0:T(8,128)(2,1)} %get-tuple-element.268), channel_id=1, source_target_pairs={{0,1},{1,0},{2,3},{3,2},{4,5},{5,4},{6,7},{7,6},{8,9},{9,8},{10,11... | collective-permute-start | bytes 2162696 | tf_op jit(solution)/shard_map/ppermute | solution.py:613
  231.1 22.9 %collective-permute-start.51 = (bf16[704,128]{1,0:T(8,128)(2,1)S(1)}, bf16[704,128]{1,0:T(8,128)(2,1)S(1)}, u32[]{:S(2)}, u32[]{:S(2)}) collective-permute-start(bf16[704,128]{1,0:T(8,128)(2,1)S(1)} %get-tuple-element.356), channel_id=1, source_target_pairs={{0,2},{1,3},{2,0},{3,1},{4,6},{5,7},{6,4},{7,5},{8,10},{9,11},{10,... | collective-permute-start | bytes 540680 | tf_op jit(solution)/shard_map/ppermute | solution.py:613
  234.0 20.0 %collective-permute-start.52 = (bf16[704,128]{1,0:T(8,128)(2,1)S(1)}, bf16[704,128]{1,0:T(8,128)(2,1)S(1)}, u32[]{:S(2)}, u32[]{:S(2)}) collective-permute-start(bf16[704,128]{1,0:T(8,128)(2,1)S(1)} %get-tuple-element.355), channel_id=1, source_target_pairs={{0,4},{1,5},{2,6},{3,7},{4,0},{5,1},{6,2},{7,3},{8,12},{9,13},{10,... | collective-permute-start | bytes 540680 | tf_op jit(solution)/shard_map/ppermute | solution.py:613
  234.0 20.0 %collective-permute-start.53 = (bf16[704,128]{1,0:T(8,128)(2,1)S(1)}, bf16[704,128]{1,0:T(8,128)(2,1)S(1)}, u32[]{:S(2)}, u32[]{:S(2)}) collective-permute-start(bf16[704,128]{1,0:T(8,128)(2,1)S(1)} %get-tuple-element.354), channel_id=1, source_target_pairs={{0,6},{1,7},{2,4},{3,5},{4,2},{5,3},{6,0},{7,1},{8,14},{9,15},{10,... | collective-permute-start | bytes 540680 | tf_op jit(solution)/shard_map/ppermute | solution.py:613
  250.7 22.5 %collective-permute-start.49 = (bf16[384,1024]{1,0:T(8,128)(2,1)S(1)}, bf16[384,1024]{1,0:T(8,128)(2,1)S(1)}, u32[]{:S(2)}, u32[]{:S(2)}) collective-permute-start(bf16[384,1024]{1,0:T(8,128)(2,1)S(1)} %add_convert_fusion.3), channel_id=1, source_target_pairs={{0,16},{8,24},{16,0},{24,8},{1,17},{9,25},{17,1},{25,9},{2,18},{10... | collective-permute-start | bytes 2359304 | tf_op jit(solution)/shard_map/ppermute | solution.py:598
  253.4 19.9 %collective-permute-start.54 = (bf16[4,704,128]{2,1,0:T(8,128)(2,1)S(1)}, bf16[4,704,128]{2,1,0:T(8,128)(2,1)S(1)}, u32[]{:S(2)}, u32[]{:S(2)}) collective-permute-start(bf16[4,704,128]{2,1,0:T(8,128)(2,1)S(1)} %copy-done.74), channel_id=1, source_target_pairs={{0,1},{1,0},{2,3},{3,2},{4,5},{5,4},{6,7},{7,6},{8,9},{9,8},{10,11... | collective-permute-start | bytes 2162696 | tf_op jit(solution)/shard_map/ppermute | solution.py:613
  254.2 19.1 %collective-permute-start.55 = (bf16[704,128]{1,0:T(8,128)(2,1)S(1)}, bf16[704,128]{1,0:T(8,128)(2,1)S(1)}, u32[]{:S(2)}, u32[]{:S(2)}) collective-permute-start(bf16[704,128]{1,0:T(8,128)(2,1)S(1)} %get-tuple-element.352), channel_id=1, source_target_pairs={{0,2},{1,3},{2,0},{3,1},{4,6},{5,7},{6,4},{7,5},{8,10},{9,11},{10,... | collective-permute-start | bytes 540680 | tf_op jit(solution)/shard_map/ppermute | solution.py:613
  255.3 18.0 %collective-permute-start.56 = (bf16[704,128]{1,0:T(8,128)(2,1)S(1)}, bf16[704,128]{1,0:T(8,128)(2,1)S(1)}, u32[]{:S(2)}, u32[]{:S(2)}) collective-permute-start(bf16[704,128]{1,0:T(8,128)(2,1)S(1)} %get-tuple-element.351), channel_id=1, source_target_pairs={{0,4},{1,5},{2,6},{3,7},{4,0},{5,1},{6,2},{7,3},{8,12},{9,13},{10,... | collective-permute-start | bytes 540680 | tf_op jit(solution)/shard_map/ppermute | solution.py:613
  280.3 17.9 %collective-permute-start.64 = (bf16[4,520,128]{2,1,0:T(8,128)(2,1)}, bf16[4,520,128]{2,1,0:T(8,128)(2,1)S(1)}, u32[]{:S(2)}, u32[]{:S(2)}) collective-permute-start(bf16[4,520,128]{2,1,0:T(8,128)(2,1)} %get-tuple-element.308), channel_id=1, source_target_pairs={{0,1},{1,0},{2,3},{3,2},{4,5},{5,4},{6,7},{7,6},{8,9},{9,8},{10,11... | collective-permute-start | bytes 1597448 | tf_op jit(solution)/shard_map/ppermute | solution.py:613
  286.7 20.5 %collective-permute-start.63 = (bf16[384,1024]{1,0:T(8,128)(2,1)S(1)}, bf16[384,1024]{1,0:T(8,128)(2,1)S(1)}, u32[]{:S(2)}, u32[]{:S(2)}) collective-permute-start(bf16[384,1024]{1,0:T(8,128)(2,1)S(1)} %add_convert_fusion.1), channel_id=1, source_target_pairs={{0,16},{8,24},{16,0},{24,8},{1,17},{9,25},{17,1},{25,9},{2,18},{10... | collective-permute-start | bytes 2359304 | tf_op jit(solution)/shard_map/ppermute | solution.py:598
  298.3 19.0 %collective-permute-start.65 = (bf16[4,776,128]{2,1,0:T(8,128)(2,1)S(1)}, bf16[4,776,128]{2,1,0:T(8,128)(2,1)S(1)}, u32[]{:S(2)}, u32[]{:S(2)}) collective-permute-start(bf16[4,776,128]{2,1,0:T(8,128)(2,1)S(1)} %copy-done.72), channel_id=1, source_target_pairs={{0,1},{1,0},{2,3},{3,2},{4,5},{5,4},{6,7},{7,6},{8,9},{9,8},{10,11... | collective-permute-start | bytes 2383880 | tf_op jit(solution)/shard_map/ppermute | solution.py:613
  299.1 17.6 %collective-permute-start.74 = (bf16[2112,128]{1,0:T(8,128)(2,1)S(1)}, bf16[2112,128]{1,0:T(8,128)(2,1)}, u32[]{:S(2)}, u32[]{:S(2)}) collective-permute-start(bf16[2112,128]{1,0:T(8,128)(2,1)S(1)} %pad_maximum_fusion.7.p0), channel_id=1, source_target_pairs={{0,16},{8,24},{16,0},{24,8},{1,17},{9,25},{17,1},{25,9},{2,18},{10... | collective-permute-start | bytes 1622024 | tf_op jit(solution)/shard_map/ppermute | solution.py:598
  322.6 18.1 %collective-permute-start.69 = (bf16[776,128]{1,0:T(8,128)(2,1)}, bf16[776,128]{1,0:T(8,128)(2,1)S(1)}, u32[]{:S(2)}, u32[]{:S(2)}) collective-permute-start(bf16[776,128]{1,0:T(8,128)(2,1)} %get-tuple-element.340), channel_id=1, source_target_pairs={{0,2},{1,3},{2,0},{3,1},{4,6},{5,7},{6,4},{7,5},{8,10},{9,11},{10,... | collective-permute-start | bytes 595976 | tf_op jit(solution)/shard_map/ppermute | solution.py:613
  325.2 17.5 %collective-permute-start.70 = (bf16[776,128]{1,0:T(8,128)(2,1)}, bf16[776,128]{1,0:T(8,128)(2,1)S(1)}, u32[]{:S(2)}, u32[]{:S(2)}) collective-permute-start(bf16[776,128]{1,0:T(8,128)(2,1)} %get-tuple-element.339), channel_id=1, source_target_pairs={{0,4},{1,5},{2,6},{3,7},{4,0},{5,1},{6,2},{7,3},{8,12},{9,13},{10,... | collective-permute-start | bytes 595976 | tf_op jit(solution)/shard_map/ppermute | solution.py:613
  (124 other events, 1104.4 us)

commit v2 on v1

--- a/solution.py
+++ b/solution.py
@@ -55,20 +55,21 @@
 
 def qkv_kernel(count, me, t0, f0, p1, p2, p3, *refs):
     pieces, rest = refs[:count], refs[count:]
-    cosine, sine, q, k, v, n, w, tv, fv, sems = rest
+    cosine, sine, q, k, v, n, w, wo, tv, fv, sems = rest
     width = q.shape[-1]
     d = tv.shape[-1]
     share = d // count
-    first = []
+    first, last = [], []
     for i, piece in enumerate(pieces):
         at = pl.ds(pl.multiple_of((me[0] ^ i) * share, share), share)
-        first.append(pltpu.make_async_copy(piece, w.at[:, at], sems.at[8 + i]))
+        first.append(pltpu.make_async_copy(piece.at[: w.shape[0]], w.at[:, at], sems.at[8 + i]))
+        last.append(pltpu.make_async_copy(piece.at[w.shape[0] :], wo.at[:, at], sems.at[16 + i]))
     loads = [(t0, f0)] + [(p.at[:, :d], p.at[:, d : d + width]) for p in (p1, p2, p3)]
     copies = []
     for i, (t, f) in enumerate(loads):
         copies.append(pltpu.make_async_copy(t, tv.at[i], sems.at[2 * i]))
         copies.append(pltpu.make_async_copy(f, fv.at[i], sems.at[2 * i + 1]))
-    for copy in copies[:2] + first + copies[2:]:
+    for copy in copies[:2] + first + copies[2:] + last:
         copy.start()
     for i in range(4):
         copies[2 * i].wait()
@@ -85,13 +86,16 @@
         k[i] = turn(u[:, width : 2 * width], c, s).astype(BF16)
         copies[2 * i + 1].wait()
         v[i] = (0.5 * u[:, 2 * width :] + 0.5 * fv[i].astype(F32)).astype(BF16)
+    for copy in last:
+        copy.wait()
 
 
 def qkv(where, t, f, packed, pieces, cosine, sine):
     rows, d = t.shape
     width = f.shape[1]
     full = lambda *shape: pl.BlockSpec(shape, lambda i, me: (0,) * len(shape))
-    shapes = [(4, rows, width)] * 3 + [(4, rows, d), (pieces[0].shape[0], d)]
+    main = 3 * width + 8
+    shapes = [(4, rows, width)] * 3 + [(4, rows, d), (main, d), (pieces[0].shape[0] - main, d)]
     return pl.pallas_call(
         functools.partial(qkv_kernel, len(pieces)),
         grid_spec=pltpu.PrefetchScalarGridSpec(
@@ -102,7 +106,7 @@
             scratch_shapes=[
                 pltpu.VMEM((4, rows, d), BF16),
                 pltpu.VMEM((4, rows, width), BF16),
-                pltpu.SemaphoreType.DMA((8 + len(pieces),)),
+                pltpu.SemaphoreType.DMA((24,)),
             ],
         ),
         out_shape=[jax.ShapeDtypeStruct(s, BF16) for s in shapes],
@@ -674,7 +678,7 @@
     if ring:
         pieces = [own_qkv, first_y]
         for i in range(3):
-            one = after(first[i], cosine, sine) if i == 0 else first[i]
+            one = after(first[i], cosine, sine, *own_units) if i == 0 else first[i]
             pieces += [one, fsdp_permute(one, 1)]
     else:
         pieces = [lax.all_gather(own_qkv, "fsdp", axis=1, tiled=True)]
@@ -696,9 +700,9 @@
         up_w = pair_send(own_units[1], gate_w[1])
     g2 = seq_permute(after(g0, packed2, *pieces[1::2]), 2)
 
-    q, k, v, normed, w_qkv = qkv(where, t0, f[0], (packed1, packed2, packed3), pieces, cosine, sine)
+    q, k, v, normed, w_qkv, w_out = qkv(where, t0, f[0], (packed1, packed2, packed3), pieces, cosine, sine)
     gains = w_qkv[3 * width : 3 * width + 8]
-    w_out_sent = w_qkv[3 * width + 8 :]
+    w_out_sent = w_out
     *m, lse_a = attention(0, me, q, k, v)
     g2 = after(g2, m[0])
     q = after(q, g2)
@@ -730,7 +734,7 @@
         "out",
         [((rows, d), F32)] + [((rows // 2, d), BF16)] * 2,
         me,
-        [*m, w_qkv, *w_out_other, t0, gains],
+        [*m, w_out, *w_out_other, t0, gains],
         cost(2 * rows * d * d, 8e6),
     )
     s1 = [seq_permute(one, 1) for one in s0]
@@ -771,7 +775,7 @@
         + [((rows, width), BF16)] * 4
         + [((8, d), F32)],
         me,
-        [*p, middle, g0, gains, w_qkv, *w_out_other],
+        [*p, middle, g0, gains, w_out, *w_out_other],
         cost(2 * rows * d * d, 12e6),
     )
     b = exchange_four([b0, b1, b2, b3])
@@ -881,19 +885,20 @@
         whole = (keep + seq_permute(send, 1).astype(F32)).astype(BF16)
         out_share = scatter_whole(jnp.transpose(whole, (1, 0, 2)))
         units_sent = jnp.concatenate([gate_share, up_share, down_share], axis=0)
-    v_all = lax.all_to_all(after(v_b, tokens_grad), "seq", split_axis=0, concat_axis=0)
+    if not ring:
+        units_far = seq_permute(units_sent, 2)
+    units_all = [units_sent, seq_permute(units_sent, 1), units_far, seq_permute(units_far, 1)]
+    v_all = lax.all_to_all(after(v_b, tokens_grad, *units_all), "seq", split_axis=0, concat_axis=0)
     output = add(middle, o[0], o1, o2)[None]
     (values_grad,) = vmem_call(
         place_values_kernel, "place_values", [((rows, d), F32)], me, [v_all], cost(0, 3e6)
     )
-    if not ring:
-        units_far = seq_permute(units_sent, 2)
     gate_grad, up_grad, down_grad = vmem_call(
         place_units_kernel,
         "place_units",
         [((share, 4 * units), F32)] * 3,
         me,
-        [units_sent, seq_permute(units_sent, 1), units_far, seq_permute(units_far, 1)],
+        units_all,
         cost(0, 3e6),
         [pltpu.VMEM((4, 3 * units, share), F32)],
     )
@@ -911,8 +916,8 @@
         cost(0, 1e6),
     )
     if ring:
-        qkv_share = add(*all_after(qkv_sent, out_grad, values_grad, output, gate_grad))
-    qkv_far = seq_permute(qkv_share, 2)
+        qkv_share = add(*all_after(qkv_sent, out_grad, gate_grad))
+    qkv_far = after(seq_permute(qkv_share, 2), values_grad, output)
     qkv_all = [qkv_share, seq_permute(qkv_share, 1), qkv_far, seq_permute(qkv_far, 1)]
     query_grad, key_grad, value_grad, gain_grad = vmem_call(
         place_qkv_kernel,

time: 361 us -> 356 us (0.986)
  local copies, waits for them, and re-layouts: 27.8 us -> 22.5 us
    concatenate x1, local copies, waits for them, and re-layouts: 0.11 us -> 3.86 us  [per_device(): own_qkv = jnp.concatenate(own_qkv, axis=0)]
    ppermute x39, waiting for transfers between devices: 25.6 us -> 29.2 us  [fsdp_permute(): return lax.ppermute(value, 'fsdp', [(i, i ^ flip) for i in range(n)])]
    unnamed x157 -> x163, local copies, waits for them, and re-layouts: 10.8 us -> 10.9 us
  transfers between devices with their start and end apart: 81 -> 81, of which waited for: 20 -> 21; matrix products, arithmetic and copies ran while one was open for 9% -> 7% of each run, Pallas kernels for 39% -> 39%
where the time goes in v2:
time: 356 us; the launch traced here: 350 us
  Pallas kernels  166 us (47%)
  starting transfers between devices  83.1 us (23%)
  waiting for transfers between devices  57.2 us (16%)
  local copies, waits for them, and re-layouts  22.5 us (6%)
  other arithmetic  20 us (6%)
    pallas_call x14, Pallas kernels, vmem_call(): pl.pallas_call(kernel, grid_spec=pltpu.PrefetchScalarGridSpec(num_scalar_...  73.6 us
    ppermute x39, starting transfers between devices, fsdp_permute(): return lax.ppermute(value, 'fsdp', [(i, i ^ flip) for i in range(n)])  59.2 us
    pallas_call x2, Pallas kernels, any_call(): pl.pallas_call(kernel, grid_spec=pltpu.PrefetchScalarGridSpec(num_scalar_...  34 us
    ppermute x39, waiting for transfers between devices, fsdp_permute(): return lax.ppermute(value, 'fsdp', [(i, i ^ flip) for i in range(n)])  29.2 us
    pallas_call x2, Pallas kernels, attention_back(): pl.pallas_call(attn_back_kernel, grid_spec=pltpu.PrefetchScalarGridSpec(n...  28.9 us
    ppermute x41, waiting for transfers between devices, seq_permute(): return lax.ppermute(value, 'seq', [(i, i ^ flip) for i in range(GROUPS)])  24.9 us
    ppermute x41, starting transfers between devices, seq_permute(): return lax.ppermute(value, 'seq', [(i, i ^ flip) for i in range(GROUPS)])  20.3 us
    pallas_call x2, Pallas kernels, attention(): pl.pallas_call(attn_kernel, grid_spec=pltpu.PrefetchScalarGridSpec(num_sc...  17.8 us
  transfers between devices with their start and end apart: 81, of which 21 were waited for; matrix products, arithmetic and copies ran while one was open for 7% of the time, Pallas kernels for 39%

profile of v2, /device:TPU:0, one launch (start us, length us, event | category | flops | bytes accessed | tf_op | source)
XLA Modules:
  0.0 350.4 jit_solution(6523824995398538756)
XLA Ops:
  4.0 3.9 %concatenate.30.refs_0_ = bf16[1288,128]{1,0:T(8,128)(2,1)} concatenate(bf16[256,128]{1,0:T(8,128)(2,1)S(1)} %bitcast.107, bf16[256,128]{1,0:T(8,128)(2,1)S(1)} %bitcast.105, bf16[256,128]{1,0:T(8,128)(2,1)S(1)} %bitcast.106, bf16[1,128]{1,0:T(2,128)(2,1)} %bitcast.108, bf16[1,128]{1,0:T(2,128)(2,1)} %bitcast.109, bf16[6,128]{1,0:T(8,128)(2,1)S(1)} %broadcast_in_dim.26, ...), dimensions={0} | concatenate | bytes 659456 | tf_op jit(solution)/shard_map/concatenate | solution.py:665
  21.6 4.3 %fusion = (f32[4,384,128]{2,1,0:T(8,128)}, f32[4,384,128]{2,1,0:T(8,128)}) fusion(f32[128]{0:T(128)S(1)} %mul.78, f32[128]{0:T(128)S(1)} %mul.75, f32[4,384]{1,0:T(4,128)S(1)} %add_convert_fusion.15), kind=kLoop, calls=%fused_computation.14 | loop fusion | flops 393216 | bytes 1580032 | tf_op jit(solution)/shard_map/mul | solution.py:672
  26.6 11.8 %collective-permute-done.5.refs_4_ = bf16[1288,128]{1,0:T(8,128)(2,1)} collective-permute-done((bf16[1288,128]{1,0:T(8,128)(2,1)}, bf16[1288,128]{1,0:T(8,128)(2,1)}, u32[]{:S(2)}, u32[]{:S(2)}) %collective-permute-start.5) | collective-permute-done | bytes 329760 | tf_op jit(solution)/shard_map/ppermute | solution.py:617
  42.4 5.5 %collective-permute-start.10 = (bf16[704,128]{1,0:T(8,128)(2,1)S(1)}, bf16[704,128]{1,0:T(8,128)(2,1)S(1)}, u32[]{:S(2)}, u32[]{:S(2)}) collective-permute-start(bf16[704,128]{1,0:T(8,128)(2,1)S(1)} %bitcast.96), channel_id=1, source_target_pairs={{0,4},{1,5},{2,6},{3,7},{4,0},{5,1},{6,2},{7,3},{8,12},{9,13},{10,... | collective-permute-start | bytes 540680 | tf_op jit(solution)/shard_map/ppermute | solution.py:617
  50.6 9.1 %collective-permute-done.10.refs_2_ = bf16[704,128]{1,0:T(8,128)(2,1)S(1)} collective-permute-done((bf16[704,128]{1,0:T(8,128)(2,1)S(1)}, bf16[704,128]{1,0:T(8,128)(2,1)S(1)}, u32[]{:S(2)}, u32[]{:S(2)}) %collective-permute-start.10) | collective-permute-done | bytes 180256 | tf_op jit(solution)/shard_map/ppermute | solution.py:617
  59.9 3.1 collective-permute-start.15
  68.6 11.3 %qkv.1 = (bf16[4,384,256]{2,1,0:T(8,128)(2,1)}, bf16[4,384,256]{2,1,0:T(8,128)(2,1)}, bf16[4,384,256]{2,1,0:T(8,128)(2,1)}, bf16[4,384,1024]{2,1,0:T(8,128)(2,1)...) custom-call(s32[1]{0:T(128)} %bitcast.1.me, bf16[384,1024]{1,0:T(8,128)(2,1)} %bitcast.70, ...), custom_call_target="tpu_custom_call" | custom-call | flops 1 | bytes 1 | tf_op jit(solution)/shard_map/qkv/pallas_call | solution.py:99
  80.0 8.4 %attention.2 = (bf16[384,128]{1,0:T(8,128)(2,1)}, bf16[384,128]{1,0:T(8,128)(2,1)}, bf16[384,128]{1,0:T(8,128)(2,1)}, bf16[384,128]{1,0:T(8,128)(2,1)}, f32[2,4,8,384]{3,2,1,0:T(8,128)}) custom-call(s32[1]{0:T(128)} %bitcast.me, bf16[4,384,256]{2,1,0:T(8,128)(2,1)} %get-tuple-element.278.q, bf16[4,384,256]{2,1,0:T(8,128)(2,1)} %get-tuple-element.180.k, ...), custom_call_target="tpu_custom_call" | custom-call | flops 1 | bytes 1 | tf_op jit(solution)/shard_map/attention/pallas_call | solution.py:167
  93.6 9.3 %attention.3 = (bf16[384,256]{1,0:T(8,128)(2,1)}, bf16[384,256]{1,0:T(8,128)(2,1)}, bf16[384,256]{1,0:T(8,128)(2,1)}, bf16[384,256]{1,0:T(8,128)(2,1)}, f32[2,4,8,384]{3,2,1,0:T(8,128)}) custom-call(s32[1]{0:T(128)} %bitcast.me, bf16[4,384,256]{2,1,0:T(8,128)(2,1)} %get-tuple-element.278.q, bf16[4,384,256]{2,1,0:T(8,128)(2,1)} %get-tuple-element.180.k, ...), custom_call_target="tpu_custom_call" | custom-call | flops 1 | bytes 1 | tf_op jit(solution)/shard_map/attention/pallas_call | solution.py:167
  109.6 4.2 %collective-permute-done.20.m2 = bf16[384,256]{1,0:T(8,128)(2,1)S(1)} collective-permute-done((bf16[384,256]{1,0:T(8,128)(2,1)}, bf16[384,256]{1,0:T(8,128)(2,1)S(1)}, u32[]{:S(2)}, u32[]{:S(2)}) %collective-permute-start.20) | collective-permute-done | bytes 196640 | tf_op jit(solution)/shard_map/ppermute | solution.py:602
  113.8 3.4 collective-permute-done.21.m3
  122.3 5.5 %out.1 = (f32[384,1024]{1,0:T(8,128)}, bf16[192,1024]{1,0:T(8,128)(2,1)}, bf16[192,1024]{1,0:T(8,128)(2,1)}) custom-call(s32[1]{0:T(128)} %bitcast.me, bf16[384,256]{1,0:T(8,128)(2,1)} %get-tuple-element.213.m0, bf16[384,256]{1,0:T(8,128)(2,1)} %copy-done.28, bf16[384,256]{1,0:T(8,128)(2,1)} %copy-done.30, bf16[384,256]{1,0:T(8,128)(2,1)} %copy-done.32, ...), custom_call_target="tpu_custom_call" | custom-call | flops 1 | bytes 1 | tf_op jit(solution)/shard_map/out/pallas_call | solution.py:293
  132.1 12.6 %mlp.2 = (bf16[768,704]{1,0:T(8,128)(2,1)}, bf16[768,704]{1,0:T(8,128)(2,1)}, bf16[768,704]{1,0:T(8,128)(2,1)}, bf16[384,1024]{1,0:T(8,128)(2,1)}, bf16[384,1024]{1,0:T(8,128)(2,1)}) custom-call(s32[1]{0:T(128)} %bitcast.1.me, bf16[192,1024]{1,0:T(8,128)(2,1)} %get-tuple-element.219.sa0.refs_2_, bf16[192,1024]{1,0:T(8,128)(2,1)} %get-tuple-element.220.sa1.refs_3_, ...), custom_call_target="tpu_custom_call" | custom-call | flops 1 | bytes 1 | tf_op jit(solution)/shard_map/mlp/pallas_call | solution.py:377
  144.8 3.3 collective-permute-done.34.sa1.refs_7_
  151.3 21.4 %mlp.3 = (bf16[768,704]{1,0:T(8,128)(2,1)}, bf16[768,704]{1,0:T(8,128)(2,1)}, bf16[768,704]{1,0:T(8,128)(2,1)}, bf16[384,1024]{1,0:T(8,128)(2,1)}, bf16[384,1024]{1,0:T(8,128)(2,1)}) custom-call(s32[1]{0:T(128)} %bitcast.1.me, bf16[192,1024]{1,0:T(8,128)(2,1)} %copy-done.11, bf16[192,1024]{1,0:T(8,128)(2,1)} %copy-done.12, bf16[192,1024]{1,0:T(8,128)(2,1)} %copy-done.13, ...), custom_call_target="tpu_custom_call" | custom-call | flops 1 | bytes 1 | tf_op jit(solution)/shard_map/mlp/pallas_call | solution.py:377
  179.2 6.4 %unit_grads.3 = (bf16[4,704,128]{2,1,0:T(8,128)(2,1)}, bf16[4,704,128]{2,1,0:T(8,128)(2,1)}) custom-call(s32[1]{0:T(128)} %bitcast.1.me, bf16[768,704]{1,0:T(8,128)(2,1)} %get-tuple-element.222.refs_0_.hn, bf16[768,704]{1,0:T(8,128)(2,1)} %get-tuple-element.233.refs_1_.hf, bf16[384,1024]{1,0:T(8,128)(2,1)} %bitcast.78, bf16[384,1024]{1,0:T(8,128)(2,1)} %copy-done.17, ...), custom_call_target="tpu_custom_call" | custom-call | flops 1 | bytes 1 | tf_op jit(solution)/shard_map/unit_grads/pallas_call | solution.py:293
  186.6 6.1 %mlp_out.1 = (bf16[384,1024]{1,0:T(8,128)(2,1)}, bf16[384,1024]{1,0:T(8,128)(2,1)}, bf16[384,1024]{1,0:T(8,128)(2,1)}, bf16[384,1024]{1,0:T(8,128)(2,1)}) custom-call(s32[1]{0:T(128)} %bitcast.1.me, bf16[768,704]{1,0:T(8,128)(2,1)} %get-tuple-element.222.refs_0_.hn, bf16[768,704]{1,0:T(8,128)(2,1)} %get-tuple-element.233.refs_1_.hf, ...), custom_call_target="tpu_custom_call" | custom-call | flops 1 | bytes 1 | tf_op jit(solution)/shard_map/mlp_out/pallas_call | solution.py:293
  193.4 6.9 %unit_grads.4 = (bf16[4,704,128]{2,1,0:T(8,128)(2,1)}, bf16[4,704,128]{2,1,0:T(8,128)(2,1)}) custom-call(s32[1]{0:T(128)} %bitcast.1.me, bf16[768,704]{1,0:T(8,128)(2,1)} %get-tuple-element.237.refs_0_, bf16[768,704]{1,0:T(8,128)(2,1)} %get-tuple-element.239.refs_1_, bf16[192,1024]{1,0:T(8,128)(2,1)} %get-tuple-element.219.sa0.refs_2_, ...), custom_call_target="tpu_custom_call" | custom-call | flops 1 | bytes 1 | tf_op jit(solution)/shard_map/unit_grads/pallas_call | solution.py:293
  206.1 5.9 %middle.1 = (f32[384,1024]{1,0:T(8,128)}, bf16[384,1024]{1,0:T(8,128)(2,1)}, bf16[384,512]{1,0:T(8,128)(2,1)}, bf16[384,256]{1,0:T(8,128)(2,1)}, bf16[384,256]{1...) custom-call(s32[1]{0:T(128)} %bitcast.me, ...), custom_call_target="tpu_custom_call" | custom-call | flops 1 | bytes 1 | tf_op jit(solution)/shard_map/middle/pallas_call | solution.py:293
  216.7 5.0 %out_grad.1 = (bf16[4,520,128]{2,1,0:T(8,128)(2,1)}, bf16[4,520,128]{2,1,0:T(8,128)(2,1)}) custom-call(s32[3]{0:T(128)} %pad_add_fusion.me, bf16[384,256]{1,0:T(8,128)(2,1)} %get-tuple-element.213.m0, bf16[384,256]{1,0:T(8,128)(2,1)} %copy-done.28, bf16[384,256]{1,0:T(8,128)(2,1)} %copy-done.30, bf16[384,256]{1,0:T(8,128)(2,1)} %copy-done.32, ...), custom_call_target="tpu_custom_call" | custom-call | flops 1 | bytes 1 | tf_op jit(solution)/shard_map/out_grad/pallas_call | solution.py:293
  221.6 6.3 %unit_grads.5 = (bf16[4,704,128]{2,1,0:T(8,128)(2,1)}, bf16[4,704,128]{2,1,0:T(8,128)(2,1)}) custom-call(s32[1]{0:T(128)} %bitcast.1.me, bf16[768,704]{1,0:T(8,128)(2,1)} %get-tuple-element.256.refs_0_, bf16[768,704]{1,0:T(8,128)(2,1)} %get-tuple-element.261.refs_1_, bf16[192,1024]{1,0:T(8,128)(2,1)} %get-tuple-element.219.sa0.refs_2_, ...), custom_call_target="tpu_custom_call" | custom-call | flops 1 | bytes 1 | tf_op jit(solution)/shard_map/unit_grads/pallas_call | solution.py:293
  233.5 14.2 %attention_back.2 = (bf16[4,384,384]{2,1,0:T(8,128)(2,1)}, bf16[4,384,128]{2,1,0:T(8,128)(2,1)}) custom-call(s32[1]{0:T(128)} %bitcast.me, bf16[4,384,256]{2,1,0:T(8,128)(2,1)} %get-tuple-element.278.q, bf16[4,384,256]{2,1,0:T(8,128)(2,1)} %get-tuple-element.180.k, bf16[4,384,256]{2,1,0:T(8,128)(2,1)} %get-tuple-element.181.v, ...), custom_call_target="tpu_custom_call" | custom-call | flops 1 | bytes 1 | tf_op jit(solution)/shard_map/attention_back/pallas_call | solution.py:245
  255.2 14.6 %attention_back.3 = (bf16[4,384,384]{2,1,0:T(8,128)(2,1)}, bf16[4,384,256]{2,1,0:T(8,128)(2,1)}) custom-call(s32[1]{0:T(128)} %bitcast.me, bf16[4,384,256]{2,1,0:T(8,128)(2,1)} %get-tuple-element.278.q, bf16[4,384,256]{2,1,0:T(8,128)(2,1)} %get-tuple-element.180.k, bf16[4,384,256]{2,1,0:T(8,128)(2,1)} %get-tuple-element.181.v, ...), custom_call_target="tpu_custom_call" | custom-call | flops 1 | bytes 1 | tf_op jit(solution)/shard_map/attention_back/pallas_call | solution.py:245
  270.2 5.1 %normed_back.1 = (bf16[384,1024]{1,0:T(8,128)(2,1)}, bf16[384,1024]{1,0:T(8,128)(2,1)}, bf16[384,1024]{1,0:T(8,128)(2,1)}) custom-call(s32[1]{0:T(128)} %bitcast.me, bf16[4,384,384]{2,1,0:T(8,128)(2,1)} %get-tuple-element.267.da, bf16[4,384,384]{2,1,0:T(8,128)(2,1)} %get-tuple-element.298.db, bf16[776,1024]{1,0:T(8,128)(2,1)} %get-tuple-element.217.w), custom_call_target="tpu_custom_call" | custom-call | flops 1 | bytes 1 | tf_op jit(solution)/shard_map/normed_back/pallas_call | solution.py:293
  283.4 8.5 %qkv_grad.1 = (bf16[4,776,128]{2,1,0:T(8,128)(2,1)}, bf16[4,776,128]{2,1,0:T(8,128)(2,1)}) custom-call(s32[3]{0:T(128)} %pad_add_fusion.me, bf16[1536,1024]{1,0:T(8,128)(2,1)} %bitcast.89, bf16[1536,384]{1,0:T(8,128)(2,1)} %bitcast.75, bf16[1536,384]{1,0:T(8,128)(2,1)} %bitcast.76, bf16[776,1024]{1,0:T(8,128)(2,1)} %get-tuple-element.217.w), custom_call_target="tpu_custom_call" | custom-call | flops 1 | bytes 1 | tf_op jit(solution)/shard_map/qkv_grad/pallas_call | solution.py:293
  296.2 3.0 collective-permute-start.69
  299.3 3.2 collective-permute-done.63.p2
  303.9 5.8 %final.1 = f32[384,1024]{1,0:T(8,128)} custom-call(s32[1]{0:T(128)} %bitcast.me, bf16[384,1024]{1,0:T(8,128)(2,1)} %copy-done.51, bf16[384,1024]{1,0:T(8,128)(2,1)} %copy-done.52, bf16[4,384,384]{2,1,0:T(8,128)(2,1)} %get-tuple-element.267.da, bf16[4,384,384]{2,1,0:T(8,128)(2,1)} %get-tuple-element.298.db, bf16[776,1024]{1,0:T(8,128)(2,1)} %get-tuple-element.217.w, ...), custom_call_target="tpu_custom_call" | custom-call | flops 1 | bytes 1 | tf_op jit(solution)/shard_map/final/pallas_call | solution.py:293
  320.4 5.4 %place_units.1 = (f32[128,2816]{1,0:T(8,128)}, f32[128,2816]{1,0:T(8,128)}, f32[128,2816]{1,0:T(8,128)}) custom-call(s32[1]{0:T(128)} %bitcast.me, bf16[2112,128]{1,0:T(8,128)(2,1)} %copy-done.26, bf16[2112,128]{1,0:T(8,128)(2,1)} %copy-done.62, bf16[2112,128]{1,0:T(8,128)(2,1)} %copy-done.61, bf16[2112,128]{1,0:T(8,128)(2,1)} %copy-done.63), custom_call_target="tpu_custom_call" | custom-call | flops 1 | bytes 1 | tf_op jit(solution)/shard_map/place_units/pallas_call | solution.py:293
  325.9 3.6 %all-to-all-start = ((bf16[4,384,256]{2,1,0:T(8,128)(2,1)}), bf16[4,384,256]{2,1,0:T(8,128)(2,1)S(1)}, u32[]{:S(2)}, u32[]{:S(2)}) async-start(bf16[4,384,256]{2,1,0:T(8,128)(2,1)} %get-tuple-element.309), calls=%async_computation | async-start | bytes 1572864 | tf_op jit(solution)/shard_map/all_to_all | solution.py:891
  335.4 3.1 fusion.1
  338.5 3.1 all-to-all-done.v
  (365 shorter events, 125.2 us)
Async XLA Ops:
  7.8 18.0 %collective-permute-start.3 = (bf16[1288,128]{1,0:T(8,128)(2,1)}, bf16[1288,128]{1,0:T(8,128)(2,1)}, u32[]{:S(2)}, u32[]{:S(2)}) collective-permute-start(bf16[1288,128]{1,0:T(8,128)(2,1)} %concatenate.30.refs_0_), channel_id=1, source_target_pairs={{0,2},{1,3},{2,0},{3,1},{4,6},{5,7},{6,4},{7,5},{8,10},{9,11},{10,... | collective-permute-start | bytes 989192 | tf_op jit(solution)/shard_map/ppermute | solution.py:617
  10.9 31.5 %collective-permute-start.2 = (bf16[1288,128]{1,0:T(8,128)(2,1)}, bf16[1288,128]{1,0:T(8,128)(2,1)}, u32[]{:S(2)}, u32[]{:S(2)}) collective-permute-start(bf16[1288,128]{1,0:T(8,128)(2,1)} %concatenate.30.refs_0_), channel_id=1, source_target_pairs={{0,1},{1,0},{2,3},{3,2},{4,5},{5,4},{6,7},{7,6},{8,9},{9,8},{10,11... | collective-permute-start | bytes 989192 | tf_op jit(solution)/shard_map/ppermute | solution.py:617
  12.4 26.0 %collective-permute-start.5 = (bf16[1288,128]{1,0:T(8,128)(2,1)}, bf16[1288,128]{1,0:T(8,128)(2,1)}, u32[]{:S(2)}, u32[]{:S(2)}) collective-permute-start(bf16[1288,128]{1,0:T(8,128)(2,1)} %concatenate.30.refs_0_), channel_id=1, source_target_pairs={{0,4},{1,5},{2,6},{3,7},{4,0},{5,1},{6,2},{7,3},{8,12},{9,13},{10,... | collective-permute-start | bytes 989192 | tf_op jit(solution)/shard_map/ppermute | solution.py:617
  15.0 24.0 %collective-permute-start.7 = (bf16[1288,128]{1,0:T(8,128)(2,1)}, bf16[1288,128]{1,0:T(8,128)(2,1)}, u32[]{:S(2)}, u32[]{:S(2)}) collective-permute-start(bf16[1288,128]{1,0:T(8,128)(2,1)} %concatenate.30.refs_0_), channel_id=1, source_target_pairs={{0,6},{1,7},{2,4},{3,5},{4,2},{5,3},{6,0},{7,1},{8,14},{9,15},{10,... | collective-permute-start | bytes 989192 | tf_op jit(solution)/shard_map/ppermute | solution.py:617
  17.1 32.1 %collective-permute-start.1 = (bf16[384,1536]{1,0:T(8,128)(2,1)}, bf16[384,1536]{1,0:T(8,128)(2,1)S(1)}, u32[]{:S(2)}, u32[]{:S(2)}) collective-permute-start(bf16[384,1536]{1,0:T(8,128)(2,1)} %pad_maximum_fusion), channel_id=1, source_target_pairs={{0,16},{8,24},{16,0},{24,8},{1,17},{9,25},{17,1},{25,9},{2,18},{10... | collective-permute-start | bytes 3538952 | tf_op jit(solution)/shard_map/ppermute | solution.py:602
  42.4 17.3 %collective-permute-start.10 = (bf16[704,128]{1,0:T(8,128)(2,1)S(1)}, bf16[704,128]{1,0:T(8,128)(2,1)S(1)}, u32[]{:S(2)}, u32[]{:S(2)}) collective-permute-start(bf16[704,128]{1,0:T(8,128)(2,1)S(1)} %bitcast.96), channel_id=1, source_target_pairs={{0,4},{1,5},{2,6},{3,7},{4,0},{5,1},{6,2},{7,3},{8,12},{9,13},{10,... | collective-permute-start | bytes 540680 | tf_op jit(solution)/shard_map/ppermute | solution.py:617
  59.9 28.5 %collective-permute-start.15 = (bf16[704,128]{1,0:T(8,128)(2,1)S(1)}, bf16[704,128]{1,0:T(8,128)(2,1)S(1)}, u32[]{:S(2)}, u32[]{:S(2)}) collective-permute-start(bf16[704,128]{1,0:T(8,128)(2,1)S(1)} %bitcast.90), channel_id=1, source_target_pairs={{0,2},{1,3},{2,0},{3,1},{4,6},{5,7},{6,4},{7,5},{8,10},{9,11},{10,... | collective-permute-start | bytes 540680 | tf_op jit(solution)/shard_map/ppermute | solution.py:617
  63.0 25.4 %collective-permute-start.16 = (bf16[704,128]{1,0:T(8,128)(2,1)S(1)}, bf16[704,128]{1,0:T(8,128)(2,1)S(1)}, u32[]{:S(2)}, u32[]{:S(2)}) collective-permute-start(bf16[704,128]{1,0:T(8,128)(2,1)S(1)} %bitcast.91), channel_id=1, source_target_pairs={{0,4},{1,5},{2,6},{3,7},{4,0},{5,1},{6,2},{7,3},{8,12},{9,13},{10,... | collective-permute-start | bytes 540680 | tf_op jit(solution)/shard_map/ppermute | solution.py:617
  63.0 25.4 %collective-permute-start.17 = (bf16[704,128]{1,0:T(8,128)(2,1)S(1)}, bf16[704,128]{1,0:T(8,128)(2,1)S(1)}, u32[]{:S(2)}, u32[]{:S(2)}) collective-permute-start(bf16[704,128]{1,0:T(8,128)(2,1)S(1)} %bitcast.92), channel_id=1, source_target_pairs={{0,6},{1,7},{2,4},{3,5},{4,2},{5,3},{6,0},{7,1},{8,14},{9,15},{10,... | collective-permute-start | bytes 540680 | tf_op jit(solution)/shard_map/ppermute | solution.py:617
  65.5 28.0 %collective-permute-start.14 = (bf16[2816,128]{1,0:T(8,128)(2,1)S(1)}, bf16[2816,128]{1,0:T(8,128)(2,1)S(1)}, u32[]{:S(2)}, u32[]{:S(2)}) collective-permute-start(bf16[2816,128]{1,0:T(8,128)(2,1)S(1)} %pad_maximum_fusion.4), channel_id=1, source_target_pairs={{0,1},{1,0},{2,3},{3,2},{4,5},{5,4},{6,7},{7,6},{8,9},{9,8},{10,11... | collective-permute-start | bytes 2162696 | tf_op jit(solution)/shard_map/ppermute | solution.py:617
  67.1 24.0 %collective-permute-start.13 = (bf16[384,1024]{1,0:T(8,128)(2,1)S(1)}, bf16[384,1024]{1,0:T(8,128)(2,1)S(1)}, u32[]{:S(2)}, u32[]{:S(2)}) collective-permute-start(bf16[384,1024]{1,0:T(8,128)(2,1)S(1)} %bitcast.80), channel_id=1, source_target_pairs={{0,16},{8,24},{16,0},{24,8},{1,17},{9,25},{17,1},{25,9},{2,18},{10... | collective-permute-start | bytes 2359304 | tf_op jit(solution)/shard_map/ppermute | solution.py:602
  88.6 17.3 %collective-permute-start.18 = (bf16[2816,128]{1,0:T(8,128)(2,1)S(1)}, bf16[2816,128]{1,0:T(8,128)(2,1)S(1)}, u32[]{:S(2)}, u32[]{:S(2)}) collective-permute-start(bf16[2816,128]{1,0:T(8,128)(2,1)S(1)} %pad_maximum_fusion.5), channel_id=1, source_target_pairs={{0,1},{1,0},{2,3},{3,2},{4,5},{5,4},{6,7},{7,6},{8,9},{9,8},{10,11... | collective-permute-start | bytes 2162696 | tf_op jit(solution)/shard_map/ppermute | solution.py:617
  93.5 35.3 %collective-permute-start.31 = (bf16[384,1024]{1,0:T(8,128)(2,1)S(1)}, bf16[384,1024]{1,0:T(8,128)(2,1)S(1)}, u32[]{:S(2)}, u32[]{:S(2)}) collective-permute-start(bf16[384,1024]{1,0:T(8,128)(2,1)S(1)} %bitcast.81), channel_id=1, source_target_pairs={{0,8},{8,0},{16,24},{24,16},{1,9},{9,1},{17,25},{25,17},{2,10},{10... | collective-permute-start | bytes 2359304 | tf_op jit(solution)/shard_map/ppermute | solution.py:602
  108.7 21.7 %collective-permute-start.32 = (bf16[2816,128]{1,0:T(8,128)(2,1)}, bf16[2816,128]{1,0:T(8,128)(2,1)S(1)}, u32[]{:S(2)}, u32[]{:S(2)}) collective-permute-start(bf16[2816,128]{1,0:T(8,128)(2,1)} %pad_maximum_fusion.6), channel_id=1, source_target_pairs={{0,1},{1,0},{2,3},{3,2},{4,5},{5,4},{6,7},{7,6},{8,9},{9,8},{10,11... | collective-permute-start | bytes 2162696 | tf_op jit(solution)/shard_map/ppermute | solution.py:617
  128.9 19.2 %collective-permute-start.34 = (bf16[192,1024]{1,0:T(8,128)(2,1)}, bf16[192,1024]{1,0:T(8,128)(2,1)S(1)}, u32[]{:S(2)}, u32[]{:S(2)}) collective-permute-start(bf16[192,1024]{1,0:T(8,128)(2,1)} %get-tuple-element.220.sa1.refs_3_), channel_id=1, source_target_pairs={{0,16},{8,24},{16,0},{24,8},{1,17},{9,25},{17,1},{25,9},{2,18},{10... | collective-permute-start | bytes 1179656 | tf_op jit(solution)/shard_map/ppermute | solution.py:602
  130.4 18.2 %collective-permute-start.37 = (bf16[384,1024]{1,0:T(8,128)(2,1)S(1)}, bf16[384,1024]{1,0:T(8,128)(2,1)S(1)}, u32[]{:S(2)}, u32[]{:S(2)}) collective-permute-start(bf16[384,1024]{1,0:T(8,128)(2,1)S(1)} %collective-permute-done.13.ga.refs_4_), channel_id=1, source_target_pairs={{0,8},{8,0},{16,24},{24,16},{1,9},{9,1},{17,25},{25,17},{2,10},{10... | collective-permute-start | bytes 2359304 | tf_op jit(solution)/shard_map/ppermute | solution.py:602
  177.0 23.2 %collective-permute-start.43 = (bf16[384,1024]{1,0:T(8,128)(2,1)S(1)}, bf16[384,1024]{1,0:T(8,128)(2,1)S(1)}, u32[]{:S(2)}, u32[]{:S(2)}) collective-permute-start(bf16[384,1024]{1,0:T(8,128)(2,1)S(1)} %add_convert_fusion.4), channel_id=1, source_target_pairs={{0,16},{8,24},{16,0},{24,8},{1,17},{9,25},{17,1},{25,9},{2,18},{10... | collective-permute-start | bytes 2359304 | tf_op jit(solution)/shard_map/ppermute | solution.py:602
  185.6 18.4 %collective-permute-start.44 = (bf16[4,704,128]{2,1,0:T(8,128)(2,1)}, bf16[4,704,128]{2,1,0:T(8,128)(2,1)S(1)}, u32[]{:S(2)}, u32[]{:S(2)}) collective-permute-start(bf16[4,704,128]{2,1,0:T(8,128)(2,1)} %get-tuple-element.247), channel_id=1, source_target_pairs={{0,1},{1,0},{2,3},{3,2},{4,5},{5,4},{6,7},{7,6},{8,9},{9,8},{10,11... | collective-permute-start | bytes 2162696 | tf_op jit(solution)/shard_map/ppermute | solution.py:617
  204.2 44.3 %collective-permute-start.50 = (bf16[4,704,128]{2,1,0:T(8,128)(2,1)}, bf16[4,704,128]{2,1,0:T(8,128)(2,1)}, u32[]{:S(2)}, u32[]{:S(2)}) collective-permute-start(bf16[4,704,128]{2,1,0:T(8,128)(2,1)} %get-tuple-element.271), channel_id=1, source_target_pairs={{0,1},{1,0},{2,3},{3,2},{4,5},{5,4},{6,7},{7,6},{8,9},{9,8},{10,11... | collective-permute-start | bytes 2162696 | tf_op jit(solution)/shard_map/ppermute | solution.py:617
  228.1 22.5 %collective-permute-start.51 = (bf16[704,128]{1,0:T(8,128)(2,1)S(1)}, bf16[704,128]{1,0:T(8,128)(2,1)S(1)}, u32[]{:S(2)}, u32[]{:S(2)}) collective-permute-start(bf16[704,128]{1,0:T(8,128)(2,1)S(1)} %get-tuple-element.360), channel_id=1, source_target_pairs={{0,2},{1,3},{2,0},{3,1},{4,6},{5,7},{6,4},{7,5},{8,10},{9,11},{10,... | collective-permute-start | bytes 540680 | tf_op jit(solution)/shard_map/ppermute | solution.py:617
  231.1 19.5 %collective-permute-start.52 = (bf16[704,128]{1,0:T(8,128)(2,1)S(1)}, bf16[704,128]{1,0:T(8,128)(2,1)S(1)}, u32[]{:S(2)}, u32[]{:S(2)}) collective-permute-start(bf16[704,128]{1,0:T(8,128)(2,1)S(1)} %get-tuple-element.359), channel_id=1, source_target_pairs={{0,4},{1,5},{2,6},{3,7},{4,0},{5,1},{6,2},{7,3},{8,12},{9,13},{10,... | collective-permute-start | bytes 540680 | tf_op jit(solution)/shard_map/ppermute | solution.py:617
  231.1 19.5 %collective-permute-start.53 = (bf16[704,128]{1,0:T(8,128)(2,1)S(1)}, bf16[704,128]{1,0:T(8,128)(2,1)S(1)}, u32[]{:S(2)}, u32[]{:S(2)}) collective-permute-start(bf16[704,128]{1,0:T(8,128)(2,1)S(1)} %get-tuple-element.358), channel_id=1, source_target_pairs={{0,6},{1,7},{2,4},{3,5},{4,2},{5,3},{6,0},{7,1},{8,14},{9,15},{10,... | collective-permute-start | bytes 540680 | tf_op jit(solution)/shard_map/ppermute | solution.py:617
  247.8 22.1 %collective-permute-start.49 = (bf16[384,1024]{1,0:T(8,128)(2,1)S(1)}, bf16[384,1024]{1,0:T(8,128)(2,1)}, u32[]{:S(2)}, u32[]{:S(2)}) collective-permute-start(bf16[384,1024]{1,0:T(8,128)(2,1)S(1)} %add_convert_fusion.3), channel_id=1, source_target_pairs={{0,16},{8,24},{16,0},{24,8},{1,17},{9,25},{17,1},{25,9},{2,18},{10... | collective-permute-start | bytes 2359304 | tf_op jit(solution)/shard_map/ppermute | solution.py:602
  249.8 20.1 %collective-permute-start.54 = (bf16[4,704,128]{2,1,0:T(8,128)(2,1)S(1)}, bf16[4,704,128]{2,1,0:T(8,128)(2,1)S(1)}, u32[]{:S(2)}, u32[]{:S(2)}) collective-permute-start(bf16[4,704,128]{2,1,0:T(8,128)(2,1)S(1)} %copy-done.76), channel_id=1, source_target_pairs={{0,1},{1,0},{2,3},{3,2},{4,5},{5,4},{6,7},{7,6},{8,9},{9,8},{10,11... | collective-permute-start | bytes 2162696 | tf_op jit(solution)/shard_map/ppermute | solution.py:617
  250.8 19.1 %collective-permute-start.55 = (bf16[704,128]{1,0:T(8,128)(2,1)S(1)}, bf16[704,128]{1,0:T(8,128)(2,1)S(1)}, u32[]{:S(2)}, u32[]{:S(2)}) collective-permute-start(bf16[704,128]{1,0:T(8,128)(2,1)S(1)} %get-tuple-element.356), channel_id=1, source_target_pairs={{0,2},{1,3},{2,0},{3,1},{4,6},{5,7},{6,4},{7,5},{8,10},{9,11},{10,... | collective-permute-start | bytes 540680 | tf_op jit(solution)/shard_map/ppermute | solution.py:617
  251.9 18.0 %collective-permute-start.56 = (bf16[704,128]{1,0:T(8,128)(2,1)S(1)}, bf16[704,128]{1,0:T(8,128)(2,1)S(1)}, u32[]{:S(2)}, u32[]{:S(2)}) collective-permute-start(bf16[704,128]{1,0:T(8,128)(2,1)S(1)} %get-tuple-element.355), channel_id=1, source_target_pairs={{0,4},{1,5},{2,6},{3,7},{4,0},{5,1},{6,2},{7,3},{8,12},{9,13},{10,... | collective-permute-start | bytes 540680 | tf_op jit(solution)/shard_map/ppermute | solution.py:617
  252.9 17.0 %collective-permute-start.57 = (bf16[704,128]{1,0:T(8,128)(2,1)S(1)}, bf16[704,128]{1,0:T(8,128)(2,1)S(1)}, u32[]{:S(2)}, u32[]{:S(2)}) collective-permute-start(bf16[704,128]{1,0:T(8,128)(2,1)S(1)} %get-tuple-element.354), channel_id=1, source_target_pairs={{0,6},{1,7},{2,4},{3,5},{4,2},{5,3},{6,0},{7,1},{8,14},{9,15},{10,... | collective-permute-start | bytes 540680 | tf_op jit(solution)/shard_map/ppermute | solution.py:617
  275.8 17.9 %collective-permute-start.67 = (bf16[4,520,128]{2,1,0:T(8,128)(2,1)S(1)}, bf16[4,520,128]{2,1,0:T(8,128)(2,1)S(1)}, u32[]{:S(2)}, u32[]{:S(2)}) collective-permute-start(bf16[4,520,128]{2,1,0:T(8,128)(2,1)S(1)} %copy-done.77), channel_id=1, source_target_pairs={{0,1},{1,0},{2,3},{3,2},{4,5},{5,4},{6,7},{7,6},{8,9},{9,8},{10,11... | collective-permute-start | bytes 1597448 | tf_op jit(solution)/shard_map/ppermute | solution.py:617
  282.0 20.5 %collective-permute-start.63 = (bf16[384,1024]{1,0:T(8,128)(2,1)S(1)}, bf16[384,1024]{1,0:T(8,128)(2,1)S(1)}, u32[]{:S(2)}, u32[]{:S(2)}) collective-permute-start(bf16[384,1024]{1,0:T(8,128)(2,1)S(1)} %add_convert_fusion.1), channel_id=1, source_target_pairs={{0,16},{8,24},{16,0},{24,8},{1,17},{9,25},{17,1},{25,9},{2,18},{10... | collective-permute-start | bytes 2359304 | tf_op jit(solution)/shard_map/ppermute | solution.py:602
  293.9 18.7 %collective-permute-start.68 = (bf16[4,776,128]{2,1,0:T(8,128)(2,1)S(1)}, bf16[4,776,128]{2,1,0:T(8,128)(2,1)S(1)}, u32[]{:S(2)}, u32[]{:S(2)}) collective-permute-start(bf16[4,776,128]{2,1,0:T(8,128)(2,1)S(1)} %copy-done.74), channel_id=1, source_target_pairs={{0,1},{1,0},{2,3},{3,2},{4,5},{5,4},{6,7},{7,6},{8,9},{9,8},{10,11... | collective-permute-start | bytes 2383880 | tf_op jit(solution)/shard_map/ppermute | solution.py:617
  295.0 16.9 %collective-permute-start.65 = (bf16[2112,128]{1,0:T(8,128)(2,1)S(1)}, bf16[2112,128]{1,0:T(8,128)(2,1)S(1)}, u32[]{:S(2)}, u32[]{:S(2)}) collective-permute-start(bf16[2112,128]{1,0:T(8,128)(2,1)S(1)} %pad_maximum_fusion.7.p0), channel_id=1, source_target_pairs={{0,16},{8,24},{16,0},{24,8},{1,17},{9,25},{17,1},{25,9},{2,18},{10... | collective-permute-start | bytes 1622024 | tf_op jit(solution)/shard_map/ppermute | solution.py:602
  314.3 17.9 %collective-permute-start.72 = (bf16[776,128]{1,0:T(8,128)(2,1)S(1)}, bf16[776,128]{1,0:T(8,128)(2,1)}, u32[]{:S(2)}, u32[]{:S(2)}) collective-permute-start(bf16[776,128]{1,0:T(8,128)(2,1)S(1)} %get-tuple-element.344), channel_id=1, source_target_pairs={{0,2},{1,3},{2,0},{3,1},{4,6},{5,7},{6,4},{7,5},{8,10},{9,11},{10,... | collective-permute-start | bytes 595976 | tf_op jit(solution)/shard_map/ppermute | solution.py:617
  (127 other events, 1231.4 us)

commit v3 on v2

--- a/solution.py
+++ b/solution.py
@@ -849,7 +849,8 @@
     beside = seq_permute(nb1, 1)
     crossed_far = seq_permute(nb_both, 2)
     qkv_sums = qkv_grads(d_a, after(d_b, nb_both, beside))
-    crossed_far = after(crossed_far, qkv_sums[0])
+    output = add(middle, o[0], o1, o2)[None]
+    crossed_far = after(crossed_far, qkv_sums[0], output)
     if ring:
         out_both = add(out_part[0], after(out_crossed, qkv_sums[0]))
         qkv_crossed = fsdp_permute(after(qkv_sums[1], out_both), 1)
@@ -888,8 +889,7 @@
     if not ring:
         units_far = seq_permute(units_sent, 2)
     units_all = [units_sent, seq_permute(units_sent, 1), units_far, seq_permute(units_far, 1)]
-    v_all = lax.all_to_all(after(v_b, tokens_grad, *units_all), "seq", split_axis=0, concat_axis=0)
-    output = add(middle, o[0], o1, o2)[None]
+    v_all = lax.all_to_all(after(v_b, tokens_grad), "seq", split_axis=0, concat_axis=0)
     (values_grad,) = vmem_call(
         place_values_kernel, "place_values", [((rows, d), F32)], me, [v_all], cost(0, 3e6)
     )
@@ -916,8 +916,8 @@
         cost(0, 1e6),
     )
     if ring:
-        qkv_share = add(*all_after(qkv_sent, out_grad, gate_grad))
-    qkv_far = after(seq_permute(qkv_share, 2), values_grad, output)
+        qkv_share = add(*all_after(qkv_sent, out_grad, gate_grad, values_grad))
+    qkv_far = seq_permute(qkv_share, 2)
     qkv_all = [qkv_share, seq_permute(qkv_share, 1), qkv_far, seq_permute(qkv_far, 1)]
     query_grad, key_grad, value_grad, gain_grad = vmem_call(
         place_qkv_kernel,

time: 356 us -> 354 us (level)
    ppermute x41, waiting for transfers between devices: 24.9 us -> 31.1 us  [seq_permute(): return lax.ppermute(value, 'seq', [(i, i ^ flip) for i in range(GROUPS)])]
    unnamed x163 -> x155, local copies, waits for them, and re-layouts: 10.9 us -> 10.1 us
  transfers between devices with their start and end apart: 81 -> 81, of which waited for: 21 -> 21; matrix products, arithmetic and copies ran while one was open for 7% -> 6% of each run, Pallas kernels for 39% -> 39%
where the time goes in v3:
time: 354 us; the launch traced here: 349 us
  Pallas kernels  166 us (47%)
  starting transfers between devices  81.6 us (23%)
  waiting for transfers between devices  60.1 us (17%)
  local copies, waits for them, and re-layouts  21.6 us (6%)
  other arithmetic  18.2 us (5%)
    pallas_call x14, Pallas kernels, vmem_call(): pl.pallas_call(kernel, grid_spec=pltpu.PrefetchScalarGridSpec(num_scalar_...  73.6 us
    ppermute x39, starting transfers between devices, fsdp_permute(): return lax.ppermute(value, 'fsdp', [(i, i ^ flip) for i in range(n)])  58.4 us
    pallas_call x2, Pallas kernels, any_call(): pl.pallas_call(kernel, grid_spec=pltpu.PrefetchScalarGridSpec(num_scalar_...  34 us
    ppermute x41, waiting for transfers between devices, seq_permute(): return lax.ppermute(value, 'seq', [(i, i ^ flip) for i in range(GROUPS)])  31.1 us
    ppermute x39, waiting for transfers between devices, fsdp_permute(): return lax.ppermute(value, 'fsdp', [(i, i ^ flip) for i in range(n)])  29 us
    pallas_call x2, Pallas kernels, attention_back(): pl.pallas_call(attn_back_kernel, grid_spec=pltpu.PrefetchScalarGridSpec(n...  28.9 us
    ppermute x41, starting transfers between devices, seq_permute(): return lax.ppermute(value, 'seq', [(i, i ^ flip) for i in range(GROUPS)])  19.7 us
    pallas_call x2, Pallas kernels, attention(): pl.pallas_call(attn_kernel, grid_spec=pltpu.PrefetchScalarGridSpec(num_sc...  17.8 us
  transfers between devices with their start and end apart: 81, of which 21 were waited for; matrix products, arithmetic and copies ran while one was open for 6% of the time, Pallas kernels for 39%

profile of v3, /device:TPU:0, one launch (start us, length us, event | category | flops | bytes accessed | tf_op | source)
XLA Modules:
  0.0 349.1 jit_solution(1004509072946911041)
XLA Ops:
  4.0 3.9 %concatenate.30.refs_0_ = bf16[1288,128]{1,0:T(8,128)(2,1)} concatenate(bf16[256,128]{1,0:T(8,128)(2,1)S(1)} %bitcast.107, bf16[256,128]{1,0:T(8,128)(2,1)S(1)} %bitcast.105, bf16[256,128]{1,0:T(8,128)(2,1)S(1)} %bitcast.106, bf16[1,128]{1,0:T(2,128)(2,1)} %bitcast.108, bf16[1,128]{1,0:T(2,128)(2,1)} %bitcast.109, bf16[6,128]{1,0:T(8,128)(2,1)S(1)} %broadcast_in_dim.26, ...), dimensions={0} | concatenate | bytes 659456 | tf_op jit(solution)/shard_map/concatenate | solution.py:665
  7.8 3.0 collective-permute-start.3
  21.6 4.3 %fusion = (f32[4,384,128]{2,1,0:T(8,128)}, f32[4,384,128]{2,1,0:T(8,128)}) fusion(f32[128]{0:T(128)S(1)} %mul.78, f32[128]{0:T(128)S(1)} %mul.75, f32[4,384]{1,0:T(4,128)S(1)} %add_convert_fusion.15), kind=kLoop, calls=%fused_computation.14 | loop fusion | flops 393216 | bytes 1580032 | tf_op jit(solution)/shard_map/mul | solution.py:672
  26.6 11.8 %collective-permute-done.5.refs_4_ = bf16[1288,128]{1,0:T(8,128)(2,1)} collective-permute-done((bf16[1288,128]{1,0:T(8,128)(2,1)}, bf16[1288,128]{1,0:T(8,128)(2,1)}, u32[]{:S(2)}, u32[]{:S(2)}) %collective-permute-start.5) | collective-permute-done | bytes 329760 | tf_op jit(solution)/shard_map/ppermute | solution.py:617
  42.4 5.5 %collective-permute-start.10 = (bf16[704,128]{1,0:T(8,128)(2,1)S(1)}, bf16[704,128]{1,0:T(8,128)(2,1)S(1)}, u32[]{:S(2)}, u32[]{:S(2)}) collective-permute-start(bf16[704,128]{1,0:T(8,128)(2,1)S(1)} %bitcast.96), channel_id=1, source_target_pairs={{0,4},{1,5},{2,6},{3,7},{4,0},{5,1},{6,2},{7,3},{8,12},{9,13},{10,... | collective-permute-start | bytes 540680 | tf_op jit(solution)/shard_map/ppermute | solution.py:617
  50.6 9.1 %collective-permute-done.10.refs_2_ = bf16[704,128]{1,0:T(8,128)(2,1)S(1)} collective-permute-done((bf16[704,128]{1,0:T(8,128)(2,1)S(1)}, bf16[704,128]{1,0:T(8,128)(2,1)S(1)}, u32[]{:S(2)}, u32[]{:S(2)}) %collective-permute-start.10) | collective-permute-done | bytes 180256 | tf_op jit(solution)/shard_map/ppermute | solution.py:617
  59.9 3.1 collective-permute-start.15
  68.6 11.3 %qkv.1 = (bf16[4,384,256]{2,1,0:T(8,128)(2,1)}, bf16[4,384,256]{2,1,0:T(8,128)(2,1)}, bf16[4,384,256]{2,1,0:T(8,128)(2,1)}, bf16[4,384,1024]{2,1,0:T(8,128)(2,1)...) custom-call(s32[1]{0:T(128)} %bitcast.1.me, bf16[384,1024]{1,0:T(8,128)(2,1)} %bitcast.70, ...), custom_call_target="tpu_custom_call" | custom-call | flops 1 | bytes 1 | tf_op jit(solution)/shard_map/qkv/pallas_call | solution.py:99
  80.0 8.4 %attention.2 = (bf16[384,128]{1,0:T(8,128)(2,1)}, bf16[384,128]{1,0:T(8,128)(2,1)}, bf16[384,128]{1,0:T(8,128)(2,1)}, bf16[384,128]{1,0:T(8,128)(2,1)}, f32[2,4,8,384]{3,2,1,0:T(8,128)}) custom-call(s32[1]{0:T(128)} %bitcast.me, bf16[4,384,256]{2,1,0:T(8,128)(2,1)} %get-tuple-element.277.q, bf16[4,384,256]{2,1,0:T(8,128)(2,1)} %get-tuple-element.179.k, ...), custom_call_target="tpu_custom_call" | custom-call | flops 1 | bytes 1 | tf_op jit(solution)/shard_map/attention/pallas_call | solution.py:167
  93.6 9.3 %attention.3 = (bf16[384,256]{1,0:T(8,128)(2,1)}, bf16[384,256]{1,0:T(8,128)(2,1)}, bf16[384,256]{1,0:T(8,128)(2,1)}, bf16[384,256]{1,0:T(8,128)(2,1)}, f32[2,4,8,384]{3,2,1,0:T(8,128)}) custom-call(s32[1]{0:T(128)} %bitcast.me, bf16[4,384,256]{2,1,0:T(8,128)(2,1)} %get-tuple-element.277.q, bf16[4,384,256]{2,1,0:T(8,128)(2,1)} %get-tuple-element.179.k, ...), custom_call_target="tpu_custom_call" | custom-call | flops 1 | bytes 1 | tf_op jit(solution)/shard_map/attention/pallas_call | solution.py:167
  109.6 4.2 %collective-permute-done.20.m2 = bf16[384,256]{1,0:T(8,128)(2,1)S(1)} collective-permute-done((bf16[384,256]{1,0:T(8,128)(2,1)}, bf16[384,256]{1,0:T(8,128)(2,1)S(1)}, u32[]{:S(2)}, u32[]{:S(2)}) %collective-permute-start.20) | collective-permute-done | bytes 196640 | tf_op jit(solution)/shard_map/ppermute | solution.py:602
  113.8 3.4 collective-permute-done.21.m3
  122.4 5.5 %out.1 = (f32[384,1024]{1,0:T(8,128)}, bf16[192,1024]{1,0:T(8,128)(2,1)}, bf16[192,1024]{1,0:T(8,128)(2,1)}) custom-call(s32[1]{0:T(128)} %bitcast.me, bf16[384,256]{1,0:T(8,128)(2,1)} %get-tuple-element.212.m0, bf16[384,256]{1,0:T(8,128)(2,1)} %copy-done.28, bf16[384,256]{1,0:T(8,128)(2,1)} %copy-done.30, bf16[384,256]{1,0:T(8,128)(2,1)} %copy-done.32, ...), custom_call_target="tpu_custom_call" | custom-call | flops 1 | bytes 1 | tf_op jit(solution)/shard_map/out/pallas_call | solution.py:293
  132.1 12.7 %mlp.2 = (bf16[768,704]{1,0:T(8,128)(2,1)}, bf16[768,704]{1,0:T(8,128)(2,1)}, bf16[768,704]{1,0:T(8,128)(2,1)}, bf16[384,1024]{1,0:T(8,128)(2,1)}, bf16[384,1024]{1,0:T(8,128)(2,1)}) custom-call(s32[1]{0:T(128)} %bitcast.1.me, bf16[192,1024]{1,0:T(8,128)(2,1)} %get-tuple-element.218.sa0.refs_2_, bf16[192,1024]{1,0:T(8,128)(2,1)} %get-tuple-element.219.sa1.refs_3_, ...), custom_call_target="tpu_custom_call" | custom-call | flops 1 | bytes 1 | tf_op jit(solution)/shard_map/mlp/pallas_call | solution.py:377
  144.8 3.3 collective-permute-done.34.sa1.refs_7_
  151.4 21.4 %mlp.3 = (bf16[768,704]{1,0:T(8,128)(2,1)}, bf16[768,704]{1,0:T(8,128)(2,1)}, bf16[768,704]{1,0:T(8,128)(2,1)}, bf16[384,1024]{1,0:T(8,128)(2,1)}, bf16[384,1024]{1,0:T(8,128)(2,1)}) custom-call(s32[1]{0:T(128)} %bitcast.1.me, bf16[192,1024]{1,0:T(8,128)(2,1)} %copy-done.11, bf16[192,1024]{1,0:T(8,128)(2,1)} %copy-done.12, bf16[192,1024]{1,0:T(8,128)(2,1)} %copy-done.13, ...), custom_call_target="tpu_custom_call" | custom-call | flops 1 | bytes 1 | tf_op jit(solution)/shard_map/mlp/pallas_call | solution.py:377
  179.3 6.4 %unit_grads.3 = (bf16[4,704,128]{2,1,0:T(8,128)(2,1)}, bf16[4,704,128]{2,1,0:T(8,128)(2,1)}) custom-call(s32[1]{0:T(128)} %bitcast.1.me, bf16[768,704]{1,0:T(8,128)(2,1)} %get-tuple-element.221.refs_0_.hn, bf16[768,704]{1,0:T(8,128)(2,1)} %get-tuple-element.232.refs_1_.hf, bf16[384,1024]{1,0:T(8,128)(2,1)} %bitcast.78, bf16[384,1024]{1,0:T(8,128)(2,1)} %copy-done.17, ...), custom_call_target="tpu_custom_call" | custom-call | flops 1 | bytes 1 | tf_op jit(solution)/shard_map/unit_grads/pallas_call | solution.py:293
  186.6 6.1 %mlp_out.1 = (bf16[384,1024]{1,0:T(8,128)(2,1)}, bf16[384,1024]{1,0:T(8,128)(2,1)}, bf16[384,1024]{1,0:T(8,128)(2,1)}, bf16[384,1024]{1,0:T(8,128)(2,1)}) custom-call(s32[1]{0:T(128)} %bitcast.1.me, bf16[768,704]{1,0:T(8,128)(2,1)} %get-tuple-element.221.refs_0_.hn, bf16[768,704]{1,0:T(8,128)(2,1)} %get-tuple-element.232.refs_1_.hf, ...), custom_call_target="tpu_custom_call" | custom-call | flops 1 | bytes 1 | tf_op jit(solution)/shard_map/mlp_out/pallas_call | solution.py:293
  193.4 6.9 %unit_grads.4 = (bf16[4,704,128]{2,1,0:T(8,128)(2,1)}, bf16[4,704,128]{2,1,0:T(8,128)(2,1)}) custom-call(s32[1]{0:T(128)} %bitcast.1.me, bf16[768,704]{1,0:T(8,128)(2,1)} %get-tuple-element.236.refs_0_, bf16[768,704]{1,0:T(8,128)(2,1)} %get-tuple-element.238.refs_1_, bf16[192,1024]{1,0:T(8,128)(2,1)} %get-tuple-element.218.sa0.refs_2_, ...), custom_call_target="tpu_custom_call" | custom-call | flops 1 | bytes 1 | tf_op jit(solution)/shard_map/unit_grads/pallas_call | solution.py:293
  206.1 5.9 %middle.1 = (f32[384,1024]{1,0:T(8,128)}, bf16[384,1024]{1,0:T(8,128)(2,1)}, bf16[384,512]{1,0:T(8,128)(2,1)}, bf16[384,256]{1,0:T(8,128)(2,1)}, bf16[384,256]{1...) custom-call(s32[1]{0:T(128)} %bitcast.me, ...), custom_call_target="tpu_custom_call" | custom-call | flops 1 | bytes 1 | tf_op jit(solution)/shard_map/middle/pallas_call | solution.py:293
  216.6 5.0 %out_grad.1 = (bf16[4,520,128]{2,1,0:T(8,128)(2,1)}, bf16[4,520,128]{2,1,0:T(8,128)(2,1)}) custom-call(s32[3]{0:T(128)} %pad_add_fusion.me, bf16[384,256]{1,0:T(8,128)(2,1)} %get-tuple-element.212.m0, bf16[384,256]{1,0:T(8,128)(2,1)} %copy-done.28, bf16[384,256]{1,0:T(8,128)(2,1)} %copy-done.30, bf16[384,256]{1,0:T(8,128)(2,1)} %copy-done.32, ...), custom_call_target="tpu_custom_call" | custom-call | flops 1 | bytes 1 | tf_op jit(solution)/shard_map/out_grad/pallas_call | solution.py:293
  221.6 6.3 %unit_grads.5 = (bf16[4,704,128]{2,1,0:T(8,128)(2,1)}, bf16[4,704,128]{2,1,0:T(8,128)(2,1)}) custom-call(s32[1]{0:T(128)} %bitcast.1.me, bf16[768,704]{1,0:T(8,128)(2,1)} %get-tuple-element.255.refs_0_, bf16[768,704]{1,0:T(8,128)(2,1)} %get-tuple-element.260.refs_1_, bf16[192,1024]{1,0:T(8,128)(2,1)} %get-tuple-element.218.sa0.refs_2_, ...), custom_call_target="tpu_custom_call" | custom-call | flops 1 | bytes 1 | tf_op jit(solution)/shard_map/unit_grads/pallas_call | solution.py:293
  233.5 14.2 %attention_back.2 = (bf16[4,384,384]{2,1,0:T(8,128)(2,1)}, bf16[4,384,128]{2,1,0:T(8,128)(2,1)}) custom-call(s32[1]{0:T(128)} %bitcast.me, bf16[4,384,256]{2,1,0:T(8,128)(2,1)} %get-tuple-element.277.q, bf16[4,384,256]{2,1,0:T(8,128)(2,1)} %get-tuple-element.179.k, bf16[4,384,256]{2,1,0:T(8,128)(2,1)} %get-tuple-element.180.v, ...), custom_call_target="tpu_custom_call" | custom-call | flops 1 | bytes 1 | tf_op jit(solution)/shard_map/attention_back/pallas_call | solution.py:245
  255.2 14.6 %attention_back.3 = (bf16[4,384,384]{2,1,0:T(8,128)(2,1)}, bf16[4,384,256]{2,1,0:T(8,128)(2,1)}) custom-call(s32[1]{0:T(128)} %bitcast.me, bf16[4,384,256]{2,1,0:T(8,128)(2,1)} %get-tuple-element.277.q, bf16[4,384,256]{2,1,0:T(8,128)(2,1)} %get-tuple-element.179.k, bf16[4,384,256]{2,1,0:T(8,128)(2,1)} %get-tuple-element.180.v, ...), custom_call_target="tpu_custom_call" | custom-call | flops 1 | bytes 1 | tf_op jit(solution)/shard_map/attention_back/pallas_call | solution.py:245
  270.2 5.1 %normed_back.1 = (bf16[384,1024]{1,0:T(8,128)(2,1)}, bf16[384,1024]{1,0:T(8,128)(2,1)}, bf16[384,1024]{1,0:T(8,128)(2,1)}) custom-call(s32[1]{0:T(128)} %bitcast.me, bf16[4,384,384]{2,1,0:T(8,128)(2,1)} %get-tuple-element.266.da, bf16[4,384,384]{2,1,0:T(8,128)(2,1)} %get-tuple-element.297.db, bf16[776,1024]{1,0:T(8,128)(2,1)} %get-tuple-element.216.w), custom_call_target="tpu_custom_call" | custom-call | flops 1 | bytes 1 | tf_op jit(solution)/shard_map/normed_back/pallas_call | solution.py:293
  283.3 8.5 %qkv_grad.1 = (bf16[4,776,128]{2,1,0:T(8,128)(2,1)}, bf16[4,776,128]{2,1,0:T(8,128)(2,1)}) custom-call(s32[3]{0:T(128)} %pad_add_fusion.me, bf16[1536,1024]{1,0:T(8,128)(2,1)} %bitcast.89, bf16[1536,384]{1,0:T(8,128)(2,1)} %bitcast.75, bf16[1536,384]{1,0:T(8,128)(2,1)} %bitcast.76, bf16[776,1024]{1,0:T(8,128)(2,1)} %get-tuple-element.216.w), custom_call_target="tpu_custom_call" | custom-call | flops 1 | bytes 1 | tf_op jit(solution)/shard_map/qkv_grad/pallas_call | solution.py:293
  296.2 3.0 collective-permute-start.66
  299.2 3.2 collective-permute-done.63.p2
  305.3 5.7 %final.1 = f32[384,1024]{1,0:T(8,128)} custom-call(s32[1]{0:T(128)} %bitcast.me, bf16[384,1024]{1,0:T(8,128)(2,1)} %copy-done.51, bf16[384,1024]{1,0:T(8,128)(2,1)} %copy-done.52, bf16[4,384,384]{2,1,0:T(8,128)(2,1)} %get-tuple-element.266.da, bf16[4,384,384]{2,1,0:T(8,128)(2,1)} %get-tuple-element.297.db, bf16[776,1024]{1,0:T(8,128)(2,1)} %get-tuple-element.216.w, ...), custom_call_target="tpu_custom_call" | custom-call | flops 1 | bytes 1 | tf_op jit(solution)/shard_map/final/pallas_call | solution.py:293
  312.5 3.5 %all-to-all-start = ((bf16[4,384,256]{2,1,0:T(8,128)(2,1)}), bf16[4,384,256]{2,1,0:T(8,128)(2,1)S(1)}, u32[]{:S(2)}, u32[]{:S(2)}) async-start(bf16[4,384,256]{2,1,0:T(8,128)(2,1)} %get-tuple-element.307), calls=%async_computation | async-start | bytes 1572864 | tf_op jit(solution)/shard_map/all_to_all | solution.py:892
  323.8 5.4 %place_units.1 = (f32[128,2816]{1,0:T(8,128)}, f32[128,2816]{1,0:T(8,128)}, f32[128,2816]{1,0:T(8,128)}) custom-call(s32[1]{0:T(128)} %bitcast.me, bf16[2112,128]{1,0:T(8,128)(2,1)} %copy-done.26, bf16[2112,128]{1,0:T(8,128)(2,1)} %collective-permute-done.73.p1, bf16[2112,128]{1,0:T(8,128)(2,1)} %collective-permute-done.74.p2, ...), custom_call_target="tpu_custom_call" | custom-call | flops 1 | bytes 1 | tf_op jit(solution)/shard_map/place_units/pallas_call | solution.py:293
  337.3 6.8 %collective-permute-done.78.p2 = bf16[776,128]{1,0:T(8,128)(2,1)S(1)} collective-permute-done((bf16[776,128]{1,0:T(8,128)(2,1)S(1)}, bf16[776,128]{1,0:T(8,128)(2,1)S(1)}, u32[]{:S(2)}, u32[]{:S(2)}) %collective-permute-start.78) | collective-permute-done | bytes 198688 | tf_op jit(solution)/shard_map/ppermute | solution.py:602
  (357 shorter events, 120.6 us)
Async XLA Ops:
  7.8 18.1 %collective-permute-start.3 = (bf16[1288,128]{1,0:T(8,128)(2,1)}, bf16[1288,128]{1,0:T(8,128)(2,1)}, u32[]{:S(2)}, u32[]{:S(2)}) collective-permute-start(bf16[1288,128]{1,0:T(8,128)(2,1)} %concatenate.30.refs_0_), channel_id=1, source_target_pairs={{0,2},{1,3},{2,0},{3,1},{4,6},{5,7},{6,4},{7,5},{8,10},{9,11},{10,... | collective-permute-start | bytes 989192 | tf_op jit(solution)/shard_map/ppermute | solution.py:617
  10.9 31.5 %collective-permute-start.2 = (bf16[1288,128]{1,0:T(8,128)(2,1)}, bf16[1288,128]{1,0:T(8,128)(2,1)}, u32[]{:S(2)}, u32[]{:S(2)}) collective-permute-start(bf16[1288,128]{1,0:T(8,128)(2,1)} %concatenate.30.refs_0_), channel_id=1, source_target_pairs={{0,1},{1,0},{2,3},{3,2},{4,5},{5,4},{6,7},{7,6},{8,9},{9,8},{10,11... | collective-permute-start | bytes 989192 | tf_op jit(solution)/shard_map/ppermute | solution.py:617
  12.4 26.0 %collective-permute-start.5 = (bf16[1288,128]{1,0:T(8,128)(2,1)}, bf16[1288,128]{1,0:T(8,128)(2,1)}, u32[]{:S(2)}, u32[]{:S(2)}) collective-permute-start(bf16[1288,128]{1,0:T(8,128)(2,1)} %concatenate.30.refs_0_), channel_id=1, source_target_pairs={{0,4},{1,5},{2,6},{3,7},{4,0},{5,1},{6,2},{7,3},{8,12},{9,13},{10,... | collective-permute-start | bytes 989192 | tf_op jit(solution)/shard_map/ppermute | solution.py:617
  15.0 24.0 %collective-permute-start.7 = (bf16[1288,128]{1,0:T(8,128)(2,1)}, bf16[1288,128]{1,0:T(8,128)(2,1)}, u32[]{:S(2)}, u32[]{:S(2)}) collective-permute-start(bf16[1288,128]{1,0:T(8,128)(2,1)} %concatenate.30.refs_0_), channel_id=1, source_target_pairs={{0,6},{1,7},{2,4},{3,5},{4,2},{5,3},{6,0},{7,1},{8,14},{9,15},{10,... | collective-permute-start | bytes 989192 | tf_op jit(solution)/shard_map/ppermute | solution.py:617
  17.1 32.1 %collective-permute-start.1 = (bf16[384,1536]{1,0:T(8,128)(2,1)}, bf16[384,1536]{1,0:T(8,128)(2,1)S(1)}, u32[]{:S(2)}, u32[]{:S(2)}) collective-permute-start(bf16[384,1536]{1,0:T(8,128)(2,1)} %pad_maximum_fusion), channel_id=1, source_target_pairs={{0,16},{8,24},{16,0},{24,8},{1,17},{9,25},{17,1},{25,9},{2,18},{10... | collective-permute-start | bytes 3538952 | tf_op jit(solution)/shard_map/ppermute | solution.py:602
  42.4 17.3 %collective-permute-start.10 = (bf16[704,128]{1,0:T(8,128)(2,1)S(1)}, bf16[704,128]{1,0:T(8,128)(2,1)S(1)}, u32[]{:S(2)}, u32[]{:S(2)}) collective-permute-start(bf16[704,128]{1,0:T(8,128)(2,1)S(1)} %bitcast.96), channel_id=1, source_target_pairs={{0,4},{1,5},{2,6},{3,7},{4,0},{5,1},{6,2},{7,3},{8,12},{9,13},{10,... | collective-permute-start | bytes 540680 | tf_op jit(solution)/shard_map/ppermute | solution.py:617
  59.9 28.5 %collective-permute-start.15 = (bf16[704,128]{1,0:T(8,128)(2,1)S(1)}, bf16[704,128]{1,0:T(8,128)(2,1)S(1)}, u32[]{:S(2)}, u32[]{:S(2)}) collective-permute-start(bf16[704,128]{1,0:T(8,128)(2,1)S(1)} %bitcast.90), channel_id=1, source_target_pairs={{0,2},{1,3},{2,0},{3,1},{4,6},{5,7},{6,4},{7,5},{8,10},{9,11},{10,... | collective-permute-start | bytes 540680 | tf_op jit(solution)/shard_map/ppermute | solution.py:617
  63.0 25.4 %collective-permute-start.16 = (bf16[704,128]{1,0:T(8,128)(2,1)S(1)}, bf16[704,128]{1,0:T(8,128)(2,1)S(1)}, u32[]{:S(2)}, u32[]{:S(2)}) collective-permute-start(bf16[704,128]{1,0:T(8,128)(2,1)S(1)} %bitcast.91), channel_id=1, source_target_pairs={{0,4},{1,5},{2,6},{3,7},{4,0},{5,1},{6,2},{7,3},{8,12},{9,13},{10,... | collective-permute-start | bytes 540680 | tf_op jit(solution)/shard_map/ppermute | solution.py:617
  63.0 25.5 %collective-permute-start.17 = (bf16[704,128]{1,0:T(8,128)(2,1)S(1)}, bf16[704,128]{1,0:T(8,128)(2,1)S(1)}, u32[]{:S(2)}, u32[]{:S(2)}) collective-permute-start(bf16[704,128]{1,0:T(8,128)(2,1)S(1)} %bitcast.92), channel_id=1, source_target_pairs={{0,6},{1,7},{2,4},{3,5},{4,2},{5,3},{6,0},{7,1},{8,14},{9,15},{10,... | collective-permute-start | bytes 540680 | tf_op jit(solution)/shard_map/ppermute | solution.py:617
  65.5 28.0 %collective-permute-start.14 = (bf16[2816,128]{1,0:T(8,128)(2,1)S(1)}, bf16[2816,128]{1,0:T(8,128)(2,1)S(1)}, u32[]{:S(2)}, u32[]{:S(2)}) collective-permute-start(bf16[2816,128]{1,0:T(8,128)(2,1)S(1)} %pad_maximum_fusion.4), channel_id=1, source_target_pairs={{0,1},{1,0},{2,3},{3,2},{4,5},{5,4},{6,7},{7,6},{8,9},{9,8},{10,11... | collective-permute-start | bytes 2162696 | tf_op jit(solution)/shard_map/ppermute | solution.py:617
  67.1 24.0 %collective-permute-start.13 = (bf16[384,1024]{1,0:T(8,128)(2,1)S(1)}, bf16[384,1024]{1,0:T(8,128)(2,1)S(1)}, u32[]{:S(2)}, u32[]{:S(2)}) collective-permute-start(bf16[384,1024]{1,0:T(8,128)(2,1)S(1)} %bitcast.80), channel_id=1, source_target_pairs={{0,16},{8,24},{16,0},{24,8},{1,17},{9,25},{17,1},{25,9},{2,18},{10... | collective-permute-start | bytes 2359304 | tf_op jit(solution)/shard_map/ppermute | solution.py:602
  88.6 17.3 %collective-permute-start.18 = (bf16[2816,128]{1,0:T(8,128)(2,1)S(1)}, bf16[2816,128]{1,0:T(8,128)(2,1)S(1)}, u32[]{:S(2)}, u32[]{:S(2)}) collective-permute-start(bf16[2816,128]{1,0:T(8,128)(2,1)S(1)} %pad_maximum_fusion.5), channel_id=1, source_target_pairs={{0,1},{1,0},{2,3},{3,2},{4,5},{5,4},{6,7},{7,6},{8,9},{9,8},{10,11... | collective-permute-start | bytes 2162696 | tf_op jit(solution)/shard_map/ppermute | solution.py:617
  93.6 35.3 %collective-permute-start.31 = (bf16[384,1024]{1,0:T(8,128)(2,1)S(1)}, bf16[384,1024]{1,0:T(8,128)(2,1)S(1)}, u32[]{:S(2)}, u32[]{:S(2)}) collective-permute-start(bf16[384,1024]{1,0:T(8,128)(2,1)S(1)} %bitcast.81), channel_id=1, source_target_pairs={{0,8},{8,0},{16,24},{24,16},{1,9},{9,1},{17,25},{25,17},{2,10},{10... | collective-permute-start | bytes 2359304 | tf_op jit(solution)/shard_map/ppermute | solution.py:602
  108.7 21.7 %collective-permute-start.32 = (bf16[2816,128]{1,0:T(8,128)(2,1)}, bf16[2816,128]{1,0:T(8,128)(2,1)S(1)}, u32[]{:S(2)}, u32[]{:S(2)}) collective-permute-start(bf16[2816,128]{1,0:T(8,128)(2,1)} %pad_maximum_fusion.6), channel_id=1, source_target_pairs={{0,1},{1,0},{2,3},{3,2},{4,5},{5,4},{6,7},{7,6},{8,9},{9,8},{10,11... | collective-permute-start | bytes 2162696 | tf_op jit(solution)/shard_map/ppermute | solution.py:617
  128.9 19.3 %collective-permute-start.34 = (bf16[192,1024]{1,0:T(8,128)(2,1)}, bf16[192,1024]{1,0:T(8,128)(2,1)S(1)}, u32[]{:S(2)}, u32[]{:S(2)}) collective-permute-start(bf16[192,1024]{1,0:T(8,128)(2,1)} %get-tuple-element.219.sa1.refs_3_), channel_id=1, source_target_pairs={{0,16},{8,24},{16,0},{24,8},{1,17},{9,25},{17,1},{25,9},{2,18},{10... | collective-permute-start | bytes 1179656 | tf_op jit(solution)/shard_map/ppermute | solution.py:602
  130.4 18.2 %collective-permute-start.37 = (bf16[384,1024]{1,0:T(8,128)(2,1)S(1)}, bf16[384,1024]{1,0:T(8,128)(2,1)S(1)}, u32[]{:S(2)}, u32[]{:S(2)}) collective-permute-start(bf16[384,1024]{1,0:T(8,128)(2,1)S(1)} %collective-permute-done.13.ga.refs_4_), channel_id=1, source_target_pairs={{0,8},{8,0},{16,24},{24,16},{1,9},{9,1},{17,25},{25,17},{2,10},{10... | collective-permute-start | bytes 2359304 | tf_op jit(solution)/shard_map/ppermute | solution.py:602
  177.0 23.2 %collective-permute-start.43 = (bf16[384,1024]{1,0:T(8,128)(2,1)S(1)}, bf16[384,1024]{1,0:T(8,128)(2,1)S(1)}, u32[]{:S(2)}, u32[]{:S(2)}) collective-permute-start(bf16[384,1024]{1,0:T(8,128)(2,1)S(1)} %add_convert_fusion.4), channel_id=1, source_target_pairs={{0,16},{8,24},{16,0},{24,8},{1,17},{9,25},{17,1},{25,9},{2,18},{10... | collective-permute-start | bytes 2359304 | tf_op jit(solution)/shard_map/ppermute | solution.py:602
  185.6 18.4 %collective-permute-start.44 = (bf16[4,704,128]{2,1,0:T(8,128)(2,1)}, bf16[4,704,128]{2,1,0:T(8,128)(2,1)S(1)}, u32[]{:S(2)}, u32[]{:S(2)}) collective-permute-start(bf16[4,704,128]{2,1,0:T(8,128)(2,1)} %get-tuple-element.246), channel_id=1, source_target_pairs={{0,1},{1,0},{2,3},{3,2},{4,5},{5,4},{6,7},{7,6},{8,9},{9,8},{10,11... | collective-permute-start | bytes 2162696 | tf_op jit(solution)/shard_map/ppermute | solution.py:617
  204.2 44.2 %collective-permute-start.50 = (bf16[4,704,128]{2,1,0:T(8,128)(2,1)}, bf16[4,704,128]{2,1,0:T(8,128)(2,1)}, u32[]{:S(2)}, u32[]{:S(2)}) collective-permute-start(bf16[4,704,128]{2,1,0:T(8,128)(2,1)} %get-tuple-element.270), channel_id=1, source_target_pairs={{0,1},{1,0},{2,3},{3,2},{4,5},{5,4},{6,7},{7,6},{8,9},{9,8},{10,11... | collective-permute-start | bytes 2162696 | tf_op jit(solution)/shard_map/ppermute | solution.py:617
  228.0 22.5 %collective-permute-start.51 = (bf16[704,128]{1,0:T(8,128)(2,1)S(1)}, bf16[704,128]{1,0:T(8,128)(2,1)S(1)}, u32[]{:S(2)}, u32[]{:S(2)}) collective-permute-start(bf16[704,128]{1,0:T(8,128)(2,1)S(1)} %get-tuple-element.358), channel_id=1, source_target_pairs={{0,2},{1,3},{2,0},{3,1},{4,6},{5,7},{6,4},{7,5},{8,10},{9,11},{10,... | collective-permute-start | bytes 540680 | tf_op jit(solution)/shard_map/ppermute | solution.py:617
  231.0 19.5 %collective-permute-start.52 = (bf16[704,128]{1,0:T(8,128)(2,1)S(1)}, bf16[704,128]{1,0:T(8,128)(2,1)S(1)}, u32[]{:S(2)}, u32[]{:S(2)}) collective-permute-start(bf16[704,128]{1,0:T(8,128)(2,1)S(1)} %get-tuple-element.357), channel_id=1, source_target_pairs={{0,4},{1,5},{2,6},{3,7},{4,0},{5,1},{6,2},{7,3},{8,12},{9,13},{10,... | collective-permute-start | bytes 540680 | tf_op jit(solution)/shard_map/ppermute | solution.py:617
  231.1 19.5 %collective-permute-start.53 = (bf16[704,128]{1,0:T(8,128)(2,1)S(1)}, bf16[704,128]{1,0:T(8,128)(2,1)S(1)}, u32[]{:S(2)}, u32[]{:S(2)}) collective-permute-start(bf16[704,128]{1,0:T(8,128)(2,1)S(1)} %get-tuple-element.356), channel_id=1, source_target_pairs={{0,6},{1,7},{2,4},{3,5},{4,2},{5,3},{6,0},{7,1},{8,14},{9,15},{10,... | collective-permute-start | bytes 540680 | tf_op jit(solution)/shard_map/ppermute | solution.py:617
  247.7 22.1 %collective-permute-start.49 = (bf16[384,1024]{1,0:T(8,128)(2,1)S(1)}, bf16[384,1024]{1,0:T(8,128)(2,1)S(1)}, u32[]{:S(2)}, u32[]{:S(2)}) collective-permute-start(bf16[384,1024]{1,0:T(8,128)(2,1)S(1)} %add_convert_fusion.3), channel_id=1, source_target_pairs={{0,16},{8,24},{16,0},{24,8},{1,17},{9,25},{17,1},{25,9},{2,18},{10... | collective-permute-start | bytes 2359304 | tf_op jit(solution)/shard_map/ppermute | solution.py:602
  249.7 20.1 %collective-permute-start.54 = (bf16[4,704,128]{2,1,0:T(8,128)(2,1)S(1)}, bf16[4,704,128]{2,1,0:T(8,128)(2,1)S(1)}, u32[]{:S(2)}, u32[]{:S(2)}) collective-permute-start(bf16[4,704,128]{2,1,0:T(8,128)(2,1)S(1)} %copy-done.72), channel_id=1, source_target_pairs={{0,1},{1,0},{2,3},{3,2},{4,5},{5,4},{6,7},{7,6},{8,9},{9,8},{10,11... | collective-permute-start | bytes 2162696 | tf_op jit(solution)/shard_map/ppermute | solution.py:617
  250.7 19.1 %collective-permute-start.55 = (bf16[704,128]{1,0:T(8,128)(2,1)S(1)}, bf16[704,128]{1,0:T(8,128)(2,1)S(1)}, u32[]{:S(2)}, u32[]{:S(2)}) collective-permute-start(bf16[704,128]{1,0:T(8,128)(2,1)S(1)} %get-tuple-element.354), channel_id=1, source_target_pairs={{0,2},{1,3},{2,0},{3,1},{4,6},{5,7},{6,4},{7,5},{8,10},{9,11},{10,... | collective-permute-start | bytes 540680 | tf_op jit(solution)/shard_map/ppermute | solution.py:617
  251.8 18.0 %collective-permute-start.56 = (bf16[704,128]{1,0:T(8,128)(2,1)S(1)}, bf16[704,128]{1,0:T(8,128)(2,1)S(1)}, u32[]{:S(2)}, u32[]{:S(2)}) collective-permute-start(bf16[704,128]{1,0:T(8,128)(2,1)S(1)} %get-tuple-element.353), channel_id=1, source_target_pairs={{0,4},{1,5},{2,6},{3,7},{4,0},{5,1},{6,2},{7,3},{8,12},{9,13},{10,... | collective-permute-start | bytes 540680 | tf_op jit(solution)/shard_map/ppermute | solution.py:617
  275.7 17.9 %collective-permute-start.64 = (bf16[4,520,128]{2,1,0:T(8,128)(2,1)S(1)}, bf16[4,520,128]{2,1,0:T(8,128)(2,1)S(1)}, u32[]{:S(2)}, u32[]{:S(2)}) collective-permute-start(bf16[4,520,128]{2,1,0:T(8,128)(2,1)S(1)} %copy-done.73), channel_id=1, source_target_pairs={{0,1},{1,0},{2,3},{3,2},{4,5},{5,4},{6,7},{7,6},{8,9},{9,8},{10,11... | collective-permute-start | bytes 1597448 | tf_op jit(solution)/shard_map/ppermute | solution.py:617
  281.9 20.5 %collective-permute-start.63 = (bf16[384,1024]{1,0:T(8,128)(2,1)S(1)}, bf16[384,1024]{1,0:T(8,128)(2,1)S(1)}, u32[]{:S(2)}, u32[]{:S(2)}) collective-permute-start(bf16[384,1024]{1,0:T(8,128)(2,1)S(1)} %add_convert_fusion.1), channel_id=1, source_target_pairs={{0,16},{8,24},{16,0},{24,8},{1,17},{9,25},{17,1},{25,9},{2,18},{10... | collective-permute-start | bytes 2359304 | tf_op jit(solution)/shard_map/ppermute | solution.py:602
  293.8 23.1 %collective-permute-start.65 = (bf16[4,776,128]{2,1,0:T(8,128)(2,1)}, bf16[4,776,128]{2,1,0:T(8,128)(2,1)S(1)}, u32[]{:S(2)}, u32[]{:S(2)}) collective-permute-start(bf16[4,776,128]{2,1,0:T(8,128)(2,1)} %get-tuple-element.312), channel_id=1, source_target_pairs={{0,1},{1,0},{2,3},{3,2},{4,5},{5,4},{6,7},{7,6},{8,9},{9,8},{10,11... | collective-permute-start | bytes 2383880 | tf_op jit(solution)/shard_map/ppermute | solution.py:617
  312.5 18.1 %all-to-all-start = ((bf16[4,384,256]{2,1,0:T(8,128)(2,1)}), bf16[4,384,256]{2,1,0:T(8,128)(2,1)S(1)}, u32[]{:S(2)}, u32[]{:S(2)}) async-start(bf16[4,384,256]{2,1,0:T(8,128)(2,1)} %get-tuple-element.307), calls=%async_computation | async-start | bytes 1572864 | tf_op jit(solution)/shard_map/all_to_all | solution.py:892
  319.3 17.2 %collective-permute-start.69 = (bf16[776,128]{1,0:T(8,128)(2,1)S(1)}, bf16[776,128]{1,0:T(8,128)(2,1)S(1)}, u32[]{:S(2)}, u32[]{:S(2)}) collective-permute-start(bf16[776,128]{1,0:T(8,128)(2,1)S(1)} %get-tuple-element.342), channel_id=1, source_target_pairs={{0,2},{1,3},{2,0},{3,1},{4,6},{5,7},{6,4},{7,5},{8,10},{9,11},{10,... | collective-permute-start | bytes 595976 | tf_op jit(solution)/shard_map/ppermute | solution.py:617
  319.5 17.2 %collective-permute-start.70 = (bf16[776,128]{1,0:T(8,128)(2,1)S(1)}, bf16[776,128]{1,0:T(8,128)(2,1)S(1)}, u32[]{:S(2)}, u32[]{:S(2)}) collective-permute-start(bf16[776,128]{1,0:T(8,128)(2,1)S(1)} %get-tuple-element.341), channel_id=1, source_target_pairs={{0,4},{1,5},{2,6},{3,7},{4,0},{5,1},{6,2},{7,3},{8,12},{9,13},{10,... | collective-permute-start | bytes 595976 | tf_op jit(solution)/shard_map/ppermute | solution.py:617
  (123 other events, 1237.3 us)

commit v4 on v3

--- a/solution.py
+++ b/solution.py
@@ -916,8 +916,8 @@
         cost(0, 1e6),
     )
     if ring:
-        qkv_share = add(*all_after(qkv_sent, out_grad, gate_grad, values_grad))
-    qkv_far = seq_permute(qkv_share, 2)
+        qkv_share = add(*all_after(qkv_sent, gate_grad, values_grad))
+    qkv_far = after(seq_permute(qkv_share, 2), out_grad)
     qkv_all = [qkv_share, seq_permute(qkv_share, 1), qkv_far, seq_permute(qkv_far, 1)]
     query_grad, key_grad, value_grad, gain_grad = vmem_call(
         place_qkv_kernel,

time: 354 us -> 352 us (level)
  waiting for transfers between devices: 60.1 us -> 55.1 us
    ppermute x41, waiting for transfers between devices: 31.1 us -> 25.2 us  [seq_permute(): return lax.ppermute(value, 'seq', [(i, i ^ flip) for i in range(GROUPS)])]
    unnamed x155 -> x157, local copies, waits for them, and re-layouts: 10.1 us -> 10.1 us
where the time goes in v4:
time: 352 us; the launch traced here: 346 us
  Pallas kernels  166 us (47%)
  starting transfers between devices  83.3 us (24%)
  waiting for transfers between devices  55.1 us (16%)
  local copies, waits for them, and re-layouts  21.7 us (6%)
  other arithmetic  18.3 us (5%)
    pallas_call x14, Pallas kernels, vmem_call(): pl.pallas_call(kernel, grid_spec=pltpu.PrefetchScalarGridSpec(num_scalar_...  73.6 us
    ppermute x39, starting transfers between devices, fsdp_permute(): return lax.ppermute(value, 'fsdp', [(i, i ^ flip) for i in range(n)])  58.2 us
    pallas_call x2, Pallas kernels, any_call(): pl.pallas_call(kernel, grid_spec=pltpu.PrefetchScalarGridSpec(num_scalar_...  34 us
    ppermute x39, waiting for transfers between devices, fsdp_permute(): return lax.ppermute(value, 'fsdp', [(i, i ^ flip) for i in range(n)])  29.9 us
    pallas_call x2, Pallas kernels, attention_back(): pl.pallas_call(attn_back_kernel, grid_spec=pltpu.PrefetchScalarGridSpec(n...  28.9 us
    ppermute x41, waiting for transfers between devices, seq_permute(): return lax.ppermute(value, 'seq', [(i, i ^ flip) for i in range(GROUPS)])  25.2 us
    ppermute x41, starting transfers between devices, seq_permute(): return lax.ppermute(value, 'seq', [(i, i ^ flip) for i in range(GROUPS)])  21.6 us
    pallas_call x2, Pallas kernels, attention(): pl.pallas_call(attn_kernel, grid_spec=pltpu.PrefetchScalarGridSpec(num_sc...  17.8 us
  transfers between devices with their start and end apart: 81, of which 21 were waited for; matrix products, arithmetic and copies ran while one was open for 6% of the time, Pallas kernels for 39%

profile of v4, /device:TPU:0, one launch (start us, length us, event | category | flops | bytes accessed | tf_op | source)
XLA Modules:
  0.0 345.8 jit_solution(18016454146426834176)
XLA Ops:
  4.0 3.9 %concatenate.30.refs_0_ = bf16[1288,128]{1,0:T(8,128)(2,1)} concatenate(bf16[256,128]{1,0:T(8,128)(2,1)S(1)} %bitcast.107, bf16[256,128]{1,0:T(8,128)(2,1)S(1)} %bitcast.105, bf16[256,128]{1,0:T(8,128)(2,1)S(1)} %bitcast.106, bf16[1,128]{1,0:T(2,128)(2,1)} %bitcast.108, bf16[1,128]{1,0:T(2,128)(2,1)} %bitcast.109, bf16[6,128]{1,0:T(8,128)(2,1)S(1)} %broadcast_in_dim.26, ...), dimensions={0} | concatenate | bytes 659456 | tf_op jit(solution)/shard_map/concatenate | solution.py:665
  7.8 3.0 collective-permute-start.3
  21.6 4.3 %fusion = (f32[4,384,128]{2,1,0:T(8,128)}, f32[4,384,128]{2,1,0:T(8,128)}) fusion(f32[128]{0:T(128)S(1)} %mul.78, f32[128]{0:T(128)S(1)} %mul.75, f32[4,384]{1,0:T(4,128)S(1)} %add_convert_fusion.15), kind=kLoop, calls=%fused_computation.14 | loop fusion | flops 393216 | bytes 1580032 | tf_op jit(solution)/shard_map/mul | solution.py:672
  26.6 11.8 %collective-permute-done.5.refs_4_ = bf16[1288,128]{1,0:T(8,128)(2,1)} collective-permute-done((bf16[1288,128]{1,0:T(8,128)(2,1)}, bf16[1288,128]{1,0:T(8,128)(2,1)}, u32[]{:S(2)}, u32[]{:S(2)}) %collective-permute-start.5) | collective-permute-done | bytes 329760 | tf_op jit(solution)/shard_map/ppermute | solution.py:617
  42.4 5.5 %collective-permute-start.10 = (bf16[704,128]{1,0:T(8,128)(2,1)S(1)}, bf16[704,128]{1,0:T(8,128)(2,1)S(1)}, u32[]{:S(2)}, u32[]{:S(2)}) collective-permute-start(bf16[704,128]{1,0:T(8,128)(2,1)S(1)} %bitcast.96), channel_id=1, source_target_pairs={{0,4},{1,5},{2,6},{3,7},{4,0},{5,1},{6,2},{7,3},{8,12},{9,13},{10,... | collective-permute-start | bytes 540680 | tf_op jit(solution)/shard_map/ppermute | solution.py:617
  50.6 9.1 %collective-permute-done.10.refs_2_ = bf16[704,128]{1,0:T(8,128)(2,1)S(1)} collective-permute-done((bf16[704,128]{1,0:T(8,128)(2,1)S(1)}, bf16[704,128]{1,0:T(8,128)(2,1)S(1)}, u32[]{:S(2)}, u32[]{:S(2)}) %collective-permute-start.10) | collective-permute-done | bytes 180256 | tf_op jit(solution)/shard_map/ppermute | solution.py:617
  59.9 3.1 collective-permute-start.15
  68.6 11.3 %qkv.1 = (bf16[4,384,256]{2,1,0:T(8,128)(2,1)}, bf16[4,384,256]{2,1,0:T(8,128)(2,1)}, bf16[4,384,256]{2,1,0:T(8,128)(2,1)}, bf16[4,384,1024]{2,1,0:T(8,128)(2,1)...) custom-call(s32[1]{0:T(128)} %bitcast.1.me, bf16[384,1024]{1,0:T(8,128)(2,1)} %bitcast.70, ...), custom_call_target="tpu_custom_call" | custom-call | flops 1 | bytes 1 | tf_op jit(solution)/shard_map/qkv/pallas_call | solution.py:99
  80.0 8.4 %attention.2 = (bf16[384,128]{1,0:T(8,128)(2,1)}, bf16[384,128]{1,0:T(8,128)(2,1)}, bf16[384,128]{1,0:T(8,128)(2,1)}, bf16[384,128]{1,0:T(8,128)(2,1)}, f32[2,4,8,384]{3,2,1,0:T(8,128)}) custom-call(s32[1]{0:T(128)} %bitcast.me, bf16[4,384,256]{2,1,0:T(8,128)(2,1)} %get-tuple-element.278.q, bf16[4,384,256]{2,1,0:T(8,128)(2,1)} %get-tuple-element.180.k, ...), custom_call_target="tpu_custom_call" | custom-call | flops 1 | bytes 1 | tf_op jit(solution)/shard_map/attention/pallas_call | solution.py:167
  93.6 9.3 %attention.3 = (bf16[384,256]{1,0:T(8,128)(2,1)}, bf16[384,256]{1,0:T(8,128)(2,1)}, bf16[384,256]{1,0:T(8,128)(2,1)}, bf16[384,256]{1,0:T(8,128)(2,1)}, f32[2,4,8,384]{3,2,1,0:T(8,128)}) custom-call(s32[1]{0:T(128)} %bitcast.me, bf16[4,384,256]{2,1,0:T(8,128)(2,1)} %get-tuple-element.278.q, bf16[4,384,256]{2,1,0:T(8,128)(2,1)} %get-tuple-element.180.k, ...), custom_call_target="tpu_custom_call" | custom-call | flops 1 | bytes 1 | tf_op jit(solution)/shard_map/attention/pallas_call | solution.py:167
  109.6 4.2 %collective-permute-done.20.m2 = bf16[384,256]{1,0:T(8,128)(2,1)S(1)} collective-permute-done((bf16[384,256]{1,0:T(8,128)(2,1)}, bf16[384,256]{1,0:T(8,128)(2,1)S(1)}, u32[]{:S(2)}, u32[]{:S(2)}) %collective-permute-start.20) | collective-permute-done | bytes 196640 | tf_op jit(solution)/shard_map/ppermute | solution.py:602
  113.8 3.4 collective-permute-done.21.m3
  122.4 5.5 %out.1 = (f32[384,1024]{1,0:T(8,128)}, bf16[192,1024]{1,0:T(8,128)(2,1)}, bf16[192,1024]{1,0:T(8,128)(2,1)}) custom-call(s32[1]{0:T(128)} %bitcast.me, bf16[384,256]{1,0:T(8,128)(2,1)} %get-tuple-element.213.m0, bf16[384,256]{1,0:T(8,128)(2,1)} %copy-done.28, bf16[384,256]{1,0:T(8,128)(2,1)} %copy-done.30, bf16[384,256]{1,0:T(8,128)(2,1)} %copy-done.32, ...), custom_call_target="tpu_custom_call" | custom-call | flops 1 | bytes 1 | tf_op jit(solution)/shard_map/out/pallas_call | solution.py:293
  132.1 12.7 %mlp.2 = (bf16[768,704]{1,0:T(8,128)(2,1)}, bf16[768,704]{1,0:T(8,128)(2,1)}, bf16[768,704]{1,0:T(8,128)(2,1)}, bf16[384,1024]{1,0:T(8,128)(2,1)}, bf16[384,1024]{1,0:T(8,128)(2,1)}) custom-call(s32[1]{0:T(128)} %bitcast.1.me, bf16[192,1024]{1,0:T(8,128)(2,1)} %get-tuple-element.219.sa0.refs_2_, bf16[192,1024]{1,0:T(8,128)(2,1)} %get-tuple-element.220.sa1.refs_3_, ...), custom_call_target="tpu_custom_call" | custom-call | flops 1 | bytes 1 | tf_op jit(solution)/shard_map/mlp/pallas_call | solution.py:377
  144.8 3.3 collective-permute-done.34.sa1.refs_7_
  151.4 21.4 %mlp.3 = (bf16[768,704]{1,0:T(8,128)(2,1)}, bf16[768,704]{1,0:T(8,128)(2,1)}, bf16[768,704]{1,0:T(8,128)(2,1)}, bf16[384,1024]{1,0:T(8,128)(2,1)}, bf16[384,1024]{1,0:T(8,128)(2,1)}) custom-call(s32[1]{0:T(128)} %bitcast.1.me, bf16[192,1024]{1,0:T(8,128)(2,1)} %copy-done.11, bf16[192,1024]{1,0:T(8,128)(2,1)} %copy-done.12, bf16[192,1024]{1,0:T(8,128)(2,1)} %copy-done.13, ...), custom_call_target="tpu_custom_call" | custom-call | flops 1 | bytes 1 | tf_op jit(solution)/shard_map/mlp/pallas_call | solution.py:377
  179.3 6.4 %unit_grads.3 = (bf16[4,704,128]{2,1,0:T(8,128)(2,1)}, bf16[4,704,128]{2,1,0:T(8,128)(2,1)}) custom-call(s32[1]{0:T(128)} %bitcast.1.me, bf16[768,704]{1,0:T(8,128)(2,1)} %get-tuple-element.222.refs_0_.hn, bf16[768,704]{1,0:T(8,128)(2,1)} %get-tuple-element.233.refs_1_.hf, bf16[384,1024]{1,0:T(8,128)(2,1)} %bitcast.78, bf16[384,1024]{1,0:T(8,128)(2,1)} %copy-done.17, ...), custom_call_target="tpu_custom_call" | custom-call | flops 1 | bytes 1 | tf_op jit(solution)/shard_map/unit_grads/pallas_call | solution.py:293
  186.6 6.1 %mlp_out.1 = (bf16[384,1024]{1,0:T(8,128)(2,1)}, bf16[384,1024]{1,0:T(8,128)(2,1)}, bf16[384,1024]{1,0:T(8,128)(2,1)}, bf16[384,1024]{1,0:T(8,128)(2,1)}) custom-call(s32[1]{0:T(128)} %bitcast.1.me, bf16[768,704]{1,0:T(8,128)(2,1)} %get-tuple-element.222.refs_0_.hn, bf16[768,704]{1,0:T(8,128)(2,1)} %get-tuple-element.233.refs_1_.hf, ...), custom_call_target="tpu_custom_call" | custom-call | flops 1 | bytes 1 | tf_op jit(solution)/shard_map/mlp_out/pallas_call | solution.py:293
  193.3 6.9 %unit_grads.4 = (bf16[4,704,128]{2,1,0:T(8,128)(2,1)}, bf16[4,704,128]{2,1,0:T(8,128)(2,1)}) custom-call(s32[1]{0:T(128)} %bitcast.1.me, bf16[768,704]{1,0:T(8,128)(2,1)} %get-tuple-element.237.refs_0_, bf16[768,704]{1,0:T(8,128)(2,1)} %get-tuple-element.239.refs_1_, bf16[192,1024]{1,0:T(8,128)(2,1)} %get-tuple-element.219.sa0.refs_2_, ...), custom_call_target="tpu_custom_call" | custom-call | flops 1 | bytes 1 | tf_op jit(solution)/shard_map/unit_grads/pallas_call | solution.py:293
  206.1 5.9 %middle.1 = (f32[384,1024]{1,0:T(8,128)}, bf16[384,1024]{1,0:T(8,128)(2,1)}, bf16[384,512]{1,0:T(8,128)(2,1)}, bf16[384,256]{1,0:T(8,128)(2,1)}, bf16[384,256]{1...) custom-call(s32[1]{0:T(128)} %bitcast.me, ...), custom_call_target="tpu_custom_call" | custom-call | flops 1 | bytes 1 | tf_op jit(solution)/shard_map/middle/pallas_call | solution.py:293
  216.6 4.9 %out_grad.1 = (bf16[4,520,128]{2,1,0:T(8,128)(2,1)}, bf16[4,520,128]{2,1,0:T(8,128)(2,1)}) custom-call(s32[3]{0:T(128)} %pad_add_fusion.me, bf16[384,256]{1,0:T(8,128)(2,1)} %get-tuple-element.213.m0, bf16[384,256]{1,0:T(8,128)(2,1)} %copy-done.28, bf16[384,256]{1,0:T(8,128)(2,1)} %copy-done.30, bf16[384,256]{1,0:T(8,128)(2,1)} %copy-done.32, ...), custom_call_target="tpu_custom_call" | custom-call | flops 1 | bytes 1 | tf_op jit(solution)/shard_map/out_grad/pallas_call | solution.py:293
  221.6 6.3 %unit_grads.5 = (bf16[4,704,128]{2,1,0:T(8,128)(2,1)}, bf16[4,704,128]{2,1,0:T(8,128)(2,1)}) custom-call(s32[1]{0:T(128)} %bitcast.1.me, bf16[768,704]{1,0:T(8,128)(2,1)} %get-tuple-element.256.refs_0_, bf16[768,704]{1,0:T(8,128)(2,1)} %get-tuple-element.261.refs_1_, bf16[192,1024]{1,0:T(8,128)(2,1)} %get-tuple-element.219.sa0.refs_2_, ...), custom_call_target="tpu_custom_call" | custom-call | flops 1 | bytes 1 | tf_op jit(solution)/shard_map/unit_grads/pallas_call | solution.py:293
  228.0 3.0 collective-permute-start.51
  233.5 14.2 %attention_back.2 = (bf16[4,384,384]{2,1,0:T(8,128)(2,1)}, bf16[4,384,128]{2,1,0:T(8,128)(2,1)}) custom-call(s32[1]{0:T(128)} %bitcast.me, bf16[4,384,256]{2,1,0:T(8,128)(2,1)} %get-tuple-element.278.q, bf16[4,384,256]{2,1,0:T(8,128)(2,1)} %get-tuple-element.180.k, bf16[4,384,256]{2,1,0:T(8,128)(2,1)} %get-tuple-element.181.v, ...), custom_call_target="tpu_custom_call" | custom-call | flops 1 | bytes 1 | tf_op jit(solution)/shard_map/attention_back/pallas_call | solution.py:245
  255.2 14.6 %attention_back.3 = (bf16[4,384,384]{2,1,0:T(8,128)(2,1)}, bf16[4,384,256]{2,1,0:T(8,128)(2,1)}) custom-call(s32[1]{0:T(128)} %bitcast.me, bf16[4,384,256]{2,1,0:T(8,128)(2,1)} %get-tuple-element.278.q, bf16[4,384,256]{2,1,0:T(8,128)(2,1)} %get-tuple-element.180.k, bf16[4,384,256]{2,1,0:T(8,128)(2,1)} %get-tuple-element.181.v, ...), custom_call_target="tpu_custom_call" | custom-call | flops 1 | bytes 1 | tf_op jit(solution)/shard_map/attention_back/pallas_call | solution.py:245
  270.2 5.1 %normed_back.1 = (bf16[384,1024]{1,0:T(8,128)(2,1)}, bf16[384,1024]{1,0:T(8,128)(2,1)}, bf16[384,1024]{1,0:T(8,128)(2,1)}) custom-call(s32[1]{0:T(128)} %bitcast.me, bf16[4,384,384]{2,1,0:T(8,128)(2,1)} %get-tuple-element.267.da, bf16[4,384,384]{2,1,0:T(8,128)(2,1)} %get-tuple-element.298.db, bf16[776,1024]{1,0:T(8,128)(2,1)} %get-tuple-element.217.w), custom_call_target="tpu_custom_call" | custom-call | flops 1 | bytes 1 | tf_op jit(solution)/shard_map/normed_back/pallas_call | solution.py:293
  283.3 8.5 %qkv_grad.1 = (bf16[4,776,128]{2,1,0:T(8,128)(2,1)}, bf16[4,776,128]{2,1,0:T(8,128)(2,1)}) custom-call(s32[3]{0:T(128)} %pad_add_fusion.me, bf16[1536,1024]{1,0:T(8,128)(2,1)} %bitcast.89, bf16[1536,384]{1,0:T(8,128)(2,1)} %bitcast.75, bf16[1536,384]{1,0:T(8,128)(2,1)} %bitcast.76, bf16[776,1024]{1,0:T(8,128)(2,1)} %get-tuple-element.217.w), custom_call_target="tpu_custom_call" | custom-call | flops 1 | bytes 1 | tf_op jit(solution)/shard_map/qkv_grad/pallas_call | solution.py:293
  296.0 3.0 collective-permute-start.66
  299.0 3.4 collective-permute-done.63.p2
  305.3 5.7 %final.1 = f32[384,1024]{1,0:T(8,128)} custom-call(s32[1]{0:T(128)} %bitcast.me, bf16[384,1024]{1,0:T(8,128)(2,1)} %copy-done.51, bf16[384,1024]{1,0:T(8,128)(2,1)} %copy-done.52, bf16[4,384,384]{2,1,0:T(8,128)(2,1)} %get-tuple-element.267.da, bf16[4,384,384]{2,1,0:T(8,128)(2,1)} %get-tuple-element.298.db, bf16[776,1024]{1,0:T(8,128)(2,1)} %get-tuple-element.217.w, ...), custom_call_target="tpu_custom_call" | custom-call | flops 1 | bytes 1 | tf_op jit(solution)/shard_map/final/pallas_call | solution.py:293
  312.0 3.5 %all-to-all-start = ((bf16[4,384,256]{2,1,0:T(8,128)(2,1)}), bf16[4,384,256]{2,1,0:T(8,128)(2,1)S(1)}, u32[]{:S(2)}, u32[]{:S(2)}) async-start(bf16[4,384,256]{2,1,0:T(8,128)(2,1)} %get-tuple-element.308), calls=%async_computation | async-start | bytes 1572864 | tf_op jit(solution)/shard_map/all_to_all | solution.py:892
  323.3 5.4 %place_units.1 = (f32[128,2816]{1,0:T(8,128)}, f32[128,2816]{1,0:T(8,128)}, f32[128,2816]{1,0:T(8,128)}) custom-call(s32[1]{0:T(128)} %bitcast.me, bf16[2112,128]{1,0:T(8,128)(2,1)} %copy-done.26, bf16[2112,128]{1,0:T(8,128)(2,1)} %collective-permute-done.72.p1, bf16[2112,128]{1,0:T(8,128)(2,1)} %collective-permute-done.73.p2, ...), custom_call_target="tpu_custom_call" | custom-call | flops 1 | bytes 1 | tf_op jit(solution)/shard_map/place_units/pallas_call | solution.py:293
  (359 shorter events, 120.9 us)
Async XLA Ops:
  7.8 18.1 %collective-permute-start.3 = (bf16[1288,128]{1,0:T(8,128)(2,1)}, bf16[1288,128]{1,0:T(8,128)(2,1)}, u32[]{:S(2)}, u32[]{:S(2)}) collective-permute-start(bf16[1288,128]{1,0:T(8,128)(2,1)} %concatenate.30.refs_0_), channel_id=1, source_target_pairs={{0,2},{1,3},{2,0},{3,1},{4,6},{5,7},{6,4},{7,5},{8,10},{9,11},{10,... | collective-permute-start | bytes 989192 | tf_op jit(solution)/shard_map/ppermute | solution.py:617
  10.9 31.5 %collective-permute-start.2 = (bf16[1288,128]{1,0:T(8,128)(2,1)}, bf16[1288,128]{1,0:T(8,128)(2,1)}, u32[]{:S(2)}, u32[]{:S(2)}) collective-permute-start(bf16[1288,128]{1,0:T(8,128)(2,1)} %concatenate.30.refs_0_), channel_id=1, source_target_pairs={{0,1},{1,0},{2,3},{3,2},{4,5},{5,4},{6,7},{7,6},{8,9},{9,8},{10,11... | collective-permute-start | bytes 989192 | tf_op jit(solution)/shard_map/ppermute | solution.py:617
  12.4 26.0 %collective-permute-start.5 = (bf16[1288,128]{1,0:T(8,128)(2,1)}, bf16[1288,128]{1,0:T(8,128)(2,1)}, u32[]{:S(2)}, u32[]{:S(2)}) collective-permute-start(bf16[1288,128]{1,0:T(8,128)(2,1)} %concatenate.30.refs_0_), channel_id=1, source_target_pairs={{0,4},{1,5},{2,6},{3,7},{4,0},{5,1},{6,2},{7,3},{8,12},{9,13},{10,... | collective-permute-start | bytes 989192 | tf_op jit(solution)/shard_map/ppermute | solution.py:617
  15.0 24.0 %collective-permute-start.7 = (bf16[1288,128]{1,0:T(8,128)(2,1)}, bf16[1288,128]{1,0:T(8,128)(2,1)}, u32[]{:S(2)}, u32[]{:S(2)}) collective-permute-start(bf16[1288,128]{1,0:T(8,128)(2,1)} %concatenate.30.refs_0_), channel_id=1, source_target_pairs={{0,6},{1,7},{2,4},{3,5},{4,2},{5,3},{6,0},{7,1},{8,14},{9,15},{10,... | collective-permute-start | bytes 989192 | tf_op jit(solution)/shard_map/ppermute | solution.py:617
  17.1 32.1 %collective-permute-start.1 = (bf16[384,1536]{1,0:T(8,128)(2,1)}, bf16[384,1536]{1,0:T(8,128)(2,1)S(1)}, u32[]{:S(2)}, u32[]{:S(2)}) collective-permute-start(bf16[384,1536]{1,0:T(8,128)(2,1)} %pad_maximum_fusion), channel_id=1, source_target_pairs={{0,16},{8,24},{16,0},{24,8},{1,17},{9,25},{17,1},{25,9},{2,18},{10... | collective-permute-start | bytes 3538952 | tf_op jit(solution)/shard_map/ppermute | solution.py:602
  42.4 17.3 %collective-permute-start.10 = (bf16[704,128]{1,0:T(8,128)(2,1)S(1)}, bf16[704,128]{1,0:T(8,128)(2,1)S(1)}, u32[]{:S(2)}, u32[]{:S(2)}) collective-permute-start(bf16[704,128]{1,0:T(8,128)(2,1)S(1)} %bitcast.96), channel_id=1, source_target_pairs={{0,4},{1,5},{2,6},{3,7},{4,0},{5,1},{6,2},{7,3},{8,12},{9,13},{10,... | collective-permute-start | bytes 540680 | tf_op jit(solution)/shard_map/ppermute | solution.py:617
  59.9 28.5 %collective-permute-start.15 = (bf16[704,128]{1,0:T(8,128)(2,1)S(1)}, bf16[704,128]{1,0:T(8,128)(2,1)S(1)}, u32[]{:S(2)}, u32[]{:S(2)}) collective-permute-start(bf16[704,128]{1,0:T(8,128)(2,1)S(1)} %bitcast.90), channel_id=1, source_target_pairs={{0,2},{1,3},{2,0},{3,1},{4,6},{5,7},{6,4},{7,5},{8,10},{9,11},{10,... | collective-permute-start | bytes 540680 | tf_op jit(solution)/shard_map/ppermute | solution.py:617
  63.0 25.4 %collective-permute-start.16 = (bf16[704,128]{1,0:T(8,128)(2,1)S(1)}, bf16[704,128]{1,0:T(8,128)(2,1)S(1)}, u32[]{:S(2)}, u32[]{:S(2)}) collective-permute-start(bf16[704,128]{1,0:T(8,128)(2,1)S(1)} %bitcast.91), channel_id=1, source_target_pairs={{0,4},{1,5},{2,6},{3,7},{4,0},{5,1},{6,2},{7,3},{8,12},{9,13},{10,... | collective-permute-start | bytes 540680 | tf_op jit(solution)/shard_map/ppermute | solution.py:617
  63.0 25.5 %collective-permute-start.17 = (bf16[704,128]{1,0:T(8,128)(2,1)S(1)}, bf16[704,128]{1,0:T(8,128)(2,1)S(1)}, u32[]{:S(2)}, u32[]{:S(2)}) collective-permute-start(bf16[704,128]{1,0:T(8,128)(2,1)S(1)} %bitcast.92), channel_id=1, source_target_pairs={{0,6},{1,7},{2,4},{3,5},{4,2},{5,3},{6,0},{7,1},{8,14},{9,15},{10,... | collective-permute-start | bytes 540680 | tf_op jit(solution)/shard_map/ppermute | solution.py:617
  65.5 28.0 %collective-permute-start.14 = (bf16[2816,128]{1,0:T(8,128)(2,1)S(1)}, bf16[2816,128]{1,0:T(8,128)(2,1)S(1)}, u32[]{:S(2)}, u32[]{:S(2)}) collective-permute-start(bf16[2816,128]{1,0:T(8,128)(2,1)S(1)} %pad_maximum_fusion.4), channel_id=1, source_target_pairs={{0,1},{1,0},{2,3},{3,2},{4,5},{5,4},{6,7},{7,6},{8,9},{9,8},{10,11... | collective-permute-start | bytes 2162696 | tf_op jit(solution)/shard_map/ppermute | solution.py:617
  67.1 24.0 %collective-permute-start.13 = (bf16[384,1024]{1,0:T(8,128)(2,1)S(1)}, bf16[384,1024]{1,0:T(8,128)(2,1)S(1)}, u32[]{:S(2)}, u32[]{:S(2)}) collective-permute-start(bf16[384,1024]{1,0:T(8,128)(2,1)S(1)} %bitcast.80), channel_id=1, source_target_pairs={{0,16},{8,24},{16,0},{24,8},{1,17},{9,25},{17,1},{25,9},{2,18},{10... | collective-permute-start | bytes 2359304 | tf_op jit(solution)/shard_map/ppermute | solution.py:602
  88.6 17.3 %collective-permute-start.18 = (bf16[2816,128]{1,0:T(8,128)(2,1)S(1)}, bf16[2816,128]{1,0:T(8,128)(2,1)S(1)}, u32[]{:S(2)}, u32[]{:S(2)}) collective-permute-start(bf16[2816,128]{1,0:T(8,128)(2,1)S(1)} %pad_maximum_fusion.5), channel_id=1, source_target_pairs={{0,1},{1,0},{2,3},{3,2},{4,5},{5,4},{6,7},{7,6},{8,9},{9,8},{10,11... | collective-permute-start | bytes 2162696 | tf_op jit(solution)/shard_map/ppermute | solution.py:617
  93.6 35.3 %collective-permute-start.31 = (bf16[384,1024]{1,0:T(8,128)(2,1)S(1)}, bf16[384,1024]{1,0:T(8,128)(2,1)S(1)}, u32[]{:S(2)}, u32[]{:S(2)}) collective-permute-start(bf16[384,1024]{1,0:T(8,128)(2,1)S(1)} %bitcast.81), channel_id=1, source_target_pairs={{0,8},{8,0},{16,24},{24,16},{1,9},{9,1},{17,25},{25,17},{2,10},{10... | collective-permute-start | bytes 2359304 | tf_op jit(solution)/shard_map/ppermute | solution.py:602
  108.7 21.7 %collective-permute-start.32 = (bf16[2816,128]{1,0:T(8,128)(2,1)}, bf16[2816,128]{1,0:T(8,128)(2,1)S(1)}, u32[]{:S(2)}, u32[]{:S(2)}) collective-permute-start(bf16[2816,128]{1,0:T(8,128)(2,1)} %pad_maximum_fusion.6), channel_id=1, source_target_pairs={{0,1},{1,0},{2,3},{3,2},{4,5},{5,4},{6,7},{7,6},{8,9},{9,8},{10,11... | collective-permute-start | bytes 2162696 | tf_op jit(solution)/shard_map/ppermute | solution.py:617
  128.9 19.3 %collective-permute-start.34 = (bf16[192,1024]{1,0:T(8,128)(2,1)}, bf16[192,1024]{1,0:T(8,128)(2,1)S(1)}, u32[]{:S(2)}, u32[]{:S(2)}) collective-permute-start(bf16[192,1024]{1,0:T(8,128)(2,1)} %get-tuple-element.220.sa1.refs_3_), channel_id=1, source_target_pairs={{0,16},{8,24},{16,0},{24,8},{1,17},{9,25},{17,1},{25,9},{2,18},{10... | collective-permute-start | bytes 1179656 | tf_op jit(solution)/shard_map/ppermute | solution.py:602
  130.4 18.2 %collective-permute-start.37 = (bf16[384,1024]{1,0:T(8,128)(2,1)S(1)}, bf16[384,1024]{1,0:T(8,128)(2,1)S(1)}, u32[]{:S(2)}, u32[]{:S(2)}) collective-permute-start(bf16[384,1024]{1,0:T(8,128)(2,1)S(1)} %collective-permute-done.13.ga.refs_4_), channel_id=1, source_target_pairs={{0,8},{8,0},{16,24},{24,16},{1,9},{9,1},{17,25},{25,17},{2,10},{10... | collective-permute-start | bytes 2359304 | tf_op jit(solution)/shard_map/ppermute | solution.py:602
  177.0 23.2 %collective-permute-start.43 = (bf16[384,1024]{1,0:T(8,128)(2,1)S(1)}, bf16[384,1024]{1,0:T(8,128)(2,1)S(1)}, u32[]{:S(2)}, u32[]{:S(2)}) collective-permute-start(bf16[384,1024]{1,0:T(8,128)(2,1)S(1)} %add_convert_fusion.4), channel_id=1, source_target_pairs={{0,16},{8,24},{16,0},{24,8},{1,17},{9,25},{17,1},{25,9},{2,18},{10... | collective-permute-start | bytes 2359304 | tf_op jit(solution)/shard_map/ppermute | solution.py:602
  185.6 18.4 %collective-permute-start.44 = (bf16[4,704,128]{2,1,0:T(8,128)(2,1)}, bf16[4,704,128]{2,1,0:T(8,128)(2,1)S(1)}, u32[]{:S(2)}, u32[]{:S(2)}) collective-permute-start(bf16[4,704,128]{2,1,0:T(8,128)(2,1)} %get-tuple-element.247), channel_id=1, source_target_pairs={{0,1},{1,0},{2,3},{3,2},{4,5},{5,4},{6,7},{7,6},{8,9},{9,8},{10,11... | collective-permute-start | bytes 2162696 | tf_op jit(solution)/shard_map/ppermute | solution.py:617
  204.2 44.2 %collective-permute-start.50 = (bf16[4,704,128]{2,1,0:T(8,128)(2,1)}, bf16[4,704,128]{2,1,0:T(8,128)(2,1)}, u32[]{:S(2)}, u32[]{:S(2)}) collective-permute-start(bf16[4,704,128]{2,1,0:T(8,128)(2,1)} %get-tuple-element.271), channel_id=1, source_target_pairs={{0,1},{1,0},{2,3},{3,2},{4,5},{5,4},{6,7},{7,6},{8,9},{9,8},{10,11... | collective-permute-start | bytes 2162696 | tf_op jit(solution)/shard_map/ppermute | solution.py:617
  228.0 22.5 %collective-permute-start.51 = (bf16[704,128]{1,0:T(8,128)(2,1)S(1)}, bf16[704,128]{1,0:T(8,128)(2,1)S(1)}, u32[]{:S(2)}, u32[]{:S(2)}) collective-permute-start(bf16[704,128]{1,0:T(8,128)(2,1)S(1)} %get-tuple-element.360), channel_id=1, source_target_pairs={{0,2},{1,3},{2,0},{3,1},{4,6},{5,7},{6,4},{7,5},{8,10},{9,11},{10,... | collective-permute-start | bytes 540680 | tf_op jit(solution)/shard_map/ppermute | solution.py:617
  231.0 19.5 %collective-permute-start.52 = (bf16[704,128]{1,0:T(8,128)(2,1)S(1)}, bf16[704,128]{1,0:T(8,128)(2,1)S(1)}, u32[]{:S(2)}, u32[]{:S(2)}) collective-permute-start(bf16[704,128]{1,0:T(8,128)(2,1)S(1)} %get-tuple-element.359), channel_id=1, source_target_pairs={{0,4},{1,5},{2,6},{3,7},{4,0},{5,1},{6,2},{7,3},{8,12},{9,13},{10,... | collective-permute-start | bytes 540680 | tf_op jit(solution)/shard_map/ppermute | solution.py:617
  231.1 19.5 %collective-permute-start.53 = (bf16[704,128]{1,0:T(8,128)(2,1)S(1)}, bf16[704,128]{1,0:T(8,128)(2,1)S(1)}, u32[]{:S(2)}, u32[]{:S(2)}) collective-permute-start(bf16[704,128]{1,0:T(8,128)(2,1)S(1)} %get-tuple-element.358), channel_id=1, source_target_pairs={{0,6},{1,7},{2,4},{3,5},{4,2},{5,3},{6,0},{7,1},{8,14},{9,15},{10,... | collective-permute-start | bytes 540680 | tf_op jit(solution)/shard_map/ppermute | solution.py:617
  247.7 22.1 %collective-permute-start.49 = (bf16[384,1024]{1,0:T(8,128)(2,1)S(1)}, bf16[384,1024]{1,0:T(8,128)(2,1)S(1)}, u32[]{:S(2)}, u32[]{:S(2)}) collective-permute-start(bf16[384,1024]{1,0:T(8,128)(2,1)S(1)} %add_convert_fusion.3), channel_id=1, source_target_pairs={{0,16},{8,24},{16,0},{24,8},{1,17},{9,25},{17,1},{25,9},{2,18},{10... | collective-permute-start | bytes 2359304 | tf_op jit(solution)/shard_map/ppermute | solution.py:602
  249.7 20.1 %collective-permute-start.54 = (bf16[4,704,128]{2,1,0:T(8,128)(2,1)S(1)}, bf16[4,704,128]{2,1,0:T(8,128)(2,1)S(1)}, u32[]{:S(2)}, u32[]{:S(2)}) collective-permute-start(bf16[4,704,128]{2,1,0:T(8,128)(2,1)S(1)} %copy-done.73), channel_id=1, source_target_pairs={{0,1},{1,0},{2,3},{3,2},{4,5},{5,4},{6,7},{7,6},{8,9},{9,8},{10,11... | collective-permute-start | bytes 2162696 | tf_op jit(solution)/shard_map/ppermute | solution.py:617
  250.7 19.1 %collective-permute-start.55 = (bf16[704,128]{1,0:T(8,128)(2,1)S(1)}, bf16[704,128]{1,0:T(8,128)(2,1)S(1)}, u32[]{:S(2)}, u32[]{:S(2)}) collective-permute-start(bf16[704,128]{1,0:T(8,128)(2,1)S(1)} %get-tuple-element.356), channel_id=1, source_target_pairs={{0,2},{1,3},{2,0},{3,1},{4,6},{5,7},{6,4},{7,5},{8,10},{9,11},{10,... | collective-permute-start | bytes 540680 | tf_op jit(solution)/shard_map/ppermute | solution.py:617
  251.8 18.0 %collective-permute-start.56 = (bf16[704,128]{1,0:T(8,128)(2,1)S(1)}, bf16[704,128]{1,0:T(8,128)(2,1)S(1)}, u32[]{:S(2)}, u32[]{:S(2)}) collective-permute-start(bf16[704,128]{1,0:T(8,128)(2,1)S(1)} %get-tuple-element.355), channel_id=1, source_target_pairs={{0,4},{1,5},{2,6},{3,7},{4,0},{5,1},{6,2},{7,3},{8,12},{9,13},{10,... | collective-permute-start | bytes 540680 | tf_op jit(solution)/shard_map/ppermute | solution.py:617
  252.8 17.0 %collective-permute-start.57 = (bf16[704,128]{1,0:T(8,128)(2,1)S(1)}, bf16[704,128]{1,0:T(8,128)(2,1)S(1)}, u32[]{:S(2)}, u32[]{:S(2)}) collective-permute-start(bf16[704,128]{1,0:T(8,128)(2,1)S(1)} %get-tuple-element.354), channel_id=1, source_target_pairs={{0,6},{1,7},{2,4},{3,5},{4,2},{5,3},{6,0},{7,1},{8,14},{9,15},{10,... | collective-permute-start | bytes 540680 | tf_op jit(solution)/shard_map/ppermute | solution.py:617
  281.9 20.5 %collective-permute-start.63 = (bf16[384,1024]{1,0:T(8,128)(2,1)S(1)}, bf16[384,1024]{1,0:T(8,128)(2,1)S(1)}, u32[]{:S(2)}, u32[]{:S(2)}) collective-permute-start(bf16[384,1024]{1,0:T(8,128)(2,1)S(1)} %add_convert_fusion.1), channel_id=1, source_target_pairs={{0,16},{8,24},{16,0},{24,8},{1,17},{9,25},{17,1},{25,9},{2,18},{10... | collective-permute-start | bytes 2359304 | tf_op jit(solution)/shard_map/ppermute | solution.py:602
  293.7 22.8 %collective-permute-start.65 = (bf16[4,776,128]{2,1,0:T(8,128)(2,1)}, bf16[4,776,128]{2,1,0:T(8,128)(2,1)S(1)}, u32[]{:S(2)}, u32[]{:S(2)}) collective-permute-start(bf16[4,776,128]{2,1,0:T(8,128)(2,1)} %get-tuple-element.313), channel_id=1, source_target_pairs={{0,1},{1,0},{2,3},{3,2},{4,5},{5,4},{6,7},{7,6},{8,9},{9,8},{10,11... | collective-permute-start | bytes 2383880 | tf_op jit(solution)/shard_map/ppermute | solution.py:617
  294.8 17.2 %collective-permute-start.73 = (bf16[2112,128]{1,0:T(8,128)(2,1)S(1)}, bf16[2112,128]{1,0:T(8,128)(2,1)}, u32[]{:S(2)}, u32[]{:S(2)}) collective-permute-start(bf16[2112,128]{1,0:T(8,128)(2,1)S(1)} %pad_maximum_fusion.7.p0), channel_id=1, source_target_pairs={{0,16},{8,24},{16,0},{24,8},{1,17},{9,25},{17,1},{25,9},{2,18},{10... | collective-permute-start | bytes 1622024 | tf_op jit(solution)/shard_map/ppermute | solution.py:602
  312.0 18.0 %all-to-all-start = ((bf16[4,384,256]{2,1,0:T(8,128)(2,1)}), bf16[4,384,256]{2,1,0:T(8,128)(2,1)S(1)}, u32[]{:S(2)}, u32[]{:S(2)}) async-start(bf16[4,384,256]{2,1,0:T(8,128)(2,1)} %get-tuple-element.308), calls=%async_computation | async-start | bytes 1572864 | tf_op jit(solution)/shard_map/all_to_all | solution.py:892
  317.3 17.2 %collective-permute-start.70 = (bf16[776,128]{1,0:T(8,128)(2,1)S(1)}, bf16[776,128]{1,0:T(8,128)(2,1)S(1)}, u32[]{:S(2)}, u32[]{:S(2)}) collective-permute-start(bf16[776,128]{1,0:T(8,128)(2,1)S(1)} %get-tuple-element.343), channel_id=1, source_target_pairs={{0,4},{1,5},{2,6},{3,7},{4,0},{5,1},{6,2},{7,3},{8,12},{9,13},{10,... | collective-permute-start | bytes 595976 | tf_op jit(solution)/shard_map/ppermute | solution.py:617
  (124 other events, 1214.4 us)
